TPU v7x, 32 devices: a whole 2x2x4 slice. The times are simulated.
32 devices in a mesh: dp: 8 (over z, x), fsdp: 4 (over y, core).
Axes of the slice: x: 2, y: 2, z: 4, core: 2. Of those that a mesh axis runs over, the one named last changes fastest.
Arguments:
- layer_input: bfloat16 [2, 32, 709, 768], P(None, ('dp', 'fsdp')), may hold values from -6 to 6
- text_lengths: int32 [2, 32], P(None, ('dp', 'fsdp')), may hold values from 40 to 512, as said below
- pos_buckets: int32 [2, 32, 709, 709], P(None, ('dp', 'fsdp')), may hold values from 0 to 31
- box_buckets: int32 [2, 32, 2, 709, 709], P(None, ('dp', 'fsdp')), may hold values from 0 to 63
- w_qkv: bfloat16 [768, 2304], P(('dp', 'fsdp')), may hold values from -0.21875 to 0.21875
- w_out: bfloat16 [768, 768], P(('dp', 'fsdp')), may hold values from -1.75 to 1.75
- w_up: bfloat16 [768, 3072], P(('dp', 'fsdp')), may hold values from -0.21875 to 0.21875
- w_down: bfloat16 [3072, 768], P(('dp', 'fsdp')), may hold values from -0.109375 to 0.109375
- norm_gains: bfloat16 [2, 768], P(None, ('dp', 'fsdp')), may hold values from 0.5 to 1.5
- norm_shifts: bfloat16 [2, 768], P(None, ('dp', 'fsdp')), may hold values from -1.75 to 1.75
- proj_biases: bfloat16 [4, 768], P(None, ('dp', 'fsdp')), may hold values from -1.75 to 1.75
- up_bias: bfloat16 [3072], P(('dp', 'fsdp')), may hold values from -1.75 to 1.75
- rel_tables: bfloat16 [160, 12], P('fsdp'), may hold values from -32 to 32
- cotangent: bfloat16 [2, 32, 709, 768], P(None, ('dp', 'fsdp')), may hold values from -6 to 6
Outputs:
- layer_output: bfloat16 [2, 32, 709, 768], P(None, ('dp', 'fsdp'))
- input_grad: float32 [2, 32, 709, 768], P(None, ('dp', 'fsdp'))
- grad_w_qkv: float32 [768, 2304], P(('dp', 'fsdp'))
- grad_w_out: float32 [768, 768], P(('dp', 'fsdp'))
- grad_w_up: float32 [768, 3072], P(('dp', 'fsdp'))
- grad_w_down: float32 [3072, 768], P(('dp', 'fsdp'))
- grad_gains: float32 [2, 768], P(None, ('dp', 'fsdp'))
- grad_shifts: float32 [2, 768], P(None, ('dp', 'fsdp'))
- grad_biases: float32 [4, 768], P(None, ('dp', 'fsdp'))
- grad_up_bias: float32 [3072], P(('dp', 'fsdp'))
- grad_tables: float32 [160, 12], P('fsdp')
Inputs may be any that keep to these rules, and one draw needn't show every extreme that they name: `text_lengths`: text slots at and past a document's length are padding keys; the image slots are always real.
All inputs are finite; a program needn't handle non-finite values.
Results may differ from a plain program's by a relative error of at most 0.013.
Values may be sent and summed in bfloat16 or wider, within the bound.
A program may use at most 384 MiB of HBM per device.

v0:
```python
from functools import partial

import jax
import jax.numpy as jnp
from jax import lax
from jax.sharding import PartitionSpec as P

HEAD_DIM = 64
POS_BINS = 32
BOX_BINS = 64
TEXT_SLOTS = 512


NEG_FILL = -1000000000.0
NORM_EPS = 1e-05
QUERY_BLOCK = 512


def inner_product(left, right):
    return lax.dot_general(
        left, right, (((0,), (0,)), ((), ())), preferred_element_type=jnp.float32
    )


def against(left, right):
    return lax.dot_general(
        left, right, (((1,), (1,)), ((), ())), preferred_element_type=jnp.float32
    )


def fetch_weights(w_qkv, w_out, w_up, w_down, norm_gains, norm_shifts, proj_biases, up_bias):
    return (
        lax.all_gather(w_qkv, ("dp", "fsdp"), axis=0, tiled=True),
        lax.all_gather(w_out, ("dp", "fsdp"), axis=0, tiled=True),
        lax.all_gather(w_up, ("dp", "fsdp"), axis=0, tiled=True),
        lax.all_gather(w_down, ("dp", "fsdp"), axis=0, tiled=True),
        lax.all_gather(norm_gains, ("dp", "fsdp"), axis=1, tiled=True),
        lax.all_gather(norm_shifts, ("dp", "fsdp"), axis=1, tiled=True),
        lax.all_gather(proj_biases, ("dp", "fsdp"), axis=1, tiled=True),
        lax.all_gather(up_bias, ("dp", "fsdp"), axis=0, tiled=True),
    )


def reduce_grads(grad_terms):
    return (
        lax.psum_scatter(grad_terms[0], ("dp", "fsdp"), scatter_dimension=0, tiled=True),
        lax.psum_scatter(grad_terms[1], ("dp", "fsdp"), scatter_dimension=0, tiled=True),
        lax.psum_scatter(grad_terms[2], ("dp", "fsdp"), scatter_dimension=0, tiled=True),
        lax.psum_scatter(grad_terms[3], ("dp", "fsdp"), scatter_dimension=0, tiled=True),
        lax.psum_scatter(grad_terms[4], ("dp", "fsdp"), scatter_dimension=1, tiled=True),
        lax.psum_scatter(grad_terms[5], ("dp", "fsdp"), scatter_dimension=1, tiled=True),
        lax.psum_scatter(grad_terms[6], ("dp", "fsdp"), scatter_dimension=1, tiled=True),
        lax.psum_scatter(grad_terms[7], ("dp", "fsdp"), scatter_dimension=0, tiled=True),
    )


def normalize(rows_in, gain_row, shift_row):
    centre = rows_in - jnp.mean(rows_in, axis=-1, keepdims=True)
    inv_std = lax.rsqrt(jnp.mean(centre * centre, axis=-1, keepdims=True) + NORM_EPS)
    normed = centre * inv_std
    return (normed * gain_row + shift_row, normed, inv_std)


def normalize_back(grad_in, normed, inv_std, gain_row):
    scaled = grad_in * gain_row
    grad_rows = inv_std * (
        scaled
        - jnp.mean(scaled, axis=-1, keepdims=True)
        - normed * jnp.mean(scaled * normed, axis=-1, keepdims=True)
    )
    return (grad_rows, jnp.sum(grad_in * normed, axis=0), jnp.sum(grad_in, axis=0))


def padded_blocks(index_rows):
    rows = index_rows.shape[0]
    padded = (rows + QUERY_BLOCK - 1) // QUERY_BLOCK * QUERY_BLOCK
    filled = jnp.pad(index_rows, ((0, padded - rows), (0, 0)))
    return filled.reshape(padded // QUERY_BLOCK, QUERY_BLOCK, index_rows.shape[1])


def bucket_onehot(pos_block, boxx_block, boxy_block, bins):
    edges = jnp.arange(bins, dtype=jnp.int32)
    hits = (
        (pos_block[..., None] == edges)
        | ((POS_BINS + boxx_block)[..., None] == edges)
        | ((POS_BINS + BOX_BINS + boxy_block)[..., None] == edges)
    )
    return hits.astype(jnp.bfloat16)


def bucket_bias(pos_idx, box_idx, table):
    rows, cols = pos_idx.shape
    bins, heads = table.shape
    blocks = (padded_blocks(pos_idx), padded_blocks(box_idx[0]), padded_blocks(box_idx[1]))

    def one_block(item):
        onehot = bucket_onehot(item[0], item[1], item[2], bins)
        return jnp.einsum("ijb,bh->hij", onehot, table, preferred_element_type=jnp.float32)

    parts = lax.map(one_block, blocks)
    count = parts.shape[0]
    joined = jnp.transpose(parts, (1, 0, 2, 3)).reshape(heads, count * QUERY_BLOCK, cols)
    return joined[:, :rows]


def bucket_grad(dscore, pos_idx, box_idx, bins):
    heads, rows, cols = dscore.shape
    blocks = (padded_blocks(pos_idx), padded_blocks(box_idx[0]), padded_blocks(box_idx[1]))
    count = blocks[0].shape[0]
    grad_pad = jnp.pad(dscore, ((0, 0), (0, count * QUERY_BLOCK - rows), (0, 0)))
    grad_blocks = jnp.transpose(grad_pad.reshape(heads, count, QUERY_BLOCK, cols), (1, 0, 2, 3))

    def add_block(total, item):
        onehot = bucket_onehot(item[0], item[1], item[2], bins)
        upper_part = item[3].astype(jnp.bfloat16)
        lower_part = (item[3] - upper_part.astype(jnp.float32)).astype(jnp.bfloat16)
        first = jnp.einsum("ijb,hij->bh", onehot, upper_part, preferred_element_type=jnp.float32)
        second = jnp.einsum("ijb,hij->bh", onehot, lower_part, preferred_element_type=jnp.float32)
        return (total + (first + second), None)

    total, unused = lax.scan(
        add_block,
        jnp.zeros((bins, heads), jnp.float32),
        (blocks[0], blocks[1], blocks[2], grad_blocks),
    )
    return total


def score_block(query_heads, key_heads, length, pos_idx, box_idx, table):
    raw_scores = jnp.einsum(
        "ihd,jhd->hij", query_heads, key_heads, preferred_element_type=jnp.float32
    )
    bias_terms = bucket_bias(pos_idx, box_idx, table)
    scores = (raw_scores + bias_terms) * 0.125
    slots = jnp.arange(key_heads.shape[0], dtype=jnp.int32)
    key_valid = (slots >= TEXT_SLOTS) | (slots < length)
    return jnp.where(key_valid[None, None, :], scores, NEG_FILL)


def attend_doc(doc_item, table):
    queries, key_rows, values, length, pos_idx, box_idx = doc_item
    seq_len, model_width = queries.shape
    heads = model_width // HEAD_DIM
    query_heads = queries.reshape(seq_len, heads, HEAD_DIM)
    key_heads = key_rows.reshape(seq_len, heads, HEAD_DIM)
    value_heads = values.reshape(seq_len, heads, HEAD_DIM)
    scores = score_block(query_heads, key_heads, length, pos_idx, box_idx, table)
    top_score = jnp.max(scores, axis=-1, keepdims=True)
    log_total = top_score + jnp.log(jnp.sum(jnp.exp(scores - top_score), axis=-1, keepdims=True))
    attn_probs = jnp.exp(scores - log_total).astype(jnp.bfloat16)
    attended = jnp.einsum(
        "hij,jhd->ihd", attn_probs, value_heads, preferred_element_type=jnp.float32
    )
    return (attended.reshape(seq_len, model_width).astype(jnp.bfloat16), log_total)


def attend_back(doc_item, table):
    queries, key_rows, values, d_attended, log_total, length, pos_idx, box_idx = doc_item
    seq_len, model_width = queries.shape
    heads = model_width // HEAD_DIM
    query_heads = queries.reshape(seq_len, heads, HEAD_DIM)
    key_heads = key_rows.reshape(seq_len, heads, HEAD_DIM)
    value_heads = values.reshape(seq_len, heads, HEAD_DIM)
    grad_heads = d_attended.reshape(seq_len, heads, HEAD_DIM)
    scores = score_block(query_heads, key_heads, length, pos_idx, box_idx, table)
    attn_probs = jnp.exp(scores - log_total)
    dvalue = jnp.einsum(
        "hij,ihd->jhd",
        attn_probs.astype(jnp.bfloat16),
        grad_heads,
        preferred_element_type=jnp.float32,
    )
    dprobs = jnp.einsum("ihd,jhd->hij", grad_heads, value_heads, preferred_element_type=jnp.float32)
    row_delta = jnp.sum(attn_probs * dprobs, axis=-1, keepdims=True)
    dscore = attn_probs * (dprobs - row_delta) * 0.125
    dscore_low = dscore.astype(jnp.bfloat16)
    dquery = jnp.einsum("hij,jhd->ihd", dscore_low, key_heads, preferred_element_type=jnp.float32)
    dkey_heads = jnp.einsum(
        "hij,ihd->jhd", dscore_low, query_heads, preferred_element_type=jnp.float32
    )
    table_grad = bucket_grad(dscore, pos_idx, box_idx, table.shape[0])
    d_mixed = jnp.concatenate(
        [
            dquery.reshape(seq_len, model_width),
            dkey_heads.reshape(seq_len, model_width),
            dvalue.reshape(seq_len, model_width),
        ],
        axis=1,
    )
    return (d_mixed.astype(jnp.bfloat16), table_grad)


def forward_pass(block_weights, doc_input, lengths, pos_idx, box_idx, table):
    w_qkv, w_out, w_up, w_down, norm_gains, norm_shifts, proj_biases, up_bias = block_weights
    doc_count, seq_len, model_width = doc_input.shape
    tok_rows = doc_input.reshape(doc_count * seq_len, model_width)
    projected = jnp.dot(tok_rows, w_qkv, preferred_element_type=jnp.float32)
    queries = (projected[:, :model_width] + proj_biases[0]).astype(jnp.bfloat16)
    key_rows = projected[:, model_width : 2 * model_width].astype(jnp.bfloat16)
    values = (projected[:, 2 * model_width :] + proj_biases[1]).astype(jnp.bfloat16)
    shape_docs = (doc_count, seq_len, model_width)
    attended, log_total = lax.map(
        partial(attend_doc, table=table),
        (
            queries.reshape(shape_docs),
            key_rows.reshape(shape_docs),
            values.reshape(shape_docs),
            lengths,
            pos_idx,
            box_idx,
        ),
    )
    attended_rows = attended.reshape(doc_count * seq_len, model_width)
    branch = jnp.dot(attended_rows, w_out, preferred_element_type=jnp.float32) + proj_biases[2]
    hidden, normed_one, inv_one = normalize(
        tok_rows.astype(jnp.float32) + branch, norm_gains[0], norm_shifts[0]
    )
    hidden_low = hidden.astype(jnp.bfloat16)
    upper = jnp.dot(hidden_low, w_up, preferred_element_type=jnp.float32) + up_bias
    active = jax.nn.gelu(upper, approximate=False).astype(jnp.bfloat16)
    ffn_out = jnp.dot(active, w_down, preferred_element_type=jnp.float32) + proj_biases[3]
    result, normed_two, inv_two = normalize(hidden + ffn_out, norm_gains[1], norm_shifts[1])
    kept_state = (
        tok_rows,
        queries,
        key_rows,
        values,
        log_total,
        attended_rows,
        normed_one,
        inv_one,
        hidden_low,
        upper,
        active,
        normed_two,
        inv_two,
    )
    return (result.astype(jnp.bfloat16).reshape(shape_docs), kept_state)


def backward_pass(block_weights, kept_state, grad_out, lengths, pos_idx, box_idx, table):
    w_qkv, w_out, w_up, w_down, norm_gains, norm_shifts, proj_biases, up_bias = block_weights
    (
        tok_rows,
        queries,
        key_rows,
        values,
        log_total,
        attended_rows,
        normed_one,
        inv_one,
        hidden_low,
        upper,
        active,
        normed_two,
        inv_two,
    ) = kept_state
    doc_count, seq_len, model_width = grad_out.shape
    row_count = doc_count * seq_len
    shape_docs = (doc_count, seq_len, model_width)
    grad_rows = grad_out.reshape(row_count, model_width).astype(jnp.float32)
    d_resid_two, d_gain_two, d_shift_two = normalize_back(
        grad_rows, normed_two, inv_two, norm_gains[1]
    )
    d_ffn = d_resid_two.astype(jnp.bfloat16)
    d_wdown = inner_product(active, d_ffn)
    d_active = against(d_ffn, w_down)
    unused, gelu_back = jax.vjp(partial(jax.nn.gelu, approximate=False), upper)
    d_upper = gelu_back(d_active)[0].astype(jnp.bfloat16)
    d_wup = inner_product(hidden_low, d_upper)
    d_hidden = against(d_upper, w_up) + d_resid_two
    d_resid_one, d_gain_one, d_shift_one = normalize_back(
        d_hidden, normed_one, inv_one, norm_gains[0]
    )
    d_branch = d_resid_one.astype(jnp.bfloat16)
    d_wout = inner_product(attended_rows, d_branch)
    d_attended = against(d_branch, w_out).astype(jnp.bfloat16)
    d_mixed, table_parts = lax.map(
        partial(attend_back, table=table),
        (
            queries.reshape(shape_docs),
            key_rows.reshape(shape_docs),
            values.reshape(shape_docs),
            d_attended.reshape(shape_docs),
            log_total,
            lengths,
            pos_idx,
            box_idx,
        ),
    )
    d_mixed = d_mixed.reshape(row_count, 3 * model_width)
    d_wqkv = inner_product(tok_rows, d_mixed)
    d_input = d_resid_one + against(d_mixed, w_qkv)
    d_biases = jnp.stack(
        [
            jnp.sum(d_mixed[:, :model_width].astype(jnp.float32), axis=0),
            jnp.sum(d_mixed[:, 2 * model_width :].astype(jnp.float32), axis=0),
            jnp.sum(d_branch.astype(jnp.float32), axis=0),
            jnp.sum(d_ffn.astype(jnp.float32), axis=0),
        ]
    )
    d_upbias = jnp.sum(d_upper.astype(jnp.float32), axis=0)
    grad_terms = (
        d_wqkv,
        d_wout,
        d_wup,
        d_wdown,
        jnp.stack([d_gain_one, d_gain_two]),
        jnp.stack([d_shift_one, d_shift_two]),
        d_biases,
        d_upbias,
    )
    return (d_input.reshape(shape_docs), grad_terms, jnp.sum(table_parts, axis=0))


def body(
    layer_input,
    text_lengths,
    pos_buckets,
    box_buckets,
    w_qkv,
    w_out,
    w_up,
    w_down,
    norm_gains,
    norm_shifts,
    proj_biases,
    up_bias,
    rel_tables,
    cotangent,
):
    micro_count = layer_input.shape[0]
    table = lax.all_gather(rel_tables, "fsdp", axis=0, tiled=True)
    outputs = []
    input_grads = []
    table_sum = jnp.zeros(table.shape, jnp.float32)
    for micro_index in range(micro_count):
        block_weights = fetch_weights(
            w_qkv, w_out, w_up, w_down, norm_gains, norm_shifts, proj_biases, up_bias
        )
        output_rows, kept_state = forward_pass(
            block_weights,
            layer_input[micro_index],
            text_lengths[micro_index],
            pos_buckets[micro_index],
            box_buckets[micro_index],
            table,
        )
        weights_back = fetch_weights(
            w_qkv, w_out, w_up, w_down, norm_gains, norm_shifts, proj_biases, up_bias
        )
        input_grad, grad_terms, table_grad = backward_pass(
            weights_back,
            kept_state,
            cotangent[micro_index],
            text_lengths[micro_index],
            pos_buckets[micro_index],
            box_buckets[micro_index],
            table,
        )
        outputs.append(output_rows)
        input_grads.append(input_grad)
        table_sum = table_sum + table_grad
        reduced = reduce_grads(grad_terms)
        shards = reduced if micro_index == 0 else jax.tree.map(jnp.add, shards, reduced)
    table_total = lax.psum(table_sum, ("dp", "fsdp"))
    table_rows = rel_tables.shape[0]
    table_shard = lax.dynamic_slice_in_dim(
        table_total, lax.axis_index("fsdp") * table_rows, table_rows, 0
    )
    return (
        jnp.stack(outputs),
        jnp.stack(input_grads),
        shards[0],
        shards[1],
        shards[2],
        shards[3],
        shards[4],
        shards[5],
        shards[6],
        shards[7],
        table_shard,
    )


def solution(mesh):
    return jax.shard_map(
        body,
        mesh=mesh,
        in_specs=(
            P(None, ("dp", "fsdp"), None, None),
            P(None, ("dp", "fsdp")),
            P(None, ("dp", "fsdp"), None, None),
            P(None, ("dp", "fsdp"), None, None, None),
            P(("dp", "fsdp"), None),
            P(("dp", "fsdp"), None),
            P(("dp", "fsdp"), None),
            P(("dp", "fsdp"), None),
            P(None, ("dp", "fsdp")),
            P(None, ("dp", "fsdp")),
            P(None, ("dp", "fsdp")),
            P(("dp", "fsdp")),
            P("fsdp", None),
            P(None, ("dp", "fsdp"), None, None),
        ),
        out_specs=(
            P(None, ("dp", "fsdp"), None, None),
            P(None, ("dp", "fsdp"), None, None),
            P(("dp", "fsdp"), None),
            P(("dp", "fsdp"), None),
            P(("dp", "fsdp"), None),
            P(("dp", "fsdp"), None),
            P(None, ("dp", "fsdp")),
            P(None, ("dp", "fsdp")),
            P(None, ("dp", "fsdp")),
            P(("dp", "fsdp")),
            P("fsdp", None),
        ),
        check_vma=False,
    )
```

profile of v0, /device:TPU:0, one launch (start us, length us, event | category | flops | bytes accessed | tf_op | source)
XLA Modules:
  0.0 2004.5 jit_solution(843695285238040704)
XLA Ops:
  14.6 42.1 %all-reduce.8 = bf16[3072]{0:T(1024)(128)(2,1)S(1)} all-reduce(bf16[3072]{0:T(1024)(128)(2,1)S(1)} %dynamic-update-slice), channel_id=1, replica_groups=mesh['dp'=8,'fsdp'=4] {'dp','fsdp'}, use_global_device_ids=true, to_apply=%add.8 | all-reduce | flops 3072 | bytes 12288
  57.3 40.1 %all-gather.2 = bf16[32,24,2]{1,2,0:T(2,128)(2,1)S(1)} all-gather(bf16[1,24,2]{1,2,0:T(2,128)(2,1)} %bitcast.405), channel_id=1, replica_groups=mesh['dp'=8,'fsdp'=4] {'dp','fsdp'}, dimensions={0}, use_global_device_ids=true | all-gather | bytes 3168 | tf_op jit(solution)/shard_map/all_gather | solution.py:37
  98.2 36.6 %all-gather.3 = bf16[32,24,2]{1,2,0:T(2,128)(2,1)S(1)} all-gather(bf16[1,24,2]{1,2,0:T(2,128)(2,1)} %bitcast.406), channel_id=1, replica_groups=mesh['dp'=8,'fsdp'=4] {'dp','fsdp'}, dimensions={0}, use_global_device_ids=true | all-gather | bytes 3168 | tf_op jit(solution)/shard_map/all_gather | solution.py:38
  140.9 38.2 %all-gather = bf16[32,24,4]{1,2,0:T(4,128)(2,1)S(1)} all-gather(bf16[1,24,4]{1,2,0:T(4,128)(2,1)} %bitcast.404), channel_id=1, replica_groups=mesh['dp'=8,'fsdp'=4] {'dp','fsdp'}, dimensions={0}, use_global_device_ids=true | all-gather | bytes 6336 | tf_op jit(solution)/shard_map/all_gather | solution.py:39
  267.9 134.2 %while.89 = (s32[]{:T(128)}, f32[2,12,512,709]{2,1,3,0:T(8,128)}, s32[2,512,709]{1,2,0:T(8,128)S(1)}, s32[2,512,709]{1,2,0:T(8,128)}, s32[2,512,709]{1,2,0:T(8,128)}, /*index=5*/bf16[160,12]{0,1:T(8,128)(2,1)S(1)}, s32[]{:T(128)}) while((s32[]{:T(128)}, f32[2,12,512,709]{2,1,3,0:T(8,128)}, s32[2,512,709]{1,2,0:T(8,128)S(1)}, ...), condition=%wide.region_9.10_spmd, body=%wide.region_8.9_spmd.sunk | while | flops 1685083136 | bytes 47921020 | solution.py:100
  271.4 63.5 %bitcast_dynamic-update-slice_fusion.5 = f32[2,12,512,709]{2,1,3,0:T(8,128)} fusion(f32[2,12,512,709]{2,1,3,0:T(8,128)} %get-tuple-element.789, s32[]{:T(128)S(6)} %copy.290, s32[512,709]{0,1:T(8,128)S(1)} %get-tuple-element.763, s32[512,709]{0,1:T(8,128)S(1)} %get-tuple-element.764, s32[512,709]{0,1:T(8,128)S(1)} %dynamic-slice_bitcast_fusion.9, ...), kind=kOutput, calls=%fused_computation.23.clone.1 | convolution fusion | flops 1684357120 | bytes 27592452 | tf_op jit(solution)/shard_map/while/body/eval_jaxpr/while/body/eval_jaxpr/ijb,bh->hij/dot_general | solution.py:98
  338.6 63.5 %bitcast_dynamic-update-slice_fusion.5 = f32[2,12,512,709]{2,1,3,0:T(8,128)} fusion(f32[2,12,512,709]{2,1,3,0:T(8,128)} %get-tuple-element.789, s32[]{:T(128)S(6)} %copy.290, s32[512,709]{0,1:T(8,128)S(1)} %get-tuple-element.763, s32[512,709]{0,1:T(8,128)S(1)} %get-tuple-element.764, s32[512,709]{0,1:T(8,128)S(1)} %dynamic-slice_bitcast_fusion.9, ...), kind=kOutput, calls=%fused_computation.23.clone.1 | convolution fusion | flops 1684357120 | bytes 27592452 | tf_op jit(solution)/shard_map/while/body/eval_jaxpr/while/body/eval_jaxpr/ijb,bh->hij/dot_general | solution.py:98
  402.0 59.0 %copy.196 = f32[12,2,512,709]{2,1,3,0:T(2,128)} copy(f32[12,2,512,709]{2,0,3,1:T(8,128)} %bitcast.354) | data formatting | bytes 69697536 | tf_op jit(solution)/shard_map/while/body/eval_jaxpr/transpose | solution.py:102
  512.0 134.4 %while.88 = (s32[]{:T(128)}, f32[2,12,512,709]{2,1,3,0:T(8,128)}, s32[2,512,709]{1,2,0:T(8,128)S(1)}, s32[2,512,709]{1,2,0:T(8,128)}, s32[2,512,709]{1,2,0:T(8,128)}, /*index=5*/bf16[160,12]{0,1:T(8,128)(2,1)S(1)}, s32[]{:T(128)}) while((s32[]{:T(128)}, f32[2,12,512,709]{2,1,3,0:T(8,128)}, s32[2,512,709]{1,2,0:T(8,128)S(1)}, ...), condition=%wide.region_1.2_spmd, body=%wide.region_0.1_spmd.sunk | while | flops 1685083136 | bytes 47921020 | solution.py:100
  515.8 63.5 %bitcast_dynamic-update-slice_fusion.4 = f32[2,12,512,709]{2,1,3,0:T(8,128)} fusion(f32[2,12,512,709]{2,1,3,0:T(8,128)} %get-tuple-element.810, s32[]{:T(128)S(6)} %copy.296, s32[512,709]{0,1:T(8,128)S(1)} %get-tuple-element.755, s32[512,709]{0,1:T(8,128)S(1)} %get-tuple-element.756, s32[512,709]{0,1:T(8,128)S(1)} %dynamic-slice_bitcast_fusion.8, ...), kind=kOutput, calls=%fused_computation.9.clone.1 | convolution fusion | flops 1684357120 | bytes 27592452 | tf_op jit(solution)/shard_map/while/body/eval_jaxpr/while/body/eval_jaxpr/ijb,bh->hij/dot_general | solution.py:98
  582.9 63.5 %bitcast_dynamic-update-slice_fusion.4 = f32[2,12,512,709]{2,1,3,0:T(8,128)} fusion(f32[2,12,512,709]{2,1,3,0:T(8,128)} %get-tuple-element.810, s32[]{:T(128)S(6)} %copy.296, s32[512,709]{0,1:T(8,128)S(1)} %get-tuple-element.755, s32[512,709]{0,1:T(8,128)S(1)} %get-tuple-element.756, s32[512,709]{0,1:T(8,128)S(1)} %dynamic-slice_bitcast_fusion.8, ...), kind=kOutput, calls=%fused_computation.9.clone.1 | convolution fusion | flops 1684357120 | bytes 27592452 | tf_op jit(solution)/shard_map/while/body/eval_jaxpr/while/body/eval_jaxpr/ijb,bh->hij/dot_general | solution.py:98
  646.4 58.0 %copy.180 = f32[12,2,512,709]{2,1,3,0:T(2,128)} copy(f32[12,2,512,709]{2,0,3,1:T(8,128)} %bitcast.355) | data formatting | bytes 69697536 | tf_op jit(solution)/shard_map/while/body/eval_jaxpr/transpose | solution.py:102
  883.7 47.8 %multiply_convert_fusion.1 = (bf16[709,3072]{1,0:T(8,128)(2,1)}, f32[709,3072]{1,0:T(8,128)}, bf16[709,3072]{1,0:T(8,128)(2,1)}, f32[709,3072]{1,0:T(8,128)}, f32[709,3072]{1,0:T(8,128)}) fusion(f32[3072]{0:T(1024)S(1)} %copy-done.82, f32[709,3072]{1,0:T(8,128)S(1)} %fusion.208, bf16[768,3072]{1,0:T(8,128)(2,1)S(1)} %copy-done.97, ...), kind=kOutput, calls=%fused_computation.111 | convolution fusion | flops 3635706624 | bytes 50481704 | tf_op jit(solution)/shard_map/dot_general | solution.py:219
  1286.9 271.2 %while.91 = (s32[]{:T(128)}, f32[160,12]{0,1:T(8,128)S(1)}, s32[2,512,709]{1,2,0:T(8,128)}, s32[2,512,709]{1,2,0:T(8,128)}, s32[2,512,709]{1,2,0:T(8,128)}, /*in...) while((s32[]{:T(128)}, f32[160,12]{0,1:T(8,128)S(1)}, s32[2,512,709]{1,2,0:T(8,128)}, ...), condition=%wide.region_63.64_spmd.clone, body=%wide.region_62.63_spmd.clone.sunk | while | flops 3386870272 | bytes 52303988 | solution.py:121
  1291.0 65.7 %fusion.303 = f32[160,12]{0,1:T(8,128)S(1)} fusion(f32[2,12,512,709]{2,1,3,0:T(8,128)} %get-tuple-element.868, s32[]{:T(128)S(6)} %copy.308, s32[512,709]{0,1:T(8,128)S(1)} %get-tuple-element.779, s32[512,709]{0,1:T(8,128)S(1)} %get-tuple-element.780, s32[512,709]{0,1:T(8,128)S(1)} %dynamic-slice_bitcast_fusion.11), kind=kOutput, calls=%fused_computation.60.clone.1 | convolution fusion | flops 1684357120 | bytes 15980036 | tf_op jit(solution)/shard_map/while/body/eval_jaxpr/while/body/eval_jaxpr/ijb,hij->bh/dot_general | solution.py:117
  1356.7 65.9 %fusion.304 = f32[160,12]{0,1:T(8,128)S(1)} fusion(f32[160,12]{0,1:T(8,128)S(1)} %fusion.303, f32[2,12,512,709]{2,1,3,0:T(8,128)} %get-tuple-element.868, s32[]{:T(128)S(6)} %copy.308, s32[512,709]{0,1:T(8,128)S(1)} %get-tuple-element.779, s32[512,709]{0,1:T(8,128)S(1)} %get-tuple-element.780, s32[512,709]{0,1:T(8,128)S(1)} %dynamic-slice_bitcast_fusion.11, ...), kind=kOutput, calls=%fused_computation.63.clone.1 | convolution fusion | flops 1701787264 | bytes 27611652 | tf_op jit(solution)/shard_map/while/body/eval_jaxpr/while/body/eval_jaxpr/ijb,hij->bh/dot_general | solution.py:118
  1426.4 65.8 %fusion.303 = f32[160,12]{0,1:T(8,128)S(1)} fusion(f32[2,12,512,709]{2,1,3,0:T(8,128)} %get-tuple-element.868, s32[]{:T(128)S(6)} %copy.308, s32[512,709]{0,1:T(8,128)S(1)} %get-tuple-element.779, s32[512,709]{0,1:T(8,128)S(1)} %get-tuple-element.780, s32[512,709]{0,1:T(8,128)S(1)} %dynamic-slice_bitcast_fusion.11), kind=kOutput, calls=%fused_computation.60.clone.1 | convolution fusion | flops 1684357120 | bytes 15980036 | tf_op jit(solution)/shard_map/while/body/eval_jaxpr/while/body/eval_jaxpr/ijb,hij->bh/dot_general | solution.py:117
  1492.2 65.8 %fusion.304 = f32[160,12]{0,1:T(8,128)S(1)} fusion(f32[160,12]{0,1:T(8,128)S(1)} %fusion.303, f32[2,12,512,709]{2,1,3,0:T(8,128)} %get-tuple-element.868, s32[]{:T(128)S(6)} %copy.308, s32[512,709]{0,1:T(8,128)S(1)} %get-tuple-element.779, s32[512,709]{0,1:T(8,128)S(1)} %get-tuple-element.780, s32[512,709]{0,1:T(8,128)S(1)} %dynamic-slice_bitcast_fusion.11, ...), kind=kOutput, calls=%fused_computation.63.clone.1 | convolution fusion | flops 1701787264 | bytes 27611652 | tf_op jit(solution)/shard_map/while/body/eval_jaxpr/while/body/eval_jaxpr/ijb,hij->bh/dot_general | solution.py:118
  1666.5 270.6 %while.90 = (s32[]{:T(128)}, f32[160,12]{0,1:T(8,128)S(1)}, s32[2,512,709]{1,2,0:T(8,128)}, s32[2,512,709]{1,2,0:T(8,128)}, s32[2,512,709]{1,2,0:T(8,128)}, /*in...) while((s32[]{:T(128)}, f32[160,12]{0,1:T(8,128)S(1)}, s32[2,512,709]{1,2,0:T(8,128)}, ...), condition=%wide.region_61.62_spmd.clone, body=%wide.region_60.61_spmd.clone.sunk | while | flops 3386870272 | bytes 52303988 | solution.py:121
  1670.3 65.8 %fusion.298 = f32[160,12]{0,1:T(8,128)S(1)} fusion(f32[2,12,512,709]{2,1,3,0:T(8,128)} %get-tuple-element.844, s32[]{:T(128)S(6)} %copy.302, s32[512,709]{0,1:T(8,128)S(1)} %get-tuple-element.771, s32[512,709]{0,1:T(8,128)S(1)} %get-tuple-element.772, s32[512,709]{0,1:T(8,128)S(1)} %dynamic-slice_bitcast_fusion.10), kind=kOutput, calls=%fused_computation.41.clone.1 | convolution fusion | flops 1684357120 | bytes 15980036 | tf_op jit(solution)/shard_map/while/body/eval_jaxpr/while/body/eval_jaxpr/ijb,hij->bh/dot_general | solution.py:117
  1736.1 65.8 %fusion.299 = f32[160,12]{0,1:T(8,128)S(1)} fusion(f32[160,12]{0,1:T(8,128)S(1)} %fusion.298, f32[2,12,512,709]{2,1,3,0:T(8,128)} %get-tuple-element.844, s32[]{:T(128)S(6)} %copy.302, s32[512,709]{0,1:T(8,128)S(1)} %get-tuple-element.771, s32[512,709]{0,1:T(8,128)S(1)} %get-tuple-element.772, s32[512,709]{0,1:T(8,128)S(1)} %dynamic-slice_bitcast_fusion.10, ...), kind=kOutput, calls=%fused_computation.44.clone.1 | convolution fusion | flops 1701787264 | bytes 27611652 | tf_op jit(solution)/shard_map/while/body/eval_jaxpr/while/body/eval_jaxpr/ijb,hij->bh/dot_general | solution.py:118
  1805.6 65.7 %fusion.298 = f32[160,12]{0,1:T(8,128)S(1)} fusion(f32[2,12,512,709]{2,1,3,0:T(8,128)} %get-tuple-element.844, s32[]{:T(128)S(6)} %copy.302, s32[512,709]{0,1:T(8,128)S(1)} %get-tuple-element.771, s32[512,709]{0,1:T(8,128)S(1)} %get-tuple-element.772, s32[512,709]{0,1:T(8,128)S(1)} %dynamic-slice_bitcast_fusion.10), kind=kOutput, calls=%fused_computation.41.clone.1 | convolution fusion | flops 1684357120 | bytes 15980036 | tf_op jit(solution)/shard_map/while/body/eval_jaxpr/while/body/eval_jaxpr/ijb,hij->bh/dot_general | solution.py:117
  1871.3 65.8 %fusion.299 = f32[160,12]{0,1:T(8,128)S(1)} fusion(f32[160,12]{0,1:T(8,128)S(1)} %fusion.298, f32[2,12,512,709]{2,1,3,0:T(8,128)} %get-tuple-element.844, s32[]{:T(128)S(6)} %copy.302, s32[512,709]{0,1:T(8,128)S(1)} %get-tuple-element.771, s32[512,709]{0,1:T(8,128)S(1)} %get-tuple-element.772, s32[512,709]{0,1:T(8,128)S(1)} %dynamic-slice_bitcast_fusion.10, ...), kind=kOutput, calls=%fused_computation.44.clone.1 | convolution fusion | flops 1701787264 | bytes 27611652 | tf_op jit(solution)/shard_map/while/body/eval_jaxpr/while/body/eval_jaxpr/ijb,hij->bh/dot_general | solution.py:118
  1956.4 37.9 %all-reduce.13 = (f32[2,768]{1,0:T(2,128)S(1)}, f32[2,768]{1,0:T(2,128)S(1)}, f32[4,768]{1,0:T(4,128)S(1)}, f32[3072]{0:T(1024)S(1)}, f32[160,12]{0,1:T(8,128)S(1)}) all-reduce(f32[2,768]{1,0:T(2,128)S(1)} %maximum_add_fusion.1, f32[2,768]{1,0:T(2,128)S(1)} %maximum_add_fusion.2, ...), channel_id=14, replica_groups=mesh['dp'=8,'fsdp'=4] {'dp','fsdp'}, use_global_device_ids=true, to_apply=%region_36.37.clone | all-reduce | flops 11136 | bytes 89088
  (428 shorter events, 847.7 us)
Async XLA Ops:
  7.2 737.9 %all-gather.9.cloned.1.call-start = ((), (), s32[]{:S(2)}) async-start(), calls=%async_computation.4 | async-start | bytes 3649536 | tf_op jit(solution)/shard_map/all_gather | solution.py:33
  7.9 812.3 %all-gather.11.cloned.1.call-start = ((), (), s32[]{:S(2)}) async-start(), calls=%async_computation.5 | async-start | bytes 1216512 | tf_op jit(solution)/shard_map/all_gather | solution.py:34
  8.7 864.9 %all-gather.13.cloned.1.call-start = ((), (), s32[]{:S(2)}) async-start(), calls=%async_computation.6 | async-start | bytes 4866048 | tf_op jit(solution)/shard_map/all_gather | solution.py:35
  9.4 922.2 %all-gather.15.cloned.1.call-start = ((), (), s32[]{:S(2)}) async-start(), calls=%async_computation.7 | async-start | bytes 4866048 | tf_op jit(solution)/shard_map/all_gather | solution.py:36
  10.0 1987.4 %reduce-scatter.10.cloned.1.call-start = ((), (), s32[]{:S(2)}) async-start(), calls=%async_computation.8 | async-start | bytes 2433024 | tf_op jit(solution)/shard_map/reduce_scatter | solution.py:47
  402.0 59.0 %copy-start.1 = (s32[2,512,709]{1,2,0:T(8,128)}, s32[2,512,709]{1,2,0:T(8,128)S(1)}, u32[]{:S(2)}) copy-start(s32[2,512,709]{1,2,0:T(8,128)S(1)} %get-tuple-element.880) | copy-start | bytes 8712196
  704.4 35.7 %copy-start.65 = (bf16[768,2]{0,1:T(2,128)(2,1)S(1)}, bf16[768,2]{0,1:T(2,128)(2,1)}, u32[]{:S(2)}) copy-start(bf16[768,2]{0,1:T(2,128)(2,1)} %reshape.454) | copy-start | bytes 9220
  704.4 35.7 %copy-start.66 = (bf16[768,2]{0,1:T(2,128)(2,1)S(1)}, bf16[768,2]{0,1:T(2,128)(2,1)}, u32[]{:S(2)}) copy-start(bf16[768,2]{0,1:T(2,128)(2,1)} %reshape.456) | copy-start | bytes 9220
  704.4 36.4 %copy-start.23 = (bf16[1,1,709,768]{3,0,2,1:T(2,128)(2,1)S(1)}, bf16[1,1,709,768]{3,0,2,1:T(2,128)(2,1)}, u32[]{:S(2)}) copy-start(bf16[1,1,709,768]{3,0,2,1:T(2,128)(2,1)} %get-tuple-element.568) | copy-start | bytes 3267076
  740.8 198.9 %copy-start.60 = (f32[768]{0:T(1024)}, f32[768]{0:T(1024)S(1)}, u32[]{:S(2)}) copy-start(f32[768]{0:T(1024)S(1)} %get-tuple-element.478) | copy-start | bytes 9220
  754.3 71.9 %copy-start.8 = (bf16[709,768]{0,1:T(8,128)(2,1)}, bf16[709,768]{0,1:T(8,128)(2,1)S(1)}, u32[]{:S(2)}) copy-start(bf16[709,768]{0,1:T(8,128)(2,1)S(1)} %copy.170) | copy-start | bytes 3267076
  873.1 114.5 %copy-start.17 = (f32[709,768]{1,0:T(8,128)}, f32[709,768]{1,0:T(8,128)S(1)}, u32[]{:S(2)}) copy-start(f32[709,768]{1,0:T(8,128)S(1)} %get-tuple-element.591) | copy-start | bytes 6534148
  873.1 114.5 %copy-start.58 = (f32[709]{0:T(1024)}, f32[709]{0:T(1024)S(1)}, u32[]{:S(2)}) copy-start(f32[709]{0:T(1024)S(1)} %broadcast_multiply_fusion.11) | copy-start | bytes 8512
  873.5 114.1 %copy-start.62 = (f32[709]{0:T(1024)}, f32[709]{0:T(1024)S(1)}, u32[]{:S(2)}) copy-start(f32[709]{0:T(1024)S(1)} %add_rsqrt_fusion.3) | copy-start | bytes 8512
  883.7 47.8 %copy-start.85 = (f32[768]{0:T(1024)S(1)}, f32[768]{0:T(1024)}, u32[]{:S(2)}) copy-start(f32[768]{0:T(1024)} %get-tuple-element.471) | copy-start | bytes 9220
  1122.1 875.3 %reduce-scatter.16.cloned.1.call-start = ((), (), s32[]{:S(2)}) async-start(), calls=%async_computation.11 | async-start | bytes 7299072
  1175.3 822.1 %reduce-scatter.12.cloned.1.call-start = ((), (), s32[]{:S(2)}) async-start(), calls=%async_computation.9 | async-start | bytes 9732096 | tf_op jit(solution)/shard_map/reduce_scatter | solution.py:48
  1286.8 710.6 %reduce-scatter.14.cloned.1.call-start = ((), (), s32[]{:S(2)}) async-start(), calls=%async_computation.10 | async-start | bytes 9732096 | tf_op jit(solution)/shard_map/reduce_scatter | solution.py:49
  1666.5 270.7 %copy-start.77 = (f32[768]{0:T(1024)S(1)}, f32[768]{0:T(1024)}, u32[]{:S(2)}) copy-start(f32[768]{0:T(1024)} %get-tuple-element.463) | copy-start | bytes 9220
  1666.5 270.7 %copy-start.76 = (f32[768]{0:T(1024)S(1)}, f32[768]{0:T(1024)}, u32[]{:S(2)}) copy-start(f32[768]{0:T(1024)} %get-tuple-element.585) | copy-start | bytes 9220
  1666.5 270.7 %copy-start.69 = (f32[768]{0:T(1024)S(1)}, f32[768]{0:T(1024)}, u32[]{:S(2)}) copy-start(f32[768]{0:T(1024)} %get-tuple-element.534) | copy-start | bytes 9220
  1666.5 270.7 %copy-start.68 = (f32[768]{0:T(1024)S(1)}, f32[768]{0:T(1024)}, u32[]{:S(2)}) copy-start(f32[768]{0:T(1024)} %get-tuple-element.575) | copy-start | bytes 9220
  1666.5 270.7 %copy-start.42 = (bf16[1,1,709,768]{3,2,1,0:T(8,128)(2,1)S(1)}, bf16[1,1,709,768]{3,2,1,0:T(8,128)(2,1)}, u32[]{:S(2)}) copy-start(bf16[1,1,709,768]{3,2,1,0:T(8,128)(2,1)} %get-tuple-element.567) | copy-start | bytes 3267076
  1666.5 270.7 %copy-start.43 = (bf16[1,1,709,768]{3,2,1,0:T(8,128)(2,1)S(1)}, bf16[1,1,709,768]{3,2,1,0:T(8,128)(2,1)}, u32[]{:S(2)}) copy-start(bf16[1,1,709,768]{3,2,1,0:T(8,128)(2,1)} %get-tuple-element.574) | copy-start | bytes 3267076
  (98 other events, 852.2 us)
Sparse Core Ops, SparseCore 0:
  10.9 62.9 all-gather.8
  76.8 52.8 all-gather.10
  132.6 62.6 all-gather.12
  198.1 62.3 all-gather.14
  1122.2 95.9 reduce-scatter.9
  1225.3 118.1 reduce-scatter.15
  1349.9 134.6 reduce-scatter.11
  1665.9 132.9 reduce-scatter.13
where the time goes:
time: 2010 us; the launch traced here: 2000 us
  matrix products  1180 us (59%)
  local copies, waits for them, and re-layouts  549 us (27%)
  blocking collectives  200 us (10%)
  other arithmetic  60.3 us (3%)
    dot_general x4, matrix products, add_block(): jnp.einsum('ijb,hij->bh', onehot, lower_part, preferred_element_type=jnp....  263 us
    dot_general x4, matrix products, add_block(): jnp.einsum('ijb,hij->bh', onehot, upper_part, preferred_element_type=jnp....  263 us
    dot_general x4, matrix products, one_block(): jnp.einsum('ijb,bh->hij', onehot, table, preferred_element_type=jnp.float32)  254 us
    reshape x4, local copies, waits for them, and re-layouts, bucket_grad(): grad_pad.reshape(heads, count, QUERY_BLOCK, cols)  140 us
    transpose x2, local copies, waits for them, and re-layouts, bucket_bias(): jnp.transpose(parts, (1, 0, 2, 3)).reshape(heads, count * QUERY_BLOCK, cols)  117 us
    unnamed x2, blocking collectives  80 us
    reshape x2, local copies, waits for them, and re-layouts, bucket_bias(): jnp.transpose(parts, (1, 0, 2, 3)).reshape(heads, count * QUERY_BLOCK, cols)  71.5 us
    sub x2, matrix products, attend_back(): dscore = attn_probs * (dprobs - row_delta) * 0.125  60.5 us
  transfers between devices with their start and end apart: 8, of which 0 were waited for; matrix products, arithmetic and copies ran while one was open for 79% of the time, Pallas kernels for 0%

commit v1 on v0

v1 whole, which is shorter than its diff:
```python
from functools import partial

import jax
import jax.numpy as jnp
from jax import lax
from jax.experimental import pallas as pl
from jax.experimental.pallas import tpu as pltpu
from jax.sharding import PartitionSpec as P

HEAD_DIM = 64
POS_BINS = 32
BOX_BINS = 64
TEXT_SLOTS = 512
NEG_FILL = -1000000000.0
NORM_EPS = 1e-05
BLOCK = 256
DENSE_BLOCK = 384
LANES = 128
HALF = 32
SCALE = 0.125
F32 = jnp.float32
BF16 = jnp.bfloat16
VMEM_LIMIT = 58 << 20


def dot(left, right):
    return jnp.dot(left, right, preferred_element_type=F32)


def dot_nt(left, right):
    return lax.dot_general(left, right, (((1,), (1,)), ((), ())), preferred_element_type=F32)


def params(count):
    return pltpu.CompilerParams(
        dimension_semantics=("arbitrary",) * count, vmem_limit_bytes=VMEM_LIMIT
    )


def resident(shape):
    zeros = (0,) * len(shape)
    return pl.BlockSpec(shape, lambda *_: zeros, pipeline_mode=pl.Buffered(1))


def live_rows(values, rows, first):
    row = first + lax.broadcasted_iota(jnp.int32, (values.shape[0], 1), 0)
    return jnp.where(row < rows, values, jnp.zeros_like(values))


def bias_kernel(rows, len_ref, tab_ref, pos_ref, box_ref, out_ref):
    heads, chunks = out_ref.shape[1], out_ref.shape[3] // LANES
    block = pl.program_id(1)
    length = len_ref[pl.program_id(0)]
    steps = jnp.minimum(BLOCK, (rows + 7) // 8 * 8 - block * BLOCK) // 8

    def fill(step, carry):
        at = pl.ds(pl.multiple_of(step * 8, 8), 8)
        for chunk in range(chunks):
            cols = slice(chunk * LANES, (chunk + 1) * LANES)
            picks = (
                box_ref[0, 0, 0, at, cols] & (BOX_BINS - 1),
                (box_ref[0, 0, 1, at, cols] & (BOX_BINS - 1)) | BOX_BINS,
                pos_ref[0, 0, at, cols] & (POS_BINS - 1),
            )
            slot = chunk * LANES + lax.broadcasted_iota(jnp.int32, (8, LANES), 1)
            valid = ((slot >= TEXT_SLOTS) & (slot < rows)) | (slot < length)
            totals = [None] * heads
            for which, pick in enumerate(picks):
                for head in range(heads):
                    line = head + (heads if which == 2 else 0)
                    entries = jnp.broadcast_to(tab_ref[line : line + 1, :], (8, LANES))
                    term = jnp.take_along_axis(entries, pick, axis=1)
                    totals[head] = term if which == 0 else totals[head] + term
            for head in range(heads):
                out_ref[0, head, at, cols] = jnp.where(valid, totals[head], NEG_FILL)
        return carry

    def blank(step, carry):
        at = pl.ds(pl.multiple_of(step * 8, 8), 8)
        for head in range(heads):
            out_ref[0, head, at, :] = jnp.zeros((8, chunks * LANES), F32)
        return carry

    lax.fori_loop(0, steps, fill, 0)
    lax.fori_loop(steps, BLOCK // 8, blank, 0)


def bias_rows(lengths, entries, pos_buckets, box_buckets, heads):
    docs, rows = pos_buckets.shape[0], pos_buckets.shape[2]
    padded = pl.cdiv(rows, BLOCK) * BLOCK
    return pl.pallas_call(
        partial(bias_kernel, rows),
        out_shape=jax.ShapeDtypeStruct((docs, heads, padded, padded), F32),
        grid=(docs, padded // BLOCK),
        in_specs=[
            pl.BlockSpec(memory_space=pltpu.SMEM),
            resident(entries.shape),
            pl.BlockSpec((1, 1, BLOCK, padded), lambda d, i: (d, 0, i, 0)),
            pl.BlockSpec((1, 1, 2, BLOCK, padded), lambda d, i: (d, 0, 0, i, 0)),
        ],
        out_specs=pl.BlockSpec((1, heads, BLOCK, padded), lambda d, i: (d, 0, i, 0)),
        compiler_params=params(2),
        cost_estimate=pl.CostEstimate(
            flops=3 * docs * heads * rows * rows,
            transcendentals=0,
            bytes_accessed=docs * padded * padded * (4 * heads + 12),
        ),
        name="bias_rows",
    )(lengths, entries, pos_buckets, box_buckets)


def project_kernel(rows, x_ref, w_ref, vec_ref, out_ref):
    width = x_ref.shape[3]
    block = live_rows(x_ref[0, 0], rows, pl.program_id(1) * x_ref.shape[2])
    queries = dot(block, w_ref[:, :width]) + vec_ref[4:5, :]
    out_ref[0, :, :width] = queries.astype(BF16) * BF16(SCALE)
    out_ref[0, :, width : 2 * width] = dot(block, w_ref[:, width : 2 * width]).astype(BF16)
    values = dot(block, w_ref[:, 2 * width :]) + vec_ref[5:6, :]
    out_ref[0, :, 2 * width :] = values.astype(BF16)


def project(layer_input, w_qkv, vectors):
    docs, unused, rows, width = layer_input.shape
    padded = pl.cdiv(rows, BLOCK) * BLOCK
    return pl.pallas_call(
        partial(project_kernel, rows),
        out_shape=jax.ShapeDtypeStruct((docs, padded, 3 * width), BF16),
        grid=(docs, padded // DENSE_BLOCK),
        in_specs=[
            pl.BlockSpec((1, 1, DENSE_BLOCK, width), lambda d, i: (d, 0, i, 0)),
            resident(w_qkv.shape),
            resident(vectors.shape),
        ],
        out_specs=pl.BlockSpec((1, DENSE_BLOCK, 3 * width), lambda d, i: (d, i, 0)),
        compiler_params=params(2),
        name="project",
    )(layer_input, w_qkv, vectors)


def attend_kernel(q_ref, k_ref, v_ref, bias_ref, probs_ref, out_ref):
    lane = lax.broadcasted_iota(jnp.int32, (1, LANES), 1)
    for pair in range(q_ref.shape[2] // LANES):
        cols = slice(pair * LANES, (pair + 1) * LANES)
        queries, key_rows, values = q_ref[0, :, cols], k_ref[0, :, cols], v_ref[0, :, cols]
        total = None
        for half in range(2):
            head = 2 * pair + half
            keep = (lane < HEAD_DIM) if half == 0 else (lane >= HEAD_DIM)
            scores = dot_nt(jnp.where(keep, queries, BF16(0)), key_rows) + bias_ref[0, head]
            top = jnp.max(scores, axis=-1, keepdims=True)
            powers = jnp.exp(scores - top)
            share = 1.0 / jnp.sum(powers, axis=-1, keepdims=True)
            probs = (powers * share).astype(BF16)
            probs_ref[0, head] = probs
            part = dot(probs, jnp.where(keep, values, BF16(0)))
            total = part if half == 0 else total + part
        out_ref[0, :, cols] = total.astype(BF16)


def attend(qkv, bias):
    docs, padded, width = qkv.shape[0], qkv.shape[1], qkv.shape[2] // 3
    heads = bias.shape[1]
    return pl.pallas_call(
        attend_kernel,
        out_shape=(
            jax.ShapeDtypeStruct((docs, heads, padded, padded), BF16),
            jax.ShapeDtypeStruct((docs, padded, width), BF16),
        ),
        grid=(docs, padded // BLOCK),
        in_specs=[
            pl.BlockSpec((1, BLOCK, width), lambda d, i: (d, i, 0)),
            pl.BlockSpec((1, padded, width), lambda d, i: (d, 0, 1)),
            pl.BlockSpec((1, padded, width), lambda d, i: (d, 0, 2)),
            pl.BlockSpec((1, heads, BLOCK, padded), lambda d, i: (d, 0, i, 0)),
        ],
        out_specs=(
            pl.BlockSpec((1, heads, BLOCK, padded), lambda d, i: (d, 0, i, 0)),
            pl.BlockSpec((1, BLOCK, width), lambda d, i: (d, i, 0)),
        ),
        compiler_params=params(2),
        name="attend",
    )(qkv, qkv, qkv, bias)


def norm(rows_in):
    centre = rows_in - jnp.mean(rows_in, axis=-1, keepdims=True)
    inv_std = lax.rsqrt(jnp.mean(centre * centre, axis=-1, keepdims=True) + NORM_EPS)
    return centre * inv_std, inv_std


def norm_back(grad_in, normed, inv_std, gain_row):
    scaled = grad_in * gain_row
    return inv_std * (
        scaled
        - jnp.mean(scaled, axis=-1, keepdims=True)
        - normed * jnp.mean(scaled * normed, axis=-1, keepdims=True)
    )


def dense_kernel(
    rows, x_ref, o_ref, cot_ref, wo_ref, wu_ref, wd_ref, vec_ref, upb_ref,
    y_ref, dr_ref, h_ref, g_ref, du_ref, df_ref, db_ref, do_ref, sums_ref, upsum_ref,
    slope_ref,
):
    width, hidden = wu_ref.shape
    first = pl.program_id(1) * x_ref.shape[2]
    vec = vec_ref[...]

    @pl.when((pl.program_id(0) == 0) & (pl.program_id(1) == 0))
    def _():
        sums_ref[...] = jnp.zeros_like(sums_ref)
        upsum_ref[...] = jnp.zeros_like(upsum_ref)

    tok = live_rows(x_ref[0, 0], rows, first).astype(F32)
    normed_one, inv_one = norm(tok + dot(o_ref[0], wo_ref[...]) + vec[6:7])
    state = normed_one * vec[0:1] + vec[2:3]
    low = state.astype(BF16)
    h_ref[0] = low
    second = state + vec[7:8]
    for part in range(hidden // width):
        cols = slice(part * width, (part + 1) * width)
        upper = dot(low, wu_ref[:, cols]) + upb_ref[:, cols]
        cdf = 0.5 * (1.0 + lax.erf(upper * (0.5**0.5)))
        slope_ref[:, cols] = cdf + upper * (jnp.exp(-0.5 * upper * upper) * 0.3989422804014327)
        active = (upper * cdf).astype(BF16)
        g_ref[0, :, cols] = active
        second = second + dot(active, wd_ref[cols, :])
    normed_two, inv_two = norm(second)
    y_ref[0, 0] = (normed_two * vec[1:2] + vec[3:4]).astype(BF16)
    grad = live_rows(cot_ref[0, 0], rows, first).astype(F32)
    sums_ref[1:2, :] += jnp.sum(grad * normed_two, axis=0, keepdims=True)
    sums_ref[3:4, :] += jnp.sum(grad, axis=0, keepdims=True)
    d_two = norm_back(grad, normed_two, inv_two, vec[1:2])
    d_ffn = d_two.astype(BF16)
    df_ref[0] = d_ffn
    sums_ref[7:8, :] += jnp.sum(d_ffn.astype(F32), axis=0, keepdims=True)
    back = d_two
    for part in range(hidden // width):
        cols = slice(part * width, (part + 1) * width)
        d_upper = (dot_nt(d_ffn, wd_ref[cols, :]) * slope_ref[:, cols]).astype(BF16)
        du_ref[0, :, cols] = d_upper
        upsum_ref[:, cols] += jnp.sum(d_upper.astype(F32), axis=0, keepdims=True)
        back = back + dot_nt(d_upper, wu_ref[:, cols])
    sums_ref[0:1, :] += jnp.sum(back * normed_one, axis=0, keepdims=True)
    sums_ref[2:3, :] += jnp.sum(back, axis=0, keepdims=True)
    d_one = norm_back(back, normed_one, inv_one, vec[0:1])
    dr_ref[0] = d_one
    d_branch = d_one.astype(BF16)
    db_ref[0] = d_branch
    sums_ref[6:7, :] += jnp.sum(d_branch.astype(F32), axis=0, keepdims=True)
    do_ref[0] = dot_nt(d_branch, wo_ref[...]).astype(BF16)


def dense(layer_input, attended, cotangent, w_out, w_up, w_down, vectors, up_row):
    docs, unused, rows, width = layer_input.shape
    padded, hidden = attended.shape[1], w_up.shape[1]
    ragged = pl.BlockSpec((1, 1, DENSE_BLOCK, width), lambda d, i: (d, 0, i, 0))
    narrow = pl.BlockSpec((1, DENSE_BLOCK, width), lambda d, i: (d, i, 0))
    wide = pl.BlockSpec((1, DENSE_BLOCK, hidden), lambda d, i: (d, i, 0))

    def rows_of(columns, dtype):
        return jax.ShapeDtypeStruct((docs, padded, columns), dtype)

    return pl.pallas_call(
        partial(dense_kernel, rows),
        out_shape=(
            jax.ShapeDtypeStruct(layer_input.shape, BF16),
            rows_of(width, F32),
            rows_of(width, BF16),
            rows_of(hidden, BF16),
            rows_of(hidden, BF16),
            rows_of(width, BF16),
            rows_of(width, BF16),
            rows_of(width, BF16),
            jax.ShapeDtypeStruct((8, width), F32),
            jax.ShapeDtypeStruct((1, hidden), F32),
        ),
        grid=(docs, padded // DENSE_BLOCK),
        in_specs=[
            ragged, narrow, ragged,
            resident(w_out.shape), resident(w_up.shape), resident(w_down.shape),
            resident(vectors.shape), resident(up_row.shape),
        ],
        out_specs=(
            ragged, narrow, narrow, wide, wide, narrow, narrow, narrow,
            pl.BlockSpec((8, width), lambda d, i: (0, 0)),
            pl.BlockSpec((1, hidden), lambda d, i: (0, 0)),
        ),
        scratch_shapes=[pltpu.VMEM((DENSE_BLOCK, hidden), F32)],
        compiler_params=params(2),
        name="dense",
    )(layer_input, attended, cotangent, w_out, w_up, w_down, vectors, up_row)


def attend_back_kernel(
    rows, q_ref, k_ref, v_ref, probs_ref, do_ref, pos_ref, box_ref, dm_ref, bins_ref,
    dk_ref, dv_ref, ds_ref,
):
    block, width = pl.program_id(1), q_ref.shape[2]
    padded = k_ref.shape[1]
    lane = lax.broadcasted_iota(jnp.int32, (1, LANES), 1)

    @pl.when((pl.program_id(0) == 0) & (block == 0))
    def _():
        bins_ref[...] = jnp.zeros_like(bins_ref)
        ds_ref[...] = jnp.zeros_like(ds_ref)

    @pl.when(block == 0)
    def _():
        dk_ref[...] = jnp.zeros_like(dk_ref)
        dv_ref[...] = jnp.zeros_like(dv_ref)

    own = pl.ds(pl.multiple_of(block * BLOCK, BLOCK), BLOCK)
    for pair in range(width // LANES):
        cols = slice(pair * LANES, (pair + 1) * LANES)
        queries, key_rows, values = q_ref[0, :, cols], k_ref[0, :, cols], v_ref[0, :, cols]
        grads = do_ref[0, :, cols]
        turned_q, turned_g = queries.T, grads.T
        total = None
        for half in range(2):
            head = 2 * pair + half
            keep = (lane < HEAD_DIM) if half == 0 else (lane >= HEAD_DIM)
            part = slice(half * HEAD_DIM, (half + 1) * HEAD_DIM)
            lines = slice(head * HEAD_DIM, (head + 1) * HEAD_DIM)
            low = probs_ref[0, head]
            probs = low.astype(F32)
            dprobs = dot_nt(jnp.where(keep, grads, BF16(0)), values)
            delta = jnp.sum(probs * dprobs, axis=-1, keepdims=True)
            dscore = probs * (dprobs - delta)
            for chunk in range(padded // LANES):
                ds_ref[chunk, pl.ds(head, BLOCK, stride=16), :] = dscore[
                    :, chunk * LANES : (chunk + 1) * LANES
                ]
            dlow = dscore.astype(BF16)
            piece = dot(dlow, jnp.where(keep, key_rows, BF16(0)))
            total = piece if half == 0 else total + piece
            dk_ref[lines, :] += dot(turned_q[part, :], dlow)
            dv_ref[lines, :] += dot(turned_g[part, :], low)
        dm_ref[0, own, cols] = (total * SCALE).astype(BF16)

    group = 8
    low_bins = lax.broadcasted_iota(jnp.int32, (HALF, padded), 0).astype(BF16)

    def hits(picks, bins):
        return jnp.where(low_bins[:bins] == picks.astype(BF16), BF16(1), BF16(0))

    def count(step, carry):
        left, right = [], []
        for line in range(group):
            row = step * group + line
            at = pl.ds(row, 1)
            pick_x = box_ref[0, 0, 0, at, :] & (BOX_BINS - 1)
            pick_y = box_ref[0, 0, 1, at, :] & (BOX_BINS - 1)
            pick_p = pos_ref[0, 0, at, :] & (POS_BINS - 1)
            here = pl.ds(pl.multiple_of(row * 16, 16), 16)
            base = jnp.concatenate(
                [ds_ref[chunk, here, :] for chunk in range(padded // LANES)], axis=1
            )
            left.append(
                jnp.concatenate(
                    [
                        base.astype(BF16),
                        (base * (pick_x >> 5).astype(F32)).astype(BF16),
                        (base * (pick_y >> 5).astype(F32)).astype(BF16),
                        (base * (pick_p >> 4).astype(F32)).astype(BF16),
                    ],
                    axis=0,
                )
            )
            right.append(
                jnp.concatenate(
                    [
                        hits(pick_x & (HALF - 1), HALF),
                        hits(pick_y & (HALF - 1), HALF),
                        hits(pick_p & (HALF // 2 - 1), HALF // 2),
                    ],
                    axis=0,
                )
            )
        sums = dot_nt(jnp.concatenate(left, axis=1), jnp.concatenate(right, axis=1))
        bins_ref[:, : sums.shape[1]] += sums
        return carry

    live = jnp.minimum(BLOCK, (rows + group - 1) // group * group - block * BLOCK)
    lax.fori_loop(0, live // group, count, 0)

    @pl.when(block == pl.num_programs(1) - 1)
    def _():
        dm_ref[0, :, width : 2 * width] = dk_ref[...].astype(BF16).T
        dm_ref[0, :, 2 * width :] = dv_ref[...].astype(BF16).T


def attend_back(qkv, probs, d_attended, pos_buckets, box_buckets):
    docs, padded, width = qkv.shape[0], qkv.shape[1], qkv.shape[2] // 3
    heads, rows = probs.shape[1], pos_buckets.shape[2]
    return pl.pallas_call(
        partial(attend_back_kernel, rows),
        out_shape=(
            jax.ShapeDtypeStruct((docs, padded, 3 * width), BF16),
            jax.ShapeDtypeStruct((64, LANES), F32),
        ),
        grid=(docs, padded // BLOCK),
        in_specs=[
            pl.BlockSpec((1, BLOCK, width), lambda d, i: (d, i, 0)),
            pl.BlockSpec((1, padded, width), lambda d, i: (d, 0, 1)),
            pl.BlockSpec((1, padded, width), lambda d, i: (d, 0, 2)),
            pl.BlockSpec((1, heads, BLOCK, padded), lambda d, i: (d, 0, i, 0)),
            pl.BlockSpec((1, BLOCK, width), lambda d, i: (d, i, 0)),
            pl.BlockSpec((1, 1, BLOCK, padded), lambda d, i: (d, 0, i, 0)),
            pl.BlockSpec((1, 1, 2, BLOCK, padded), lambda d, i: (d, 0, 0, i, 0)),
        ],
        out_specs=(
            pl.BlockSpec((1, padded, 3 * width), lambda d, i: (d, 0, 0)),
            pl.BlockSpec((64, LANES), lambda d, i: (0, 0)),
        ),
        scratch_shapes=[
            pltpu.VMEM((width, padded), F32),
            pltpu.VMEM((width, padded), F32),
            pltpu.VMEM((padded // LANES, BLOCK * 16, LANES), F32),
        ],
        compiler_params=params(2),
        name="attend_back",
    )(qkv, qkv, qkv, probs, d_attended, pos_buckets, box_buckets)


def table_entries(table):
    heads = table.shape[1]
    lines = table.astype(F32).T * SCALE
    boxes = lines[:, POS_BINS:]
    spots = jnp.pad(lines[:, :POS_BINS], ((0, 0), (0, LANES - POS_BINS)))
    return jnp.concatenate([boxes, spots], axis=0).reshape(2 * heads, LANES)


def table_grad(bins, heads):
    base, upper = bins[:heads], (bins[16 : 16 + heads], bins[32 : 32 + heads], bins[48 : 48 + heads])
    pieces = []
    for which, (first, size) in enumerate(((0, HALF), (HALF, HALF), (2 * HALF, HALF // 2))):
        high = upper[which][:, first : first + size]
        pieces.append(jnp.concatenate([base[:, first : first + size] - high, high], axis=1))
    return jnp.concatenate([pieces[2], pieces[0], pieces[1]], axis=1).T * SCALE


def local_step(lengths, pos_buckets, box_buckets, layer_input, cotangent, weights, vectors, up_row, table):
    w_qkv, w_out, w_up, w_down = weights
    heads, width = table.shape[1], layer_input.shape[3]
    docs, rows = layer_input.shape[0], layer_input.shape[2]
    bias = bias_rows(lengths, table_entries(table), pos_buckets, box_buckets, heads)
    qkv = project(layer_input, w_qkv, vectors)
    probs, attended = attend(qkv, bias)
    result, d_one, low, active, d_upper, d_ffn, d_branch, d_attended, sums, up_sum = dense(
        layer_input, attended, cotangent, w_out, w_up, w_down, vectors, up_row
    )

    def across(left, right):
        left, right = (item.reshape(-1, item.shape[-1]) for item in (left, right))
        return lax.dot_general(left, right, (((0,), (0,)), ((), ())), preferred_element_type=F32)

    d_down = across(active, d_ffn)
    d_up = across(low, d_upper)
    d_out = across(attended, d_branch)
    d_mixed, bins = attend_back(qkv, probs, d_attended, pos_buckets, box_buckets)
    padded = d_mixed.shape[1]
    tok = jnp.pad(layer_input[:, 0], ((0, 0), (0, padded - rows), (0, 0)))
    d_qkv = across(tok, d_mixed)
    flat = d_mixed.reshape(docs * padded, 3 * width)
    back = dot_nt(flat, w_qkv).reshape(docs, padded, width)
    input_grad = (d_one + back)[:, None, :rows]
    mixed_sum = jnp.sum(flat.astype(F32), axis=0)
    return (
        result, input_grad, d_qkv, d_out, d_up, d_down, sums, up_sum, mixed_sum,
        table_grad(bins, heads),
    )


def body(
    layer_input, text_lengths, pos_buckets, box_buckets, w_qkv, w_out, w_up, w_down,
    norm_gains, norm_shifts, proj_biases, up_bias, rel_tables, cotangent,
):
    axes = ("dp", "fsdp")
    width = layer_input.shape[3]
    hidden = w_up.shape[1]
    table = lax.all_gather(rel_tables, "fsdp", axis=0, tiled=True)
    own = norm_gains.shape[1]
    small = jnp.concatenate(
        [
            jnp.concatenate([norm_gains, norm_shifts, proj_biases], axis=0).reshape(-1),
            up_bias,
        ]
    )
    every = lax.all_gather(small, axes, axis=0)
    devices = every.shape[0]
    vectors = every[:, : 8 * own].reshape(devices, 8, own)
    vectors = jnp.transpose(vectors, (1, 0, 2)).reshape(8, width).astype(F32)
    up_row = every[:, 8 * own :].reshape(1, hidden).astype(F32)
    weights = tuple(
        lax.all_gather(item, axes, axis=0, tiled=True) for item in (w_qkv, w_out, w_up, w_down)
    )
    (
        result, input_grad, d_qkv, d_out, d_up, d_down, sums, up_sum, mixed_sum, d_table,
    ) = local_step(
        text_lengths[:, 0], pos_buckets, box_buckets, layer_input, cotangent, weights, vectors,
        up_row, table,
    )
    shards = [
        lax.psum_scatter(item.astype(BF16), axes, scatter_dimension=0, tiled=True).astype(F32)
        for item in (d_qkv, d_out, d_up, d_down)
    ]
    sums = sums.at[4].set(mixed_sum[:width]).at[5].set(mixed_sum[2 * width :])
    sums, up_sum, d_table = lax.psum((sums, up_sum, d_table), axes)
    place = lax.axis_index(axes)
    sums = lax.dynamic_slice_in_dim(sums, place * own, own, 1)
    up_sum = lax.dynamic_slice_in_dim(up_sum[0], place * up_bias.shape[0], up_bias.shape[0], 0)
    table_rows = rel_tables.shape[0]
    d_table = lax.dynamic_slice_in_dim(d_table, lax.axis_index("fsdp") * table_rows, table_rows, 0)
    return (
        result, input_grad, *shards, sums[0:2], sums[2:4], sums[4:8], up_sum, d_table,
    )


def solution(mesh):
    both = ("dp", "fsdp")
    docs = P(None, both, None, None)
    return jax.shard_map(
        body,
        mesh=mesh,
        in_specs=(
            docs, P(None, both), docs, P(None, both, None, None, None),
            P(both, None), P(both, None), P(both, None), P(both, None),
            P(None, both), P(None, both), P(None, both), P(both), P("fsdp", None), docs,
        ),
        out_specs=(
            docs, docs, P(both, None), P(both, None), P(both, None), P(both, None),
            P(None, both), P(None, both), P(None, both), P(both), P("fsdp", None),
        ),
        check_vma=False,
    )
```

time: 2010 us -> 829 us (0.41)
  matrix products: 1180 us -> 49.5 us
  local copies, waits for them, and re-layouts: 549 us -> 43.2 us
  Pallas kernels: 0 us -> 329 us
  waiting for transfers between devices: 2.72 us -> 276 us
  blocking collectives: 200 us -> 90.2 us
  other arithmetic: 60.3 us -> 17.3 us
    dot_general x46 -> x5, matrix products: 1110 us -> 49.5 us  [the longest x4 41.5 us: across(): lax.dot_general(left, right, (((0,), (0,)), ((), ())), preferred_element_...]
    pallas_call x0 -> x5, Pallas kernels: none -> 329 us  [the longest x1 157 us: attend_back(): pl.pallas_call(partial(attend_back_kernel, rows), out_shape=(jax.ShapeDty...]
    reduce_scatter x3 -> x4, waiting for transfers between devices: 0.01 us -> 214 us  [body(): lax.psum_scatter(item.astype(BF16), axes, scatter_dimension=0, tiled=True)]
    reshape x6 -> x1, local copies, waits for them, and re-layouts: 211 us -> 0.08 us  [body(): jnp.concatenate([norm_gains, norm_shifts, proj_biases], axis=0).reshape(-1)]
    transpose x2 -> x0, local copies, waits for them, and re-layouts: 117 us -> none  [bucket_bias(): jnp.transpose(parts, (1, 0, 2, 3)).reshape(heads, count * QUERY_BLOCK, cols)]
    all_gather x3 -> x0, blocking collectives: 115 us -> none  [the longest x1 40.1 us: fetch_weights(): lax.all_gather(norm_gains, ('dp', 'fsdp'), axis=1, tiled=True)]
    pad x8 -> x0, local copies, waits for them, and re-layouts: 62.6 us -> none  [the longest x2 46.5 us: bucket_grad(): jnp.pad(dscore, ((0, 0), (0, count * QUERY_BLOCK - rows), (0, 0)))]
    sub x2 -> x0, matrix products: 60.5 us -> none  [attend_back(): dscore = attn_probs * (dprobs - row_delta) * 0.125]
  transfers between devices with their start and end apart: 8 -> 8, of which waited for: 0 -> 3; matrix products, arithmetic and copies ran while one was open for 79% -> 12% of each run, Pallas kernels for 0% -> 34%
where the time goes in v1:
time: 829 us; the launch traced here: 820 us
  Pallas kernels  329 us (40%)
  waiting for transfers between devices  276 us (33%)
  blocking collectives  90.2 us (11%)
  matrix products  49.5 us (6%)
  local copies, waits for them, and re-layouts  43.2 us (5%)
  other arithmetic  17.3 us (2%)
  between operations  14.8 us (2%)
    reduce_scatter x4, waiting for transfers between devices, body(): lax.psum_scatter(item.astype(BF16), axes, scatter_dimension=0, tiled=True)  214 us
    pallas_call x1, Pallas kernels, attend_back(): pl.pallas_call(partial(attend_back_kernel, rows), out_shape=(jax.ShapeDty...  157 us
    pallas_call x1, Pallas kernels, bias_rows(): pl.pallas_call(partial(bias_kernel, rows), out_shape=jax.ShapeDtypeStruct...  69.4 us
    all_gather x4, waiting for transfers between devices, body(): lax.all_gather(item, axes, axis=0, tiled=True)  59.4 us
    pallas_call x1, Pallas kernels, dense(): pl.pallas_call(partial(dense_kernel, rows), out_shape=(jax.ShapeDtypeStru...  52.4 us
    unnamed x1, blocking collectives  42.4 us
    psum x1, blocking collectives, body(): sums, up_sum, d_table = lax.psum((sums, up_sum, d_table), axes)  42.2 us
    dot_general x4, matrix products, across(): lax.dot_general(left, right, (((0,), (0,)), ((), ())), preferred_element_...  41.5 us
  transfers between devices with their start and end apart: 8, of which 3 were waited for; matrix products, arithmetic and copies ran while one was open for 12% of the time, Pallas kernels for 34%

profile of v1, /device:TPU:0, one launch (start us, length us, event | category | flops | bytes accessed | tf_op | source)
XLA Modules:
  0.0 820.2 jit_solution(7857273750140527223)
XLA Ops:
  10.1 3.3 copy.60.x_ref
  13.3 5.0 copy.64
  18.8 42.4 %all-reduce.1 = bf16[9216]{0:T(1024)(128)(2,1)S(1)} all-reduce(bf16[9216]{0:T(1024)(128)(2,1)S(1)} %dynamic-update-slice.6), channel_id=2, replica_groups=mesh['dp'=8,'fsdp'=4] {'dp','fsdp'}, use_global_device_ids=true, to_apply=%add.1 | all-reduce | flops 9216 | bytes 36864
  62.2 5.6 all-gather.1
  67.9 8.0 copy.59.box_ref
  75.8 2.4 copy.58.pos_ref
  81.3 69.4 %bias_rows.1.bias_ref = f32[2,12,768,768]{3,2,1,0:T(8,128)} custom-call(s32[2]{0:T(128)} %bitcast.38, f32[24,128]{1,0:T(8,128)} %pad_maximum_fusion.tab_ref, s32[2,1,709,709]{3,2,1,0:T(8,128)} %copy.58.pos_ref, s32[2,1,2,709,709]{4,3,2,1,0:T(8,128)} %copy.59.box_ref), custom_call_target="tpu_custom_call" | custom-call | flops 36193032 | bytes 70778880 | tf_op jit(solution)/shard_map/bias_rows/pallas_call | solution.py:91
  150.7 9.7 %project.1.q_ref.k_ref.v_ref = bf16[2,768,2304]{2,1,0:T(8,128)(2,1)} custom-call(bf16[2,1,709,768]{3,2,1,0:T(8,128)(2,1)} %copy.60.x_ref, bf16[768,2304]{1,0:T(8,128)(2,1)} %all-gather.7.cloned.1.call-done.w_ref, f32[8,768]{1,0:T(8,128)} %reshape.113.vec_ref), custom_call_target="tpu_custom_call" | custom-call | tf_op jit(solution)/shard_map/project/pallas_call | solution.py:125
  160.5 40.8 %attend.1 = (bf16[2,12,768,768]{3,2,1,0:T(8,128)(2,1)}, bf16[2,768,768]{2,1,0:T(8,128)(2,1)}) custom-call(bf16[2,768,2304]{2,1,0:T(8,128)(2,1)} %project.1.q_ref.k_ref.v_ref, bf16[2,768,2304]{2,1,0:T(8,128)(2,1)} %project.1.q_ref.k_ref.v_ref, bf16[2,768,2304]{2,1,0:T(8,128)(2,1)} %project.1.q_ref.k_ref.v_ref, f32[2,12,768,768]{3,2,1,0:T(8,128)} %bias_rows.1.bias_ref), custom_call_target="tpu_custom_call" | custom-call | tf_op jit(solution)/shard_map/attend/pallas_call | solution.py:163
  201.3 59.4 %all-gather.13.cloned.1.call-done.wd_ref = bf16[3072,768]{1,0:T(8,128)(2,1)} async-done(((bf16[96,768]{1,0:T(8,128)(2,1)}), bf16[3072,768]{1,0:T(8,128)(2,1)}) %all-gather.13.cloned.1.call-update) | async-done | bytes 4718608 | tf_op jit(solution)/shard_map/all_gather | solution.py:496
  260.7 52.4 %dense.1 = (bf16[2,1,709,768]{3,2,1,0:T(8,128)(2,1)}, f32[2,768,768]{2,1,0:T(8,128)}, bf16[2,768,768]{2,1,0:T(8,128)(2,1)}, bf16[2,768,3072]{2,1,0:T(8,128)(2,1)...) custom-call(bf16[2,1,709,768]{3,2,1,0:T(8,128)(2,1)} %copy.60.x_ref,, ...), custom_call_target="tpu_custom_call" | custom-call | tf_op jit(solution)/shard_map/dense/pallas_call | solution.py:264
  313.1 4.8 bitcast_convert_fusion.3
  317.9 156.8 %attend_back.1 = (bf16[2,768,2304]{2,1,0:T(8,128)(2,1)}, f32[64,128]{1,0:T(8,128)}) custom-call(bf16[2,768,2304]{2,1,0:T(8,128)(2,1)} %project.1.q_ref.k_ref.v_ref, bf16[2,768,2304]{2,1,0:T(8,128)(2,1)} %project.1.q_ref.k_ref.v_ref, bf16[2,768,2304]{2,1,0:T(8,128)(2,1)} %project.1.q_ref.k_ref.v_ref, bf16[2,12,768,768]{3,2,1,0:T(8,128)(2,1)} %get-tuple-element.52.probs_ref, ...), custom_call_target="tpu_custom_call" | custom-call | tf_op jit(solution)/shard_map/attend_back/pallas_call | solution.py:396
  474.7 10.4 %bitcast_convert_fusion.2 = bf16[768,2304]{1,0:T(8,128)(2,1)} fusion(bf16[2,768,2304]{2,1,0:T(8,128)(2,1)} %get-tuple-element.54, bf16[2,709,768]{1,2,0:T(8,128)(2,1)S(1)} %bitcast.34), kind=kOutput, calls=%fused_computation.3 | convolution fusion | flops 5437587456 | bytes 12794880 | tf_op jit(solution)/shard_map/dot_general | solution.py:456
  485.2 13.4 %bitcast_convert_fusion = bf16[3072,768]{1,0:T(8,128)(2,1)} fusion(bf16[2,768,3072]{2,1,0:T(8,128)(2,1)} %get-tuple-element.58, bf16[2,768,768]{2,1,0:T(8,128)(2,1)S(1)} %copy-done.13), kind=kOutput, calls=%fused_computation.1 | convolution fusion | flops 7250116608 | bytes 16515072 | tf_op jit(solution)/shard_map/dot_general | solution.py:456
  500.3 13.0 %bitcast_convert_fusion.1 = bf16[768,3072]{1,0:T(8,128)(2,1)} fusion(bf16[2,768,768]{2,1,0:T(8,128)(2,1)S(1)} %copy-done.12, bf16[2,768,3072]{2,1,0:T(8,128)(2,1)} %get-tuple-element.57), kind=kOutput, calls=%fused_computation.2 | convolution fusion | flops 7250116608 | bytes 16515072 | tf_op jit(solution)/shard_map/dot_general | solution.py:456
  513.3 4.4 convert_reduce_fusion
  524.9 42.2 %all-reduce.2 = (f32[8,768]{1,0:T(8,128)}, f32[1,3072]{1,0:T(1,128)}, f32[160,12]{0,1:T(8,128)}) all-reduce(f32[8,768]{1,0:T(8,128)} %scatter.9, f32[1,3072]{1,0:T(1,128)} %get-tuple-element.61, f32[160,12]{0,1:T(8,128)S(1)} %multiply_bitcast_fusion), channel_id=1, replica_groups=mesh['dp'=8,'fsdp'=4] {'dp','fsdp'}, use_global_device_ids=true, to_apply=%region_5.6 | all-reduce | flops 11136 | bytes 89088 | tf_op jit(solution)/shard_map/psum | solution.py:509
  568.4 7.9 fusion.1
  576.3 2.8 fusion
  579.1 6.5 copy.69
  585.7 4.7 copy.68
  595.8 103.0 %reduce-scatter.11.cloned.1.call-done = bf16[96,768]{1,0:T(8,128)(2,1)} async-done(((bf16[3072,768]{1,0:T(8,128)(2,1)}), bf16[96,768]{1,0:T(8,128)(2,1)}) %reduce-scatter.11.cloned.1.call-update) | async-done | bytes 147472 | tf_op jit(solution)/shard_map/reduce_scatter | solution.py:505
  700.5 110.8 %reduce-scatter.9.cloned.1.call-done = bf16[24,3072]{1,0:T(8,128)(2,1)} async-done(((bf16[768,3072]{1,0:T(8,128)(2,1)}), bf16[24,3072]{1,0:T(8,128)(2,1)}) %reduce-scatter.9.cloned.1.call-update) | async-done | bytes 147472 | tf_op jit(solution)/shard_map/reduce_scatter | solution.py:505
  (90 shorter events, 26.5 us)
Async XLA Ops:
  7.2 6.2 copy-start
  7.2 143.5 %all-gather.7.cloned.1.call-start = ((), (), s32[]{:S(2)}) async-start(), calls=%async_computation.4 | async-start | bytes 3649536 | tf_op jit(solution)/shard_map/all_gather | solution.py:496
  7.9 193.4 %all-gather.9.cloned.1.call-start = ((), (), s32[]{:S(2)}) async-start(), calls=%async_computation.5 | async-start | bytes 1216512 | tf_op jit(solution)/shard_map/all_gather | solution.py:496
  8.7 192.6 %all-gather.11.cloned.1.call-start = ((), (), s32[]{:S(2)}) async-start(), calls=%async_computation.6 | async-start | bytes 4866048 | tf_op jit(solution)/shard_map/all_gather | solution.py:496
  9.4 251.3 %all-gather.13.cloned.1.call-start = ((), (), s32[]{:S(2)}) async-start(), calls=%async_computation.7 | async-start | bytes 4866048 | tf_op jit(solution)/shard_map/all_gather | solution.py:496
  10.0 582.8 %reduce-scatter.7.cloned.1.call-start = ((), (), s32[]{:S(2)}) async-start(), calls=%async_computation.9 | async-start | bytes 1216512 | tf_op jit(solution)/shard_map/reduce_scatter | solution.py:505
  10.0 8.3 %copy-start.7 = (bf16[4,24]{1,0:T(4,128)(2,1)S(1)}, bf16[4,24]{1,0:T(4,128)(2,1)}, u32[]{:S(2)}) copy-start(bf16[4,24]{1,0:T(4,128)(2,1)} %param.28) | copy-start | bytes 580
  10.0 8.3 %copy-start.10 = (bf16[2,24]{1,0:T(2,128)(2,1)S(1)}, bf16[2,24]{1,0:T(2,128)(2,1)}, u32[]{:S(2)}) copy-start(bf16[2,24]{1,0:T(2,128)(2,1)} %param.27) | copy-start | bytes 292
  10.1 8.3 %copy-start.11 = (bf16[2,24]{1,0:T(2,128)(2,1)S(1)}, bf16[2,24]{1,0:T(2,128)(2,1)}, u32[]{:S(2)}) copy-start(bf16[2,24]{1,0:T(2,128)(2,1)} %param.26) | copy-start | bytes 292
  10.1 8.4 %copy-start.9 = (bf16[96]{0:T(256)(128)(2,1)S(1)}, bf16[96]{0:T(256)(128)(2,1)}, u32[]{:S(2)}) copy-start(bf16[96]{0:T(256)(128)(2,1)} %param.29) | copy-start | bytes 580
  10.1 52.1 %copy-start.5 = (bf16[40,12]{0,1:T(8,128)(2,1)S(1)}, bf16[40,12]{0,1:T(8,128)(2,1)}, u32[]{:S(2)}) copy-start(bf16[40,12]{0,1:T(8,128)(2,1)} %param.30) | copy-start | bytes 2884
  61.4 14.4 %slice-start = ((s8[4356096]{0:T(1024)(128)(4,1)}), s8[161792]{0:T(1024)(128)(4,1)S(1)}, s32[]{:S(2)}) async-start(s8[4356096]{0:T(1024)(128)(4,1)} %bitcast.32), calls=%async_computation.12 | async-start | bytes 323584
  67.9 8.0 slice-start.1
  75.8 3.1 copy-start.4
  78.2 2.4 copy-start.8
  260.7 52.4 %copy-start.3 = (bf16[2,768,768]{2,1,0:T(8,128)(2,1)S(1)}, bf16[2,768,768]{2,1,0:T(8,128)(2,1)}, u32[]{:S(2)}) copy-start(bf16[2,768,768]{2,1,0:T(8,128)(2,1)} %get-tuple-element.49.o_ref) | copy-start | bytes 7077892
  317.9 276.4 %reduce-scatter.5.cloned.1.call-start = ((), (), s32[]{:S(2)}) async-start(), calls=%async_computation.8 | async-start | bytes 3649536 | tf_op jit(solution)/shard_map/reduce_scatter | solution.py:505
  317.9 156.8 %copy-start.2 = (bf16[2,1,709,768]{2,3,0,1:T(8,128)(2,1)S(1)}, bf16[2,1,709,768]{2,3,0,1:T(8,128)(2,1)}, u32[]{:S(2)}) copy-start(bf16[2,1,709,768]{2,3,0,1:T(8,128)(2,1)} %copy.64) | copy-start | bytes 6534148
  474.7 10.5 %copy-start.13 = (bf16[2,768,768]{2,1,0:T(8,128)(2,1)S(1)}, bf16[2,768,768]{2,1,0:T(8,128)(2,1)}, u32[]{:S(2)}) copy-start(bf16[2,768,768]{2,1,0:T(8,128)(2,1)} %get-tuple-element.59) | copy-start | bytes 7077892
  485.1 213.8 %reduce-scatter.11.cloned.1.call-start = ((), (), s32[]{:S(2)}) async-start(), calls=%async_computation.11 | async-start | bytes 4866048 | tf_op jit(solution)/shard_map/reduce_scatter | solution.py:505
  498.5 1.7 copy-start.12
  498.6 312.7 %reduce-scatter.9.cloned.1.call-start = ((), (), s32[]{:S(2)}) async-start(), calls=%async_computation.10 | async-start | bytes 4866048 | tf_op jit(solution)/shard_map/reduce_scatter | solution.py:505
  513.3 55.0 %copy-start.1 = (bf16[768,2304]{1,0:T(8,128)(2,1)S(1)}, bf16[768,2304]{1,0:T(8,128)(2,1)}, u32[]{:S(2)}) copy-start(bf16[768,2304]{1,0:T(8,128)(2,1)} %all-gather.7.cloned.1.call-done.w_ref) | copy-start | bytes 10616836
  579.1 12.5 %copy-start.6 = (f32[160,12]{0,1:T(8,128)S(1)}, f32[160,12]{0,1:T(8,128)}, u32[]{:S(2)}) copy-start(f32[160,12]{0,1:T(8,128)} %get-tuple-element.98) | copy-start | bytes 23044
Sparse Core Ops, SparseCore 0:
  10.9 63.2 all-gather.6
  77.1 52.9 all-gather.8
  133.0 62.4 all-gather.10
  198.3 62.3 all-gather.12
  318.0 95.0 reduce-scatter.6
  485.2 102.2 reduce-scatter.4
  593.0 105.8 reduce-scatter.10
  705.2 106.0 reduce-scatter.8

commit v2 on v1

--- a/solution.py
+++ b/solution.py
@@ -40,6 +40,10 @@
 def resident(shape):
     zeros = (0,) * len(shape)
     return pl.BlockSpec(shape, lambda *_: zeros, pipeline_mode=pl.Buffered(1))
+
+
+def columns(shape, place):
+    return pl.BlockSpec(shape, lambda *_: (0, place), pipeline_mode=pl.Buffered(1))
 
 
 def live_rows(values, rows, first):
@@ -109,9 +113,10 @@
     )(lengths, entries, pos_buckets, box_buckets)
 
 
-def project_kernel(rows, x_ref, w_ref, vec_ref, out_ref):
+def project_kernel(rows, x_ref, w_ref, vec_ref, out_ref, tok_ref):
     width = x_ref.shape[3]
     block = live_rows(x_ref[0, 0], rows, pl.program_id(1) * x_ref.shape[2])
+    tok_ref[0] = block
     queries = dot(block, w_ref[:, :width]) + vec_ref[4:5, :]
     out_ref[0, :, :width] = queries.astype(BF16) * BF16(SCALE)
     out_ref[0, :, width : 2 * width] = dot(block, w_ref[:, width : 2 * width]).astype(BF16)
@@ -119,22 +124,28 @@
     out_ref[0, :, 2 * width :] = values.astype(BF16)
 
 
-def project(layer_input, w_qkv, vectors):
+def project(layer_input, w_mixed, vectors):
     docs, unused, rows, width = layer_input.shape
     padded = pl.cdiv(rows, BLOCK) * BLOCK
     return pl.pallas_call(
         partial(project_kernel, rows),
-        out_shape=jax.ShapeDtypeStruct((docs, padded, 3 * width), BF16),
+        out_shape=(
+            jax.ShapeDtypeStruct((docs, padded, 3 * width), BF16),
+            jax.ShapeDtypeStruct((docs, padded, width), BF16),
+        ),
         grid=(docs, padded // DENSE_BLOCK),
         in_specs=[
             pl.BlockSpec((1, 1, DENSE_BLOCK, width), lambda d, i: (d, 0, i, 0)),
-            resident(w_qkv.shape),
+            columns((width, 3 * width), 0),
             resident(vectors.shape),
         ],
-        out_specs=pl.BlockSpec((1, DENSE_BLOCK, 3 * width), lambda d, i: (d, i, 0)),
+        out_specs=(
+            pl.BlockSpec((1, DENSE_BLOCK, 3 * width), lambda d, i: (d, i, 0)),
+            pl.BlockSpec((1, DENSE_BLOCK, width), lambda d, i: (d, i, 0)),
+        ),
         compiler_params=params(2),
         name="project",
-    )(layer_input, w_qkv, vectors)
+    )(layer_input, w_mixed, vectors)
 
 
 def attend_kernel(q_ref, k_ref, v_ref, bias_ref, probs_ref, out_ref):
@@ -251,9 +262,9 @@
     do_ref[0] = dot_nt(d_branch, wo_ref[...]).astype(BF16)
 
 
-def dense(layer_input, attended, cotangent, w_out, w_up, w_down, vectors, up_row):
+def dense(layer_input, attended, cotangent, w_mixed, w_down, vectors, up_row):
     docs, unused, rows, width = layer_input.shape
-    padded, hidden = attended.shape[1], w_up.shape[1]
+    padded, hidden = attended.shape[1], w_down.shape[0]
     ragged = pl.BlockSpec((1, 1, DENSE_BLOCK, width), lambda d, i: (d, 0, i, 0))
     narrow = pl.BlockSpec((1, DENSE_BLOCK, width), lambda d, i: (d, i, 0))
     wide = pl.BlockSpec((1, DENSE_BLOCK, hidden), lambda d, i: (d, i, 0))
@@ -278,7 +289,8 @@
         grid=(docs, padded // DENSE_BLOCK),
         in_specs=[
             ragged, narrow, ragged,
-            resident(w_out.shape), resident(w_up.shape), resident(w_down.shape),
+            columns((width, width), 3), columns((width, hidden), 4 * width // hidden),
+            resident(w_down.shape),
             resident(vectors.shape), resident(up_row.shape),
         ],
         out_specs=(
@@ -289,7 +301,7 @@
         scratch_shapes=[pltpu.VMEM((DENSE_BLOCK, hidden), F32)],
         compiler_params=params(2),
         name="dense",
-    )(layer_input, attended, cotangent, w_out, w_up, w_down, vectors, up_row)
+    )(layer_input, attended, cotangent, w_mixed, w_mixed, w_down, vectors, up_row)
 
 
 def attend_back_kernel(
@@ -338,7 +350,7 @@
             dv_ref[lines, :] += dot(turned_g[part, :], low)
         dm_ref[0, own, cols] = (total * SCALE).astype(BF16)
 
-    group = 8
+    group = 16
     low_bins = lax.broadcasted_iota(jnp.int32, (HALF, padded), 0).astype(BF16)
 
     def hits(picks, bins):
@@ -440,35 +452,339 @@
     return jnp.concatenate([pieces[2], pieces[0], pieces[1]], axis=1).T * SCALE
 
 
-def local_step(lengths, pos_buckets, box_buckets, layer_input, cotangent, weights, vectors, up_row, table):
-    w_qkv, w_out, w_up, w_down = weights
+def branch_up_grads(attended, d_branch, low, d_upper):
+    rows, width = attended.shape
+    parts = 1 + d_upper.shape[1] // width
+
+    def kernel(a_ref, b_ref, l_ref, u_ref, out_ref, turned_ref):
+        part = pl.program_id(0)
+
+        @pl.when(part == 0)
+        def _():
+            out_ref[...] = dot(a_ref[...].T, b_ref[...]).astype(BF16)
+            turned_ref[...] = l_ref[...].T
+
+        @pl.when(part > 0)
+        def _():
+            out_ref[...] = dot(turned_ref[...], u_ref[...]).astype(BF16)
+
+    return pl.pallas_call(
+        kernel,
+        out_shape=jax.ShapeDtypeStruct((width, parts * width), BF16),
+        grid=(parts,),
+        in_specs=[
+            resident((rows, width)),
+            resident((rows, width)),
+            resident((rows, width)),
+            pl.BlockSpec((rows, width), lambda p: (0, jnp.maximum(p - 1, 0))),
+        ],
+        out_specs=pl.BlockSpec((width, width), lambda p: (0, p)),
+        scratch_shapes=[pltpu.VMEM((width, rows), BF16)],
+        compiler_params=params(1),
+        cost_estimate=pl.CostEstimate(
+            flops=2 * rows * width * width * parts, transcendentals=0,
+            bytes_accessed=2 * rows * width * (parts + 3),
+        ),
+        name="branch_up_grads",
+    )(attended, d_branch, low, d_upper)
+
+
+def down_grads(active, d_ffn):
+    rows, width = d_ffn.shape
+    parts = active.shape[1] // width
+
+    def kernel(g_ref, f_ref, out_ref):
+        out_ref[...] = dot(g_ref[...].T, f_ref[...]).astype(BF16)
+
+    return pl.pallas_call(
+        kernel,
+        out_shape=jax.ShapeDtypeStruct((parts * width, width), BF16),
+        grid=(parts,),
+        in_specs=[pl.BlockSpec((rows, width), lambda p: (0, p)), resident((rows, width))],
+        out_specs=pl.BlockSpec((width, width), lambda p: (p, 0)),
+        compiler_params=params(1),
+        cost_estimate=pl.CostEstimate(
+            flops=2 * rows * width * width * parts, transcendentals=0,
+            bytes_accessed=2 * rows * width * (parts + 2),
+        ),
+        name="down_grads",
+    )(active, d_ffn)
+
+
+def mixed_grads(tok, d_mixed):
+    rows, width = tok.shape
+    parts = d_mixed.shape[1] // width
+
+    def kernel(t_ref, m_ref, out_ref, turned_ref):
+        @pl.when(pl.program_id(0) == 0)
+        def _():
+            turned_ref[...] = t_ref[...].T
+
+        out_ref[...] = dot(turned_ref[...], m_ref[...]).astype(BF16)
+
+    return pl.pallas_call(
+        kernel,
+        out_shape=jax.ShapeDtypeStruct((width, parts * width), BF16),
+        grid=(parts,),
+        in_specs=[resident((rows, width)), pl.BlockSpec((rows, width), lambda p: (0, p))],
+        out_specs=pl.BlockSpec((width, width), lambda p: (0, p)),
+        scratch_shapes=[pltpu.VMEM((width, rows), BF16)],
+        compiler_params=params(1),
+        cost_estimate=pl.CostEstimate(
+            flops=2 * rows * width * width * parts, transcendentals=0,
+            bytes_accessed=2 * rows * width * (parts + 2),
+        ),
+        name="mixed_grads",
+    )(tok, d_mixed)
+
+
+def input_grads(d_mixed, d_one, w_mixed, rows):
+    docs, padded, width = d_one.shape
+
+    def kernel(m_ref, d_ref, w_ref, out_ref, sum_ref):
+        @pl.when((pl.program_id(0) == 0) & (pl.program_id(1) == 0))
+        def _():
+            sum_ref[...] = jnp.zeros_like(sum_ref)
+
+        block = m_ref[0]
+        out_ref[0, 0] = d_ref[0] + dot_nt(block, w_ref[...])
+        sum_ref[...] += jnp.sum(block.astype(F32), axis=0, keepdims=True)
+
+    return pl.pallas_call(
+        kernel,
+        out_shape=(
+            jax.ShapeDtypeStruct((docs, 1, rows, width), F32),
+            jax.ShapeDtypeStruct((1, 3 * width), F32),
+        ),
+        grid=(docs, padded // DENSE_BLOCK),
+        in_specs=[
+            pl.BlockSpec((1, DENSE_BLOCK, 3 * width), lambda d, i: (d, i, 0)),
+            pl.BlockSpec((1, DENSE_BLOCK, width), lambda d, i: (d, i, 0)),
+            columns((width, 3 * width), 0),
+        ],
+        out_specs=(
+            pl.BlockSpec((1, 1, DENSE_BLOCK, width), lambda d, i: (d, 0, i, 0)),
+            pl.BlockSpec((1, 3 * width), lambda d, i: (0, 0)),
+        ),
+        compiler_params=params(2),
+        name="input_grads",
+    )(d_mixed, d_one, w_mixed)
+
+
+def reduce_kernel(
+    dims, grad_ref, small_ref, out_ref, sums_ref,
+    got_c, one, got_xa, got_yb, two_a, two_b, got_ya, got_xb, three, got_z,
+    sums, got_s, send_sems, recv_sems,
+):
+    deep, across, along, cores = dims
+    dp, fsdp = lax.axis_index("dp"), lax.axis_index("fsdp")
+    z, x = dp // across, dp % across
+    y, c = fsdp // cores, fsdp % cores
+    width = grad_ref.shape[5]
+    cut = width // LANES // 2 * LANES
+    lower, upper = slice(0, cut), slice(cut, width)
+
+    def peer(axis, step):
+        place = [z, x, y, c]
+        place[axis] = (place[axis] + step) % dims[axis]
+        return place[axis], (place[0] * across + place[1], place[2] * cores + place[3])
+
+    barrier = pltpu.get_barrier_semaphore()
+    partners = 0
+    for axis in range(4):
+        for step in range(1, dims[axis]):
+            pl.semaphore_signal(
+                barrier, inc=1, device_id=peer(axis, step)[1], device_id_type=pl.DeviceIdType.MESH
+            )
+            partners += 1
+    pl.semaphore_wait(barrier, partners)
+
+    def exchange(stage, axis, source, target):
+        copies = []
+        for step in range(1, dims[axis]):
+            place, device = peer(axis, step)
+            copies.append(
+                pltpu.make_async_remote_copy(
+                    src_ref=source(place),
+                    dst_ref=target(step - 1),
+                    send_sem=send_sems.at[stage, step - 1],
+                    recv_sem=recv_sems.at[stage, step - 1],
+                    device_id=device,
+                    device_id_type=pl.DeviceIdType.MESH,
+                )
+            )
+        for copy in copies:
+            copy.start()
+        return copies
+
+    def finish(copies):
+        for copy in copies:
+            copy.wait()
+
+    def joined(own, others):
+        total = own.astype(F32)
+        for other in others:
+            total = total + other.astype(F32)
+        return total
+
+    def small_step(stage, axis, level):
+        own = small_ref if level == 0 else sums.at[level - 1]
+        first = sum(dims[later] - 1 for later in (3, 1, 2, 0)[:level])
+        return exchange(stage, axis, lambda place: own, lambda slot: got_s.at[first + slot])
+
+    def small_join(axis, level):
+        own = small_ref if level == 0 else sums.at[level - 1]
+        first = sum(dims[later] - 1 for later in (3, 1, 2, 0)[:level])
+        return joined(own[...], [got_s[first + slot] for slot in range(dims[axis] - 1)])
+
+    copies_c = exchange(0, 3, lambda t: grad_ref.at[:, :, :, t], lambda slot: got_c.at[slot])
+    copies_s = small_step(7, 3, 0)
+    finish(copies_s)
+    finish(copies_c)
+    sums[0] = small_join(3, 0)
+    copies_s = small_step(8, 1, 1)
+
+    def add_cores(k, carry):
+        for i in range(across):
+            for j in range(along):
+                one[k, i, j] = joined(
+                    grad_ref[k, i, j, c], [got_c[s, k, i, j] for s in range(cores - 1)]
+                ).astype(BF16)
+        return carry
+
+    lax.fori_loop(0, deep, add_cores, 0)
+    copies_xa = exchange(1, 1, lambda t: one.at[:, t, :, :, lower], lambda slot: got_xa.at[slot])
+    copies_yb = exchange(2, 2, lambda t: one.at[:, :, t, :, upper], lambda slot: got_yb.at[slot])
+    finish(copies_s)
+    sums[1] = small_join(1, 1)
+    copies_s = small_step(9, 2, 2)
+    finish(copies_xa)
+
+    def add_xa(k, carry):
+        for j in range(along):
+            two_a[k, j] = joined(
+                one[k, x, j, :, lower], [got_xa[s, k, j] for s in range(across - 1)]
+            ).astype(BF16)
+        return carry
+
+    lax.fori_loop(0, deep, add_xa, 0)
+    copies_ya = exchange(3, 2, lambda t: two_a.at[:, t], lambda slot: got_ya.at[slot])
+    finish(copies_yb)
+
+    def add_yb(k, carry):
+        for i in range(across):
+            two_b[k, i] = joined(
+                one[k, i, y, :, upper], [got_yb[s, k, i] for s in range(along - 1)]
+            ).astype(BF16)
+        return carry
+
+    lax.fori_loop(0, deep, add_yb, 0)
+    copies_xb = exchange(4, 1, lambda t: two_b.at[:, t], lambda slot: got_xb.at[slot])
+    finish(copies_s)
+    sums[2] = small_join(2, 2)
+    copies_s = small_step(10, 0, 3)
+    finish(copies_ya)
+
+    def add_ya(k, carry):
+        three[k, :, lower] = joined(
+            two_a[k, y], [got_ya[s, k] for s in range(along - 1)]
+        ).astype(BF16)
+        return carry
+
+    lax.fori_loop(0, deep, add_ya, 0)
+    copies_za = exchange(
+        5, 0, lambda t: three.at[t, :, lower], lambda slot: got_z.at[slot, :, lower]
+    )
+    finish(copies_xb)
+
+    def add_xb(k, carry):
+        three[k, :, upper] = joined(
+            two_b[k, x], [got_xb[s, k] for s in range(across - 1)]
+        ).astype(BF16)
+        return carry
+
+    lax.fori_loop(0, deep, add_xb, 0)
+    copies_zb = exchange(
+        6, 0, lambda t: three.at[t, :, upper], lambda slot: got_z.at[slot, :, upper]
+    )
+    finish(copies_s)
+    sums_ref[...] = small_join(0, 3)
+    finish(copies_za)
+    finish(copies_zb)
+    out_ref[...] = joined(three[z], [got_z[s] for s in range(deep - 1)])
+
+
+def reduce_tail(grad, small, dp, fsdp):
+    across = 1 << ((dp.bit_length() - 1) // 2)
+    across = across if dp % across == 0 else 1
+    cores = 2 if fsdp % 2 == 0 else 1
+    dims = (dp // across, across, fsdp // cores, cores)
+    deep, across, along, cores = dims
+    width = grad.shape[1]
+    rows = grad.shape[0] // (dp * fsdp)
+    cut = width // LANES // 2 * LANES
+    rest = width - cut
+    slots = sum(dims) - 4
+    vmem = pl.BlockSpec(memory_space=pltpu.VMEM)
+    most = max(max(dims) - 1, 1)
+
+    def held(*shape):
+        return pltpu.VMEM(tuple(max(item, 1) for item in shape), BF16)
+
+    return pl.pallas_call(
+        partial(reduce_kernel, dims),
+        out_shape=(
+            jax.ShapeDtypeStruct((rows, width), F32),
+            jax.ShapeDtypeStruct(small.shape, F32),
+        ),
+        in_specs=[vmem, vmem],
+        out_specs=(vmem, vmem),
+        scratch_shapes=[
+            held(cores - 1, deep, across, along, rows, width),
+            held(deep, across, along, rows, width),
+            held(across - 1, deep, along, rows, cut),
+            held(along - 1, deep, across, rows, rest),
+            held(deep, along, rows, cut),
+            held(deep, across, rows, rest),
+            held(along - 1, deep, rows, cut),
+            held(across - 1, deep, rows, rest),
+            held(deep, rows, width),
+            held(deep - 1, rows, width),
+            pltpu.VMEM((3,) + small.shape, F32),
+            pltpu.VMEM((slots,) + small.shape, F32),
+            pltpu.SemaphoreType.DMA((11, most)),
+            pltpu.SemaphoreType.DMA((11, most)),
+        ],
+        compiler_params=pltpu.CompilerParams(
+            collective_id=0, has_side_effects=True, vmem_limit_bytes=VMEM_LIMIT
+        ),
+        name="reduce_tail",
+    )(grad.reshape(deep, across, along, cores, rows, width), small)
+
+
+def local_step(lengths, pos_buckets, box_buckets, layer_input, cotangent, w_mixed, w_down, vectors, up_row, table):
     heads, width = table.shape[1], layer_input.shape[3]
     docs, rows = layer_input.shape[0], layer_input.shape[2]
     bias = bias_rows(lengths, table_entries(table), pos_buckets, box_buckets, heads)
-    qkv = project(layer_input, w_qkv, vectors)
+    qkv, tok = project(layer_input, w_mixed, vectors)
     probs, attended = attend(qkv, bias)
     result, d_one, low, active, d_upper, d_ffn, d_branch, d_attended, sums, up_sum = dense(
-        layer_input, attended, cotangent, w_out, w_up, w_down, vectors, up_row
-    )
-
-    def across(left, right):
-        left, right = (item.reshape(-1, item.shape[-1]) for item in (left, right))
-        return lax.dot_general(left, right, (((0,), (0,)), ((), ())), preferred_element_type=F32)
-
-    d_down = across(active, d_ffn)
-    d_up = across(low, d_upper)
-    d_out = across(attended, d_branch)
+        layer_input, attended, cotangent, w_mixed, w_down, vectors, up_row
+    )
+
+    def flat(item):
+        return item.reshape(-1, item.shape[-1])
+
+    d_down = down_grads(flat(active), flat(d_ffn))
+    d_branch_up = branch_up_grads(flat(attended), flat(d_branch), flat(low), flat(d_upper))
     d_mixed, bins = attend_back(qkv, probs, d_attended, pos_buckets, box_buckets)
-    padded = d_mixed.shape[1]
-    tok = jnp.pad(layer_input[:, 0], ((0, 0), (0, padded - rows), (0, 0)))
-    d_qkv = across(tok, d_mixed)
-    flat = d_mixed.reshape(docs * padded, 3 * width)
-    back = dot_nt(flat, w_qkv).reshape(docs, padded, width)
-    input_grad = (d_one + back)[:, None, :rows]
-    mixed_sum = jnp.sum(flat.astype(F32), axis=0)
+    d_qkv = mixed_grads(flat(tok), flat(d_mixed))
+    input_grad, mixed_sum = input_grads(d_mixed, d_one, w_mixed, rows)
+    sums = jnp.concatenate(
+        [sums[:4], mixed_sum[:, :width], mixed_sum[:, 2 * width :], sums[6:]], axis=0
+    )
     return (
-        result, input_grad, d_qkv, d_out, d_up, d_down, sums, up_sum, mixed_sum,
-        table_grad(bins, heads),
+        result, input_grad, d_qkv, d_branch_up, d_down, sums, up_sum, bins,
     )
 
 
@@ -477,43 +793,42 @@
     norm_gains, norm_shifts, proj_biases, up_bias, rel_tables, cotangent,
 ):
     axes = ("dp", "fsdp")
-    width = layer_input.shape[3]
-    hidden = w_up.shape[1]
+    width, hidden = layer_input.shape[3], w_up.shape[1]
+    own = norm_gains.shape[1]
     table = lax.all_gather(rel_tables, "fsdp", axis=0, tiled=True)
-    own = norm_gains.shape[1]
+    heads = table.shape[1]
     small = jnp.concatenate(
-        [
-            jnp.concatenate([norm_gains, norm_shifts, proj_biases], axis=0).reshape(-1),
-            up_bias,
-        ]
-    )
-    every = lax.all_gather(small, axes, axis=0)
-    devices = every.shape[0]
-    vectors = every[:, : 8 * own].reshape(devices, 8, own)
-    vectors = jnp.transpose(vectors, (1, 0, 2)).reshape(8, width).astype(F32)
-    up_row = every[:, 8 * own :].reshape(1, hidden).astype(F32)
-    weights = tuple(
-        lax.all_gather(item, axes, axis=0, tiled=True) for item in (w_qkv, w_out, w_up, w_down)
-    )
-    (
-        result, input_grad, d_qkv, d_out, d_up, d_down, sums, up_sum, mixed_sum, d_table,
-    ) = local_step(
-        text_lengths[:, 0], pos_buckets, box_buckets, layer_input, cotangent, weights, vectors,
-        up_row, table,
-    )
-    shards = [
-        lax.psum_scatter(item.astype(BF16), axes, scatter_dimension=0, tiled=True).astype(F32)
-        for item in (d_qkv, d_out, d_up, d_down)
-    ]
-    sums = sums.at[4].set(mixed_sum[:width]).at[5].set(mixed_sum[2 * width :])
-    sums, up_sum, d_table = lax.psum((sums, up_sum, d_table), axes)
+        [norm_gains.T, norm_shifts.T, proj_biases.T, up_bias.reshape(own, hidden // width)], axis=1
+    )
+    small = jnp.pad(small, ((0, 0), (0, LANES - small.shape[1])))
+    w_mixed = lax.all_gather(
+        jnp.concatenate([w_qkv, w_out, w_up, small], axis=1), axes, axis=0, tiled=True
+    )
+    w_down = lax.all_gather(w_down, axes, axis=0, tiled=True)
+    small = w_mixed[:, 4 * width + hidden :].astype(F32)
+    vectors = small[:, :8].T
+    up_row = small[:, 8 : 8 + hidden // width].reshape(1, hidden)
+    result, input_grad, d_qkv, d_branch_up, d_down, sums, up_sum, bins = local_step(
+        text_lengths[:, 0], pos_buckets, box_buckets, layer_input, cotangent, w_mixed, w_down,
+        vectors, up_row, table,
+    )
+    d_down = lax.psum_scatter(d_down, axes, scatter_dimension=0, tiled=True).astype(F32)
+    d_branch_up = lax.psum_scatter(d_branch_up, axes, scatter_dimension=0, tiled=True).astype(F32)
+    packed = jnp.concatenate(
+        [sums.reshape(-1, LANES), up_sum.reshape(-1, LANES), bins], axis=0
+    )
+    d_qkv, packed = reduce_tail(d_qkv, packed, lax.axis_size("dp"), lax.axis_size("fsdp"))
+    lines = 8 * width // LANES
     place = lax.axis_index(axes)
-    sums = lax.dynamic_slice_in_dim(sums, place * own, own, 1)
-    up_sum = lax.dynamic_slice_in_dim(up_sum[0], place * up_bias.shape[0], up_bias.shape[0], 0)
+    sums = lax.dynamic_slice_in_dim(packed[:lines].reshape(8, width), place * own, own, 1)
+    up_sum = packed[lines : lines + hidden // LANES].reshape(hidden)
+    up_sum = lax.dynamic_slice_in_dim(up_sum, place * up_bias.shape[0], up_bias.shape[0], 0)
+    d_table = table_grad(packed[lines + hidden // LANES :], heads)
     table_rows = rel_tables.shape[0]
     d_table = lax.dynamic_slice_in_dim(d_table, lax.axis_index("fsdp") * table_rows, table_rows, 0)
     return (
-        result, input_grad, *shards, sums[0:2], sums[2:4], sums[4:8], up_sum, d_table,
+        result, input_grad, d_qkv, d_branch_up[:, :width], d_branch_up[:, width:], d_down,
+        sums[0:2], sums[2:4], sums[4:8], up_sum, d_table,
     )
 
 

time: 829 us -> 495 us (0.60)
  waiting for transfers between devices: 276 us -> 5.48 us
  Pallas kernels: 329 us -> 416 us
  blocking collectives: 90.2 us -> 6.2 us
  matrix products: 49.5 us -> 0 us
  other arithmetic: 17.3 us -> 6.59 us
    reduce_scatter x4 -> x2, waiting for transfers between devices: 214 us -> 0.01 us  [the longest x1 0.01 us: body(): lax.psum_scatter(d_down, axes, scatter_dimension=0, tiled=True).astype(F32)]
    pallas_call x1 -> x6, Pallas kernels: 9.74 us -> 101 us  [the longest x1 42.9 us: reduce_tail(): pl.pallas_call(partial(reduce_kernel, dims), out_shape=(jax.ShapeDtypeStr...]
    all_gather x4 -> x2, waiting for transfers between devices: 59.4 us -> 4.73 us  [the longest x1 4.73 us: body(): w_down = lax.all_gather(w_down, axes, axis=0, tiled=True)]
    dot_general x5 -> x0, matrix products: 49.5 us -> none  [the longest x4 41.5 us: across(): lax.dot_general(left, right, (((0,), (0,)), ((), ())), preferred_element_...]
    unnamed x1 -> x0, blocking collectives: 42.4 us -> none
    psum x1 -> x0, blocking collectives: 42.2 us -> none  [body(): sums, up_sum, d_table = lax.psum((sums, up_sum, d_table), axes)]
    unnamed x41 -> x32, local copies, waits for them, and re-layouts: 33.3 us -> 31 us
  transfers between devices with their start and end apart: 8 -> 4, of which waited for: 3 -> 1; matrix products, arithmetic and copies ran while one was open for 12% -> 8% of each run, Pallas kernels for 34% -> 72%
where the time goes in v2:
time: 495 us; the launch traced here: 489 us
  Pallas kernels  416 us (84%)
  local copies, waits for them, and re-layouts  40.1 us (8%)
  between operations  14.1 us (3%)
  other arithmetic  6.59 us (1%)
  blocking collectives  6.2 us (1%)
  waiting for transfers between devices  5.48 us (1%)
    pallas_call x1, Pallas kernels, attend_back(): pl.pallas_call(partial(attend_back_kernel, rows), out_shape=(jax.ShapeDty...  152 us
    pallas_call x1, Pallas kernels, bias_rows(): pl.pallas_call(partial(bias_kernel, rows), out_shape=jax.ShapeDtypeStruct...  69.4 us
    pallas_call x1, Pallas kernels, dense(): pl.pallas_call(partial(dense_kernel, rows), out_shape=(jax.ShapeDtypeStru...  52 us
    pallas_call x1, Pallas kernels, reduce_tail(): pl.pallas_call(partial(reduce_kernel, dims), out_shape=(jax.ShapeDtypeStr...  42.9 us
    pallas_call x1, Pallas kernels, attend(): pl.pallas_call(attend_kernel, out_shape=(jax.ShapeDtypeStruct((docs, head...  40.7 us
    unnamed x32, local copies, waits for them, and re-layouts  31 us
    pallas_call x1, Pallas kernels, branch_up_grads(): pl.pallas_call(kernel, out_shape=jax.ShapeDtypeStruct((width, parts * wid...  15.3 us
    pallas_call x1, Pallas kernels, down_grads(): pl.pallas_call(kernel, out_shape=jax.ShapeDtypeStruct((parts * width, wid...  11.7 us
  transfers between devices with their start and end apart: 4, of which 1 were waited for; matrix products, arithmetic and copies ran while one was open for 8% of the time, Pallas kernels for 72%

profile of v2, /device:TPU:0, one launch (start us, length us, event | category | flops | bytes accessed | tf_op | source)
XLA Modules:
  0.0 488.5 jit_solution(13297289016065138416)
XLA Ops:
  10.3 1.7 pad_maximum_fusion
  12.9 3.3 copy.63.x_ref
  16.2 6.2 %all-gather = bf16[4,40,12]{1,2,0:T(8,128)(2,1)S(1)} all-gather(bf16[1,40,12]{1,2,0:T(8,128)(2,1)S(1)} %bitcast.34), channel_id=1, replica_groups=mesh['dp'=8,'fsdp'=4] {'fsdp'}, dimensions={0}, use_global_device_ids=true | all-gather | bytes 4800 | tf_op jit(solution)/shard_map/all_gather | solution.py:798
  22.5 8.1 %copy.62.box_ref = s32[2,1,2,709,709]{4,3,2,1,0:T(8,128)} copy(s32[2,1,2,709,709]{4,2,3,1,0:T(2,128)} %param.17) | data formatting | bytes 16085792 | tf_op args[3]
  30.6 2.3 copy.61.pos_ref
  33.1 1.7 copy.64.cot_ref
  35.4 69.4 %bias_rows.1.bias_ref = f32[2,12,768,768]{3,2,1,0:T(8,128)} custom-call(s32[2]{0:T(128)} %bitcast.35, f32[24,128]{1,0:T(8,128)} %pad_maximum_fusion.3.tab_ref, s32[2,1,709,709]{3,2,1,0:T(8,128)} %copy.61.pos_ref, s32[2,1,2,709,709]{4,3,2,1,0:T(8,128)} %copy.62.box_ref), custom_call_target="tpu_custom_call" | custom-call | flops 36193032 | bytes 70778880 | tf_op jit(solution)/shard_map/bias_rows/pallas_call | solution.py:95
  104.9 1.0 slice_convert_fusion
  106.8 0.9 reshape.68.upb_ref
  107.6 9.9 %project.1 = (bf16[2,768,2304]{2,1,0:T(8,128)(2,1)}, bf16[2,768,768]{2,1,0:T(8,128)(2,1)}) custom-call(bf16[2,1,709,768]{3,2,1,0:T(8,128)(2,1)} %copy.63.x_ref, bf16[768,6272]{1,0:T(8,128)(2,1)} %all-gather.4.cloned.1.call-done.w_ref.wo_ref.wu_ref, f32[8,768]{1,0:T(8,128)} %copy.59.vec_ref), custom_call_target="tpu_custom_call" | custom-call | tf_op jit(solution)/shard_map/project/pallas_call | solution.py:130
  117.6 40.7 %attend.1 = (bf16[2,12,768,768]{3,2,1,0:T(8,128)(2,1)}, bf16[2,768,768]{2,1,0:T(8,128)(2,1)}) custom-call(bf16[2,768,2304]{2,1,0:T(8,128)(2,1)} %get-tuple-element.31.q_ref.k_ref.v_ref, bf16[2,768,2304]{2,1,0:T(8,128)(2,1)} %get-tuple-element.31.q_ref.k_ref.v_ref, bf16[2,768,2304]{2,1,0:T(8,128)(2,1)} %get-tuple-element.31.q_ref.k_ref.v_ref, ...), custom_call_target="tpu_custom_call" | custom-call | tf_op jit(solution)/shard_map/attend/pallas_call | solution.py:174
  158.3 4.7 all-gather.6.cloned.1.call-done.wd_ref
  163.0 52.0 %dense.1 = (bf16[2,1,709,768]{3,2,1,0:T(8,128)(2,1)}, f32[2,768,768]{2,1,0:T(8,128)}, bf16[2,768,768]{2,1,0:T(8,128)(2,1)}, bf16[2,768,3072]{2,1,0:T(8,128)(2,1)...) custom-call(bf16[2,1,709,768]{3,2,1,0:T(8,128)(2,1)} %copy.63.x_ref,, ...), custom_call_target="tpu_custom_call" | custom-call | tf_op jit(solution)/shard_map/dense/pallas_call | solution.py:275
  215.0 11.7 %down_grads.1 = bf16[3072,768]{1,0:T(8,128)(2,1)} custom-call(bf16[1536,3072]{1,0:T(8,128)(2,1)} %bitcast.37, bf16[1536,768]{1,0:T(8,128)(2,1)} %bitcast.41), custom_call_target="tpu_custom_call" | custom-call | flops 7247757312 | bytes 14155776 | tf_op jit(solution)/shard_map/down_grads/pallas_call | solution.py:499
  226.8 15.3 %branch_up_grads.1 = bf16[768,3840]{1,0:T(8,128)(2,1)} custom-call(bf16[1536,768]{1,0:T(8,128)(2,1)} %bitcast.28, bf16[1536,768]{1,0:T(8,128)(2,1)} %bitcast.40, bf16[1536,768]{1,0:T(8,128)(2,1)} %bitcast.39, bf16[1536,3072]{1,0:T(8,128)(2,1)} %bitcast.36), custom_call_target="tpu_custom_call" | custom-call | flops 9059696640 | bytes 18874368 | tf_op jit(solution)/shard_map/branch_up_grads/pallas_call | solution.py:471
  242.8 152.4 %attend_back.1 = (bf16[2,768,2304]{2,1,0:T(8,128)(2,1)}, f32[64,128]{1,0:T(8,128)}) custom-call(bf16[2,768,2304]{2,1,0:T(8,128)(2,1)} %get-tuple-element.31.q_ref.k_ref.v_ref, bf16[2,768,2304]{2,1,0:T(8,128)(2,1)} %get-tuple-element.31.q_ref.k_ref.v_ref, bf16[2,768,2304]{2,1,0:T(8,128)(2,1)} %get-tuple-element.31.q_ref.k_ref.v_ref, ...), custom_call_target="tpu_custom_call" | custom-call | tf_op jit(solution)/shard_map/attend_back/pallas_call | solution.py:408
  395.2 11.1 %input_grads.1 = (f32[2,1,709,768]{3,2,1,0:T(8,128)}, f32[1,2304]{1,0:T(1,128)}) custom-call(bf16[2,768,2304]{2,1,0:T(8,128)(2,1)} %get-tuple-element.36.m_ref, f32[2,768,768]{2,1,0:T(8,128)} %get-tuple-element.37.d_ref, bf16[768,6272]{1,0:T(8,128)(2,1)} %all-gather.4.cloned.1.call-done.w_ref.wo_ref.wu_ref), custom_call_target="tpu_custom_call" | custom-call | tf_op jit(solution)/shard_map/input_grads/pallas_call | solution.py:553
  407.8 10.4 %mixed_grads.1 = bf16[768,2304]{1,0:T(8,128)(2,1)} custom-call(bf16[1536,768]{1,0:T(8,128)(2,1)} %bitcast.38, bf16[1536,2304]{1,0:T(8,128)(2,1)} %bitcast.24), custom_call_target="tpu_custom_call" | custom-call | flops 5435817984 | bytes 11796480 | tf_op jit(solution)/shard_map/mixed_grads/pallas_call | solution.py:525
  418.1 42.9 %reduce_tail.1 = (f32[24,2304]{1,0:T(8,128)}, f32[136,128]{1,0:T(8,128)}) custom-call(bf16[4,2,2,2,24,2304]{5,4,3,2,1,0:T(8,128)(2,1)} %bitcast.27, f32[136,128]{1,0:T(8,128)} %pad_maximum_fusion.1.small_ref), custom_call_target="tpu_custom_call" | custom-call | tf_op jit(solution)/shard_map/reduce_tail/pallas_call | solution.py:734
  462.4 8.8 %copy.69 = f32[2,1,709,768]{3,1,2,0:T(1,128)} copy(f32[2,1,709,768]{3,2,1,0:T(8,128)} %get-tuple-element.74) | data formatting | bytes 8712192
  471.3 3.0 copy.68
  476.4 1.6 convert_element_type.19
  478.0 1.6 slice.110
  479.6 1.4 slice.109
  (65 shorter events, 12.2 us)
Async XLA Ops:
  7.2 9.0 %copy-start.7 = (bf16[40,12]{0,1:T(8,128)(2,1)S(1)}, bf16[40,12]{0,1:T(8,128)(2,1)}, u32[]{:S(2)}) copy-start(bf16[40,12]{0,1:T(8,128)(2,1)} %param.26) | copy-start | bytes 2884
  7.2 97.7 %all-gather.4.cloned.1.call-start = ((), (), s32[]{:S(2)}) async-start(), calls=%async_computation.2 | async-start | bytes 9934848 | tf_op jit(solution)/shard_map/all_gather | solution.py:804
  12.1 150.9 %all-gather.6.cloned.1.call-start = ((), (), s32[]{:S(2)}) async-start(), calls=%async_computation.3 | async-start | bytes 4866048 | tf_op jit(solution)/shard_map/all_gather | solution.py:807
  12.9 463.5 %reduce-scatter.5.cloned.1.call-start = ((), (), s32[]{:S(2)}) async-start(), calls=%async_computation.5 | async-start | bytes 4866048 | tf_op jit(solution)/shard_map/reduce_scatter | solution.py:815
  12.9 17.7 %slice-start = ((s8[4356096]{0:T(1024)(128)(4,1)}), s8[161792]{0:T(1024)(128)(4,1)S(1)}, s32[]{:S(2)}) async-start(s8[4356096]{0:T(1024)(128)(4,1)} %bitcast.25), calls=%async_computation.6 | async-start | bytes 323584
  22.5 8.1 %slice-start.1 = ((s8[4356096]{0:T(1024)(128)(4,1)}), s8[4194304]{0:T(1024)(128)(4,1)S(1)}, s32[]{:S(2)}) async-start(s8[4356096]{0:T(1024)(128)(4,1)} %bitcast.25), calls=%async_computation.7 | async-start | bytes 8388608
  30.6 2.5 copy-start.1
  30.6 4.1 copy-start.8
  226.7 251.3 %reduce-scatter.3.cloned.1.call-start = ((), (), s32[]{:S(2)}) async-start(), calls=%async_computation.4 | async-start | bytes 6082560 | tf_op jit(solution)/shard_map/reduce_scatter | solution.py:816
  242.0 0.7 copy-start.5
  395.2 11.9 %copy-start.4 = (f32[64,128]{1,0:T(8,128)S(1)}, f32[64,128]{1,0:T(8,128)}, u32[]{:S(2)}) copy-start(f32[64,128]{1,0:T(8,128)} %get-tuple-element.43) | copy-start | bytes 98308
  395.2 11.9 %copy-start.6 = (f32[1,3072]{1,0:T(1,128)S(1)}, f32[1,3072]{1,0:T(1,128)}, u32[]{:S(2)}) copy-start(f32[1,3072]{1,0:T(1,128)} %get-tuple-element.42) | copy-start | bytes 36868
  461.8 9.5 %copy-start = (bf16[2,1,709,768]{3,2,1,0:T(8,128)(2,1)S(1)}, bf16[2,1,709,768]{3,2,1,0:T(8,128)(2,1)}, u32[]{:S(2)}) copy-start(bf16[2,1,709,768]{3,2,1,0:T(8,128)(2,1)} %get-tuple-element.73) | copy-start | bytes 6534148
  462.4 11.8 %copy-start.3 = (f32[136,128]{1,0:T(8,128)S(1)}, f32[136,128]{1,0:T(8,128)}, u32[]{:S(2)}) copy-start(f32[136,128]{1,0:T(8,128)} %get-tuple-element.50) | copy-start | bytes 208900
  471.3 9.8 %copy-start.2 = (f32[24,2304]{1,0:T(8,128)S(1)}, f32[24,2304]{1,0:T(8,128)}, u32[]{:S(2)}) copy-start(f32[24,2304]{1,0:T(8,128)} %get-tuple-element.109) | copy-start | bytes 663556
Sparse Core Ops, SparseCore 0:
  12.2 85.5 all-gather.3
  100.7 62.2 all-gather.5
  226.8 105.7 reduce-scatter.4
  339.1 114.9 reduce-scatter.2

commit v3 on v2

--- a/solution.py
+++ b/solution.py
@@ -17,6 +17,8 @@
 DENSE_BLOCK = 384
 LANES = 128
 HALF = 32
+SPLIT = 1
+LINES = 1
 SCALE = 0.125
 F32 = jnp.float32
 BF16 = jnp.bfloat16
@@ -306,7 +308,7 @@
 
 def attend_back_kernel(
     rows, q_ref, k_ref, v_ref, probs_ref, do_ref, pos_ref, box_ref, dm_ref, bins_ref,
-    dk_ref, dv_ref, ds_ref,
+    dk_ref, dv_ref, ds_ref, acc_ref, picks_ref,
 ):
     block, width = pl.program_id(1), q_ref.shape[2]
     padded = k_ref.shape[1]
@@ -314,7 +316,7 @@
 
     @pl.when((pl.program_id(0) == 0) & (block == 0))
     def _():
-        bins_ref[...] = jnp.zeros_like(bins_ref)
+        acc_ref[...] = jnp.zeros_like(acc_ref)
         ds_ref[...] = jnp.zeros_like(ds_ref)
 
     @pl.when(block == 0)
@@ -350,47 +352,64 @@
             dv_ref[lines, :] += dot(turned_g[part, :], low)
         dm_ref[0, own, cols] = (total * SCALE).astype(BF16)
 
-    group = 16
-    low_bins = lax.broadcasted_iota(jnp.int32, (HALF, padded), 0).astype(BF16)
+    group = 32
+    low_bins = lax.broadcasted_iota(jnp.int32, (HALF, LANES), 0).astype(BF16)
 
     def hits(picks, bins):
-        return jnp.where(low_bins[:bins] == picks.astype(BF16), BF16(1), BF16(0))
+        low = picks.astype(BF16)
+        return jnp.concatenate(
+            [
+                jnp.where(low_bins[first : first + 16] == low, BF16(1), BF16(0))
+                for first in range(0, bins, 16)
+            ],
+            axis=0,
+        )
+
+    for place, (picks, bits) in enumerate(
+        (
+            (box_ref[0, 0, 0], BOX_BINS),
+            (box_ref[0, 0, 1], BOX_BINS),
+            (pos_ref[0, 0], POS_BINS),
+        )
+    ):
+        half = bits // 2
+        for chunk in range(padded // LANES):
+            part = picks[:, chunk * LANES : (chunk + 1) * LANES] & (bits - 1)
+            picks_ref[2 * place, chunk] = (part & (half - 1)).astype(F32)
+            picks_ref[2 * place + 1, chunk] = (part >> (half.bit_length() - 1)).astype(F32)
 
     def count(step, carry):
-        left, right = [], []
-        for line in range(group):
-            row = step * group + line
-            at = pl.ds(row, 1)
-            pick_x = box_ref[0, 0, 0, at, :] & (BOX_BINS - 1)
-            pick_y = box_ref[0, 0, 1, at, :] & (BOX_BINS - 1)
-            pick_p = pos_ref[0, 0, at, :] & (POS_BINS - 1)
-            here = pl.ds(pl.multiple_of(row * 16, 16), 16)
-            base = jnp.concatenate(
-                [ds_ref[chunk, here, :] for chunk in range(padded // LANES)], axis=1
-            )
-            left.append(
-                jnp.concatenate(
-                    [
-                        base.astype(BF16),
-                        (base * (pick_x >> 5).astype(F32)).astype(BF16),
-                        (base * (pick_y >> 5).astype(F32)).astype(BF16),
-                        (base * (pick_p >> 4).astype(F32)).astype(BF16),
-                    ],
-                    axis=0,
-                )
-            )
-            right.append(
-                jnp.concatenate(
-                    [
-                        hits(pick_x & (HALF - 1), HALF),
-                        hits(pick_y & (HALF - 1), HALF),
-                        hits(pick_p & (HALF // 2 - 1), HALF // 2),
-                    ],
-                    axis=0,
-                )
-            )
-        sums = dot_nt(jnp.concatenate(left, axis=1), jnp.concatenate(right, axis=1))
-        bins_ref[:, : sums.shape[1]] += sums
+        total = None
+        for line in range(0, group, LINES):
+            left, right = [], []
+            for own in range(LINES):
+                row = step * group + line + own
+                here = pl.ds(pl.multiple_of(row * 16, 16), 16)
+                again = pl.ds(row, 16, stride=0)
+                for chunk in range(padded // LANES):
+                    base = ds_ref[chunk, here, :]
+                    left.append(
+                        jnp.concatenate(
+                            [base.astype(BF16)]
+                            + [
+                                (base * picks_ref[2 * place + 1, chunk, again, :]).astype(BF16)
+                                for place in range(3)
+                            ],
+                            axis=0,
+                        )
+                    )
+                    right.append(
+                        jnp.concatenate(
+                            [
+                                hits(picks_ref[2 * place, chunk, again, :], bins)
+                                for place, bins in enumerate((HALF, HALF, HALF // 2))
+                            ],
+                            axis=0,
+                        )
+                    )
+            part = dot_nt(jnp.concatenate(left, axis=1), jnp.concatenate(right, axis=1))
+            total = part if total is None else total + part
+        acc_ref[0, :, : total.shape[1]] += total
         return carry
 
     live = jnp.minimum(BLOCK, (rows + group - 1) // group * group - block * BLOCK)
@@ -400,6 +419,7 @@
     def _():
         dm_ref[0, :, width : 2 * width] = dk_ref[...].astype(BF16).T
         dm_ref[0, :, 2 * width :] = dv_ref[...].astype(BF16).T
+        bins_ref[...] = jnp.sum(acc_ref[...], axis=0)
 
 
 def attend_back(qkv, probs, d_attended, pos_buckets, box_buckets):
@@ -429,6 +449,8 @@
             pltpu.VMEM((width, padded), F32),
             pltpu.VMEM((width, padded), F32),
             pltpu.VMEM((padded // LANES, BLOCK * 16, LANES), F32),
+            pltpu.VMEM((SPLIT, 64, LANES), F32),
+            pltpu.VMEM((6, padded // LANES, BLOCK, LANES), F32),
         ],
         compiler_params=params(2),
         name="attend_back",
@@ -511,95 +533,62 @@
     )(active, d_ffn)
 
 
-def mixed_grads(tok, d_mixed):
-    rows, width = tok.shape
-    parts = d_mixed.shape[1] // width
-
-    def kernel(t_ref, m_ref, out_ref, turned_ref):
-        @pl.when(pl.program_id(0) == 0)
-        def _():
-            turned_ref[...] = t_ref[...].T
-
-        out_ref[...] = dot(turned_ref[...], m_ref[...]).astype(BF16)
-
-    return pl.pallas_call(
-        kernel,
-        out_shape=jax.ShapeDtypeStruct((width, parts * width), BF16),
-        grid=(parts,),
-        in_specs=[resident((rows, width)), pl.BlockSpec((rows, width), lambda p: (0, p))],
-        out_specs=pl.BlockSpec((width, width), lambda p: (0, p)),
-        scratch_shapes=[pltpu.VMEM((width, rows), BF16)],
-        compiler_params=params(1),
-        cost_estimate=pl.CostEstimate(
-            flops=2 * rows * width * width * parts, transcendentals=0,
-            bytes_accessed=2 * rows * width * (parts + 2),
-        ),
-        name="mixed_grads",
-    )(tok, d_mixed)
-
-
-def input_grads(d_mixed, d_one, w_mixed, rows):
-    docs, padded, width = d_one.shape
-
-    def kernel(m_ref, d_ref, w_ref, out_ref, sum_ref):
-        @pl.when((pl.program_id(0) == 0) & (pl.program_id(1) == 0))
-        def _():
-            sum_ref[...] = jnp.zeros_like(sum_ref)
-
-        block = m_ref[0]
-        out_ref[0, 0] = d_ref[0] + dot_nt(block, w_ref[...])
-        sum_ref[...] += jnp.sum(block.astype(F32), axis=0, keepdims=True)
-
-    return pl.pallas_call(
-        kernel,
-        out_shape=(
-            jax.ShapeDtypeStruct((docs, 1, rows, width), F32),
-            jax.ShapeDtypeStruct((1, 3 * width), F32),
-        ),
-        grid=(docs, padded // DENSE_BLOCK),
-        in_specs=[
-            pl.BlockSpec((1, DENSE_BLOCK, 3 * width), lambda d, i: (d, i, 0)),
-            pl.BlockSpec((1, DENSE_BLOCK, width), lambda d, i: (d, i, 0)),
-            columns((width, 3 * width), 0),
-        ],
-        out_specs=(
-            pl.BlockSpec((1, 1, DENSE_BLOCK, width), lambda d, i: (d, 0, i, 0)),
-            pl.BlockSpec((1, 3 * width), lambda d, i: (0, 0)),
-        ),
-        compiler_params=params(2),
-        name="input_grads",
-    )(d_mixed, d_one, w_mixed)
-
-
-def reduce_kernel(
-    dims, grad_ref, small_ref, out_ref, sums_ref,
-    got_c, one, got_xa, got_yb, two_a, two_b, got_ya, got_xb, three, got_z,
-    sums, got_s, send_sems, recv_sems,
+ORDERS = ((3, 1, 2, 0), (3, 2, 1, 0), (3, 1, 2, 0))
+MESH = pl.DeviceIdType.MESH
+
+
+def remaining(part, level):
+    return [axis for axis in range(4) if axis not in ORDERS[part][:level]]
+
+
+def tail_kernel(
+    dims, w_ref, tok_ref, mixed_ref, one_ref, small_ref, grad_ref, sums_ref, input_ref, *scratch
 ):
+    parts, width = len(ORDERS), tok_ref.shape[1]
+    holders = [scratch[8 * part : 8 * part + 4] for part in range(parts)]
+    inboxes = [scratch[8 * part + 4 : 8 * part + 8] for part in range(parts)]
+    (
+        tok, turned, mixed, weights, kept, stage, own_sums, got_sums,
+        send_sems, recv_sems, load_sems, keep_sems, store_sems,
+    ) = scratch[8 * parts :]
     deep, across, along, cores = dims
     dp, fsdp = lax.axis_index("dp"), lax.axis_index("fsdp")
-    z, x = dp // across, dp % across
-    y, c = fsdp // cores, fsdp % cores
-    width = grad_ref.shape[5]
-    cut = width // LANES // 2 * LANES
-    lower, upper = slice(0, cut), slice(cut, width)
+    mine = (dp // across, dp % across, fsdp // cores, fsdp % cores)
+    docs, padded = one_ref.shape[0], one_ref.shape[1]
+    rows, block = input_ref.shape[1], kept.shape[1]
+    own_lines = small_ref.shape[0]
 
     def peer(axis, step):
-        place = [z, x, y, c]
+        place = list(mine)
         place[axis] = (place[axis] + step) % dims[axis]
         return place[axis], (place[0] * across + place[1], place[2] * cores + place[3])
+
+    loads = [pltpu.make_async_copy(tok_ref, tok, load_sems.at[0])]
+    for part in range(parts):
+        loads.append(
+            pltpu.make_async_copy(
+                mixed_ref.at[:, pl.ds(part * width, width)], mixed.at[part], load_sems.at[1 + part]
+            )
+        )
+    loads.append(
+        pltpu.make_async_copy(
+            w_ref.at[:, pl.ds(0, parts * width)], weights, load_sems.at[1 + parts]
+        )
+    )
+    for load in loads:
+        load.start()
 
     barrier = pltpu.get_barrier_semaphore()
     partners = 0
     for axis in range(4):
         for step in range(1, dims[axis]):
-            pl.semaphore_signal(
-                barrier, inc=1, device_id=peer(axis, step)[1], device_id_type=pl.DeviceIdType.MESH
-            )
+            pl.semaphore_signal(barrier, inc=1, device_id=peer(axis, step)[1], device_id_type=MESH)
             partners += 1
     pl.semaphore_wait(barrier, partners)
 
-    def exchange(stage, axis, source, target):
+    flying = {}
+
+    def launch(lane, axis, source, target):
         copies = []
         for step in range(1, dims[axis]):
             place, device = peer(axis, step)
@@ -607,18 +596,18 @@
                 pltpu.make_async_remote_copy(
                     src_ref=source(place),
                     dst_ref=target(step - 1),
-                    send_sem=send_sems.at[stage, step - 1],
-                    recv_sem=recv_sems.at[stage, step - 1],
+                    send_sem=send_sems.at[lane, step - 1],
+                    recv_sem=recv_sems.at[lane, step - 1],
                     device_id=device,
-                    device_id_type=pl.DeviceIdType.MESH,
+                    device_id_type=MESH,
                 )
             )
         for copy in copies:
             copy.start()
-        return copies
-
-    def finish(copies):
-        for copy in copies:
+        flying[lane] = copies
+
+    def land(lane):
+        for copy in flying.pop(lane):
             copy.wait()
 
     def joined(own, others):
@@ -627,139 +616,224 @@
             total = total + other.astype(F32)
         return total
 
-    def small_step(stage, axis, level):
-        own = small_ref if level == 0 else sums.at[level - 1]
-        first = sum(dims[later] - 1 for later in (3, 1, 2, 0)[:level])
-        return exchange(stage, axis, lambda place: own, lambda slot: got_s.at[first + slot])
-
-    def small_join(axis, level):
-        own = small_ref if level == 0 else sums.at[level - 1]
-        first = sum(dims[later] - 1 for later in (3, 1, 2, 0)[:level])
-        return joined(own[...], [got_s[first + slot] for slot in range(dims[axis] - 1)])
-
-    copies_c = exchange(0, 3, lambda t: grad_ref.at[:, :, :, t], lambda slot: got_c.at[slot])
-    copies_s = small_step(7, 3, 0)
-    finish(copies_s)
-    finish(copies_c)
-    sums[0] = small_join(3, 0)
-    copies_s = small_step(8, 1, 1)
-
-    def add_cores(k, carry):
-        for i in range(across):
-            for j in range(along):
-                one[k, i, j] = joined(
-                    grad_ref[k, i, j, c], [got_c[s, k, i, j] for s in range(cores - 1)]
+    def send(part, level):
+        axis, axes = ORDERS[part][level], remaining(part, level)
+
+        def source(place):
+            return holders[part][level].at[
+                tuple(place if item == axis else slice(None) for item in axes)
+            ]
+
+        launch(4 * part + level, axis, source, lambda slot: inboxes[part][level].at[slot])
+
+    def join(part, level):
+        land(4 * part + level)
+        axis, axes = ORDERS[part][level], remaining(part, level)
+        source, box = holders[part][level], inboxes[part][level]
+        left = [item for item in axes if item != axis]
+        count = dims[axis] - 1
+        if not left:
+            grad_ref[:, part * width : (part + 1) * width] = joined(
+                source[mine[axis]], [box[slot] for slot in range(count)]
+            )
+            return
+        spots = [()]
+        for item in left[1:]:
+            spots = [spot + (place,) for spot in spots for place in range(dims[item])]
+
+        def add(k, carry):
+            for spot in spots:
+                there = (k,) + spot
+                where = dict(zip(left, there))
+                where[axis] = mine[axis]
+                own = tuple(where[item] for item in axes)
+                holders[part][level + 1][there] = joined(
+                    source[own], [box[(slot,) + there] for slot in range(count)]
                 ).astype(BF16)
-        return carry
-
-    lax.fori_loop(0, deep, add_cores, 0)
-    copies_xa = exchange(1, 1, lambda t: one.at[:, t, :, :, lower], lambda slot: got_xa.at[slot])
-    copies_yb = exchange(2, 2, lambda t: one.at[:, :, t, :, upper], lambda slot: got_yb.at[slot])
-    finish(copies_s)
-    sums[1] = small_join(1, 1)
-    copies_s = small_step(9, 2, 2)
-    finish(copies_xa)
-
-    def add_xa(k, carry):
-        for j in range(along):
-            two_a[k, j] = joined(
-                one[k, x, j, :, lower], [got_xa[s, k, j] for s in range(across - 1)]
-            ).astype(BF16)
-        return carry
-
-    lax.fori_loop(0, deep, add_xa, 0)
-    copies_ya = exchange(3, 2, lambda t: two_a.at[:, t], lambda slot: got_ya.at[slot])
-    finish(copies_yb)
-
-    def add_yb(k, carry):
-        for i in range(across):
-            two_b[k, i] = joined(
-                one[k, i, y, :, upper], [got_yb[s, k, i] for s in range(along - 1)]
-            ).astype(BF16)
-        return carry
-
-    lax.fori_loop(0, deep, add_yb, 0)
-    copies_xb = exchange(4, 1, lambda t: two_b.at[:, t], lambda slot: got_xb.at[slot])
-    finish(copies_s)
-    sums[2] = small_join(2, 2)
-    copies_s = small_step(10, 0, 3)
-    finish(copies_ya)
-
-    def add_ya(k, carry):
-        three[k, :, lower] = joined(
-            two_a[k, y], [got_ya[s, k] for s in range(along - 1)]
-        ).astype(BF16)
-        return carry
-
-    lax.fori_loop(0, deep, add_ya, 0)
-    copies_za = exchange(
-        5, 0, lambda t: three.at[t, :, lower], lambda slot: got_z.at[slot, :, lower]
-    )
-    finish(copies_xb)
-
-    def add_xb(k, carry):
-        three[k, :, upper] = joined(
-            two_b[k, x], [got_xb[s, k] for s in range(across - 1)]
-        ).astype(BF16)
-        return carry
-
-    lax.fori_loop(0, deep, add_xb, 0)
-    copies_zb = exchange(
-        6, 0, lambda t: three.at[t, :, upper], lambda slot: got_z.at[slot, :, upper]
-    )
-    finish(copies_s)
-    sums_ref[...] = small_join(0, 3)
-    finish(copies_za)
-    finish(copies_zb)
-    out_ref[...] = joined(three[z], [got_z[s] for s in range(deep - 1)])
-
-
-def reduce_tail(grad, small, dp, fsdp):
+            return carry
+
+        lax.fori_loop(0, dims[left[0]], add, 0)
+        send(part, level + 1)
+
+    small_order = (3, 1, 2, 0)
+
+    def small_send(level):
+        axis = small_order[level]
+        first = sum(dims[item] - 1 for item in small_order[:level])
+        launch(
+            4 * parts + level, axis,
+            lambda place: own_sums.at[level], lambda slot: got_sums.at[first + slot],
+        )
+
+    def small_join(level):
+        land(4 * parts + level)
+        axis = small_order[level]
+        first = sum(dims[item] - 1 for item in small_order[:level])
+        total = joined(
+            own_sums[level], [got_sums[first + slot] for slot in range(dims[axis] - 1)]
+        )
+        if level == 3:
+            sums_ref[...] = total
+        else:
+            own_sums[level + 1] = total
+            small_send(level + 1)
+
+    spans = [(doc, first) for doc in range(docs) for first in range(0, padded, block)]
+
+    def keep(step):
+        doc, first = spans[step]
+        return pltpu.make_async_copy(
+            one_ref.at[doc, pl.ds(first, block), :], kept.at[step % 2], keep_sems.at[step % 2]
+        )
+
+    def store(step):
+        doc, first = spans[step]
+        count = min(block, rows - first)
+        return pltpu.make_async_copy(
+            stage.at[step % 2, pl.ds(0, count)],
+            input_ref.at[doc, pl.ds(first, count)],
+            store_sems.at[step % 2],
+        )
+
+    def input_step(step):
+        doc, first = spans[step]
+        if step == 0:
+            loads[1 + parts].wait()
+            keep(0).start()
+        if step + 1 < len(spans):
+            keep(step + 1).start()
+        keep(step).wait()
+        if step >= 2:
+            store(step - 2).wait()
+        at = pl.ds(doc * padded + first, block)
+        total = kept[step % 2]
+        for part in range(parts):
+            total = total + dot_nt(
+                mixed[part, at, :], weights[:, part * width : (part + 1) * width]
+            )
+        stage[step % 2, :, 0, :] = total
+        store(step).start()
+
+    loads[0].wait()
+    turned[...] = tok[...].T
+    ones = jnp.ones((16, tok.shape[0]), BF16)
+    own_sums[0, 0:own_lines] = small_ref[...]
+
+    def multiply(part):
+        loads[1 + part].wait()
+        rest = holders[part][0].shape
+        block_rows = dot(turned[...], mixed[part]).astype(BF16)
+        holders[part][0][...] = block_rows.reshape(rest)
+        line = dot(ones, mixed[part])[0:8]
+        share = 8 * width // LANES // 8
+        for chunk in range(share):
+            own_sums[0, pl.ds(own_lines + (part * share + chunk) * 8, 8)] = line[
+                :, chunk * LANES : (chunk + 1) * LANES
+            ]
+        send(part, 0)
+
+    multiply(0)
+    multiply(1)
+    multiply(2)
+    small_send(0)
+    join(0, 0)
+    input_step(0)
+    join(1, 0)
+    join(0, 1)
+    small_join(0)
+    join(2, 0)
+    join(1, 1)
+    input_step(1)
+    join(0, 2)
+    small_join(1)
+    join(2, 1)
+    join(1, 2)
+    input_step(2)
+    small_join(2)
+    join(2, 2)
+    input_step(3)
+    join(0, 3)
+    join(1, 3)
+    join(2, 3)
+    small_join(3)
+    for step in range(max(len(spans) - 2, 0), len(spans)):
+        store(step).wait()
+
+
+def split_mesh(dp, fsdp):
     across = 1 << ((dp.bit_length() - 1) // 2)
     across = across if dp % across == 0 else 1
     cores = 2 if fsdp % 2 == 0 else 1
-    dims = (dp // across, across, fsdp // cores, cores)
-    deep, across, along, cores = dims
-    width = grad.shape[1]
-    rows = grad.shape[0] // (dp * fsdp)
-    cut = width // LANES // 2 * LANES
-    rest = width - cut
-    slots = sum(dims) - 4
+    return dp // across, across, fsdp // cores, cores
+
+
+def tail(w_mixed, tok, d_mixed, d_one, small, rows, dims):
+    docs, padded, width = d_one.shape
+    parts = len(ORDERS)
+    devices = dims[0] * dims[1] * dims[2] * dims[3]
+    own = width // devices
+    lines = small.shape[0] + parts * 8 * width // LANES
+    any_space = pl.BlockSpec(memory_space=pl.ANY)
     vmem = pl.BlockSpec(memory_space=pltpu.VMEM)
+    scratch = []
+    for part in range(parts):
+        boxes = []
+        for level in range(4):
+            axes = remaining(part, level)
+            axis = ORDERS[part][level]
+            scratch.append(pltpu.VMEM(tuple(dims[item] for item in axes) + (own, width), BF16))
+            boxes.append(
+                pltpu.VMEM(
+                    (max(dims[axis] - 1, 1),)
+                    + tuple(dims[item] for item in axes if item != axis)
+                    + (own, width),
+                    BF16,
+                )
+            )
+        scratch += boxes
     most = max(max(dims) - 1, 1)
-
-    def held(*shape):
-        return pltpu.VMEM(tuple(max(item, 1) for item in shape), BF16)
-
+    flat = docs * padded
+    scratch += [
+        pltpu.VMEM((flat, width), BF16),
+        pltpu.VMEM((width, flat), BF16),
+        pltpu.VMEM((parts, flat, width), BF16),
+        pltpu.VMEM((width, parts * width), BF16),
+        pltpu.VMEM((2, DENSE_BLOCK, width), F32),
+        pltpu.VMEM((2, DENSE_BLOCK, 1, width), F32),
+        pltpu.VMEM((4, lines, LANES), F32),
+        pltpu.VMEM((sum(dims) - 4, lines, LANES), F32),
+        pltpu.SemaphoreType.DMA((4 * parts + 4, most)),
+        pltpu.SemaphoreType.DMA((4 * parts + 4, most)),
+        pltpu.SemaphoreType.DMA((parts + 2,)),
+        pltpu.SemaphoreType.DMA((2,)),
+        pltpu.SemaphoreType.DMA((2,)),
+    ]
     return pl.pallas_call(
-        partial(reduce_kernel, dims),
+        partial(tail_kernel, dims),
         out_shape=(
-            jax.ShapeDtypeStruct((rows, width), F32),
-            jax.ShapeDtypeStruct(small.shape, F32),
-        ),
-        in_specs=[vmem, vmem],
-        out_specs=(vmem, vmem),
-        scratch_shapes=[
-            held(cores - 1, deep, across, along, rows, width),
-            held(deep, across, along, rows, width),
-            held(across - 1, deep, along, rows, cut),
-            held(along - 1, deep, across, rows, rest),
-            held(deep, along, rows, cut),
-            held(deep, across, rows, rest),
-            held(along - 1, deep, rows, cut),
-            held(across - 1, deep, rows, rest),
-            held(deep, rows, width),
-            held(deep - 1, rows, width),
-            pltpu.VMEM((3,) + small.shape, F32),
-            pltpu.VMEM((slots,) + small.shape, F32),
-            pltpu.SemaphoreType.DMA((11, most)),
-            pltpu.SemaphoreType.DMA((11, most)),
-        ],
+            jax.ShapeDtypeStruct((own, parts * width), F32),
+            jax.ShapeDtypeStruct((lines, LANES), F32),
+            jax.ShapeDtypeStruct((docs, rows, 1, width), F32),
+        ),
+        in_specs=[any_space, any_space, any_space, any_space, vmem],
+        out_specs=(vmem, vmem, any_space),
+        scratch_shapes=scratch,
         compiler_params=pltpu.CompilerParams(
             collective_id=0, has_side_effects=True, vmem_limit_bytes=VMEM_LIMIT
         ),
-        name="reduce_tail",
-    )(grad.reshape(deep, across, along, cores, rows, width), small)
+        name="tail",
+    )(w_mixed, tok, d_mixed, d_one, small)
+
+
+def small_results(packed, width, hidden, heads):
+    lines, more = 8 * width // LANES, hidden // LANES
+    sums = packed[:lines].reshape(8, width)
+    up_sum = packed[lines : lines + more].reshape(hidden)
+    d_table = table_grad(packed[lines + more : lines + more + 64], heads)
+    mixed = packed[lines + more + 64 :].reshape(3, width // LANES, 8, LANES)[:, :, 0]
+    mixed = mixed.reshape(3, width)
+    d_biases = jnp.concatenate([mixed[0:1], mixed[2:3], sums[6:8]], axis=0)
+    return sums[0:2], sums[2:4], d_biases, up_sum, d_table
 
 
 def local_step(lengths, pos_buckets, box_buckets, layer_input, cotangent, w_mixed, w_down, vectors, up_row, table):
@@ -778,14 +852,10 @@
     d_down = down_grads(flat(active), flat(d_ffn))
     d_branch_up = branch_up_grads(flat(attended), flat(d_branch), flat(low), flat(d_upper))
     d_mixed, bins = attend_back(qkv, probs, d_attended, pos_buckets, box_buckets)
-    d_qkv = mixed_grads(flat(tok), flat(d_mixed))
-    input_grad, mixed_sum = input_grads(d_mixed, d_one, w_mixed, rows)
-    sums = jnp.concatenate(
-        [sums[:4], mixed_sum[:, :width], mixed_sum[:, 2 * width :], sums[6:]], axis=0
-    )
-    return (
-        result, input_grad, d_qkv, d_branch_up, d_down, sums, up_sum, bins,
-    )
+    packed = jnp.concatenate(
+        [sums.reshape(-1, LANES), up_sum.reshape(-1, LANES), bins], axis=0
+    )
+    return result, d_branch_up, d_down, (w_mixed, flat(tok), flat(d_mixed), d_one, packed, rows)
 
 
 def body(
@@ -808,27 +878,27 @@
     small = w_mixed[:, 4 * width + hidden :].astype(F32)
     vectors = small[:, :8].T
     up_row = small[:, 8 : 8 + hidden // width].reshape(1, hidden)
-    result, input_grad, d_qkv, d_branch_up, d_down, sums, up_sum, bins = local_step(
+    result, d_branch_up, d_down, rest = local_step(
         text_lengths[:, 0], pos_buckets, box_buckets, layer_input, cotangent, w_mixed, w_down,
         vectors, up_row, table,
     )
     d_down = lax.psum_scatter(d_down, axes, scatter_dimension=0, tiled=True).astype(F32)
     d_branch_up = lax.psum_scatter(d_branch_up, axes, scatter_dimension=0, tiled=True).astype(F32)
-    packed = jnp.concatenate(
-        [sums.reshape(-1, LANES), up_sum.reshape(-1, LANES), bins], axis=0
-    )
-    d_qkv, packed = reduce_tail(d_qkv, packed, lax.axis_size("dp"), lax.axis_size("fsdp"))
-    lines = 8 * width // LANES
+    d_qkv, packed, input_grad = tail(
+        *rest, split_mesh(lax.axis_size("dp"), lax.axis_size("fsdp"))
+    )
+    d_gains, d_shifts, d_biases, up_sum, d_table = small_results(packed, width, hidden, heads)
     place = lax.axis_index(axes)
-    sums = lax.dynamic_slice_in_dim(packed[:lines].reshape(8, width), place * own, own, 1)
-    up_sum = packed[lines : lines + hidden // LANES].reshape(hidden)
+    d_gains, d_shifts, d_biases = (
+        lax.dynamic_slice_in_dim(item, place * own, own, 1)
+        for item in (d_gains, d_shifts, d_biases)
+    )
     up_sum = lax.dynamic_slice_in_dim(up_sum, place * up_bias.shape[0], up_bias.shape[0], 0)
-    d_table = table_grad(packed[lines + hidden // LANES :], heads)
     table_rows = rel_tables.shape[0]
     d_table = lax.dynamic_slice_in_dim(d_table, lax.axis_index("fsdp") * table_rows, table_rows, 0)
     return (
-        result, input_grad, d_qkv, d_branch_up[:, :width], d_branch_up[:, width:], d_down,
-        sums[0:2], sums[2:4], sums[4:8], up_sum, d_table,
+        result, jnp.transpose(input_grad, (0, 2, 1, 3)), d_qkv, d_branch_up[:, :width], d_branch_up[:, width:], d_down,
+        d_gains, d_shifts, d_biases, up_sum, d_table,
     )
 
 

time: 495 us -> 492 us (level)
  Pallas kernels: 416 us -> 406 us
    pallas_call x1, Pallas kernels: 152 us -> 134 us  [attend_back(): pl.pallas_call(partial(attend_back_kernel, rows), out_shape=(jax.ShapeDty...]
    pallas_call x3 -> x1, Pallas kernels: 64.4 us -> 72.7 us  [tail(): pl.pallas_call(partial(tail_kernel, dims), out_shape=(jax.ShapeDtypeStruc...]
    unnamed x32 -> x28, local copies, waits for them, and re-layouts: 31 us -> 29.5 us
  transfers between devices with their start and end apart: 4 -> 4, of which waited for: 1 -> 2; matrix products, arithmetic and copies ran while one was open for 8% -> 7% of each run, Pallas kernels for 72% -> 71%
where the time goes in v3:
time: 492 us; the launch traced here: 484 us
  Pallas kernels  406 us (83%)
  local copies, waits for them, and re-layouts  38.9 us (8%)
  between operations  14.3 us (3%)
  waiting for transfers between devices  9.59 us (2%)
  other arithmetic  9.47 us (2%)
  blocking collectives  6.2 us (1%)
    pallas_call x1, Pallas kernels, attend_back(): pl.pallas_call(partial(attend_back_kernel, rows), out_shape=(jax.ShapeDty...  134 us
    pallas_call x1, Pallas kernels, tail(): pl.pallas_call(partial(tail_kernel, dims), out_shape=(jax.ShapeDtypeStruc...  72.7 us
    pallas_call x1, Pallas kernels, bias_rows(): pl.pallas_call(partial(bias_kernel, rows), out_shape=jax.ShapeDtypeStruct...  69.5 us
    pallas_call x1, Pallas kernels, dense(): pl.pallas_call(partial(dense_kernel, rows), out_shape=(jax.ShapeDtypeStru...  52.2 us
    pallas_call x1, Pallas kernels, attend(): pl.pallas_call(attend_kernel, out_shape=(jax.ShapeDtypeStruct((docs, head...  40.8 us
    unnamed x28, local copies, waits for them, and re-layouts  29.5 us
    pallas_call x1, Pallas kernels, branch_up_grads(): pl.pallas_call(kernel, out_shape=jax.ShapeDtypeStruct((width, parts * wid...  15.5 us
    pallas_call x1, Pallas kernels, down_grads(): pl.pallas_call(kernel, out_shape=jax.ShapeDtypeStruct((parts * width, wid...  11.7 us
  transfers between devices with their start and end apart: 4, of which 2 were waited for; matrix products, arithmetic and copies ran while one was open for 7% of the time, Pallas kernels for 71%

profile of v3, /device:TPU:0, one launch (start us, length us, event | category | flops | bytes accessed | tf_op | source)
XLA Modules:
  0.0 484.4 jit_solution(8258138533091432495)
XLA Ops:
  10.3 1.7 pad_maximum_fusion
  12.9 3.3 copy.61.x_ref
  16.2 6.2 %all-gather = bf16[4,40,12]{1,2,0:T(8,128)(2,1)S(1)} all-gather(bf16[1,40,12]{1,2,0:T(8,128)(2,1)S(1)} %bitcast.41), channel_id=1, replica_groups=mesh['dp'=8,'fsdp'=4] {'fsdp'}, dimensions={0}, use_global_device_ids=true | all-gather | bytes 4800 | tf_op jit(solution)/shard_map/all_gather | solution.py:868
  22.5 8.1 %copy.60.box_ref = s32[2,1,2,709,709]{4,3,2,1,0:T(8,128)} copy(s32[2,1,2,709,709]{4,2,3,1,0:T(2,128)} %param.17) | data formatting | bytes 16085792 | tf_op args[3]
  30.6 2.3 copy.59.pos_ref
  33.1 1.6 copy.62.cot_ref
  35.4 69.5 %bias_rows.1.bias_ref = f32[2,12,768,768]{3,2,1,0:T(8,128)} custom-call(s32[2]{0:T(128)} %bitcast.42, f32[24,128]{1,0:T(8,128)} %pad_maximum_fusion.2.tab_ref, s32[2,1,709,709]{3,2,1,0:T(8,128)} %copy.59.pos_ref, s32[2,1,2,709,709]{4,3,2,1,0:T(8,128)} %copy.60.box_ref), custom_call_target="tpu_custom_call" | custom-call | flops 36193032 | bytes 70778880 | tf_op jit(solution)/shard_map/bias_rows/pallas_call | solution.py:97
  104.9 1.0 slice_convert_fusion
  107.7 9.9 %project.1 = (bf16[2,768,2304]{2,1,0:T(8,128)(2,1)}, bf16[2,768,768]{2,1,0:T(8,128)(2,1)}) custom-call(bf16[2,1,709,768]{3,2,1,0:T(8,128)(2,1)} %copy.61.x_ref, bf16[768,6272]{1,0:T(8,128)(2,1)} %all-gather.4.cloned.1.call-done.w_ref.wo_ref.wu_ref, f32[8,768]{1,0:T(8,128)} %copy.57.vec_ref), custom_call_target="tpu_custom_call" | custom-call | tf_op jit(solution)/shard_map/project/pallas_call | solution.py:132
  117.6 40.8 %attend.1 = (bf16[2,12,768,768]{3,2,1,0:T(8,128)(2,1)}, bf16[2,768,768]{2,1,0:T(8,128)(2,1)}) custom-call(bf16[2,768,2304]{2,1,0:T(8,128)(2,1)} %get-tuple-element.30.q_ref.k_ref.v_ref, bf16[2,768,2304]{2,1,0:T(8,128)(2,1)} %get-tuple-element.30.q_ref.k_ref.v_ref, bf16[2,768,2304]{2,1,0:T(8,128)(2,1)} %get-tuple-element.30.q_ref.k_ref.v_ref, ...), custom_call_target="tpu_custom_call" | custom-call | tf_op jit(solution)/shard_map/attend/pallas_call | solution.py:176
  158.3 4.7 all-gather.6.cloned.1.call-done.wd_ref
  163.0 52.2 %dense.1 = (bf16[2,1,709,768]{3,2,1,0:T(8,128)(2,1)}, f32[2,768,768]{2,1,0:T(8,128)}, bf16[2,768,768]{2,1,0:T(8,128)(2,1)}, bf16[2,768,3072]{2,1,0:T(8,128)(2,1)...) custom-call(bf16[2,1,709,768]{3,2,1,0:T(8,128)(2,1)} %copy.61.x_ref,, ...), custom_call_target="tpu_custom_call" | custom-call | tf_op jit(solution)/shard_map/dense/pallas_call | solution.py:277
  215.2 11.7 %down_grads.1 = bf16[3072,768]{1,0:T(8,128)(2,1)} custom-call(bf16[1536,3072]{1,0:T(8,128)(2,1)} %bitcast.44, bf16[1536,768]{1,0:T(8,128)(2,1)} %bitcast.47), custom_call_target="tpu_custom_call" | custom-call | flops 7247757312 | bytes 14155776 | tf_op jit(solution)/shard_map/down_grads/pallas_call | solution.py:521
  226.9 15.5 %branch_up_grads.1 = bf16[768,3840]{1,0:T(8,128)(2,1)} custom-call(bf16[1536,768]{1,0:T(8,128)(2,1)} %bitcast.34, bf16[1536,768]{1,0:T(8,128)(2,1)} %bitcast.46, bf16[1536,768]{1,0:T(8,128)(2,1)} %bitcast.45, bf16[1536,3072]{1,0:T(8,128)(2,1)} %bitcast.43), custom_call_target="tpu_custom_call" | custom-call | flops 9059696640 | bytes 18874368 | tf_op jit(solution)/shard_map/branch_up_grads/pallas_call | solution.py:493
  243.2 133.6 %attend_back.1 = (bf16[2,768,2304]{2,1,0:T(8,128)(2,1)}, f32[64,128]{1,0:T(8,128)}) custom-call(bf16[2,768,2304]{2,1,0:T(8,128)(2,1)} %get-tuple-element.30.q_ref.k_ref.v_ref, bf16[2,768,2304]{2,1,0:T(8,128)(2,1)} %get-tuple-element.30.q_ref.k_ref.v_ref, bf16[2,768,2304]{2,1,0:T(8,128)(2,1)} %get-tuple-element.30.q_ref.k_ref.v_ref, ...), custom_call_target="tpu_custom_call" | custom-call | tf_op jit(solution)/shard_map/attend_back/pallas_call | solution.py:428
  376.8 1.4 pad_maximum_fusion.1.small_ref
  378.2 72.7 %tail.1 = (f32[24,2304]{1,0:T(8,128)}, f32[280,128]{1,0:T(8,128)}, f32[2,709,1,768]{3,2,1,0:T(1,128)}) custom-call(bf16[768,6272]{1,0:T(8,128)(2,1)} %all-gather.4.cloned.1.call-done.w_ref.wo_ref.wu_ref, bf16[1536,768]{1,0:T(8,128)(2,1)} %bitcast.33, bf16[1536,2304]{1,0:T(8,128)(2,1)} %bitcast.29, f32[2,768,768]{2,1,0:T(8,128)} %get-tuple-element.37.one_ref, ...), custom_call_target="tpu_custom_call" | custom-call | tf_op jit(solution)/shard_map/tail/pallas_call | solution.py:811
  450.8 0.9 slice.109
  452.5 3.0 copy.66
  460.6 1.6 convert_element_type.19
  462.2 4.2 reduce-scatter.3.cloned.1.call-done
  466.4 1.6 slice.129
  468.0 1.4 slice.128
  469.4 7.3 %copy.69 = f32[2,1,709,768]{3,1,2,0:T(1,128)} copy(f32[2,1,709,768]{3,1,2,0:T(1,128)} %bitcast.30) | data formatting | bytes 8712192
  (58 shorter events, 13.9 us)
Async XLA Ops:
  7.2 9.0 %copy-start.5 = (bf16[40,12]{0,1:T(8,128)(2,1)S(1)}, bf16[40,12]{0,1:T(8,128)(2,1)}, u32[]{:S(2)}) copy-start(bf16[40,12]{0,1:T(8,128)(2,1)} %param.26) | copy-start | bytes 2884
  7.2 97.7 %all-gather.4.cloned.1.call-start = ((), (), s32[]{:S(2)}) async-start(), calls=%async_computation.2 | async-start | bytes 9934848 | tf_op jit(solution)/shard_map/all_gather | solution.py:874
  12.1 150.9 %all-gather.6.cloned.1.call-start = ((), (), s32[]{:S(2)}) async-start(), calls=%async_computation.3 | async-start | bytes 4866048 | tf_op jit(solution)/shard_map/all_gather | solution.py:877
  12.9 447.7 %reduce-scatter.5.cloned.1.call-start = ((), (), s32[]{:S(2)}) async-start(), calls=%async_computation.5 | async-start | bytes 4866048 | tf_op jit(solution)/shard_map/reduce_scatter | solution.py:885
  12.9 17.7 %slice-start = ((s8[4356096]{0:T(1024)(128)(4,1)}), s8[161792]{0:T(1024)(128)(4,1)S(1)}, s32[]{:S(2)}) async-start(s8[4356096]{0:T(1024)(128)(4,1)} %bitcast.31), calls=%async_computation.6 | async-start | bytes 323584
  22.5 8.1 %slice-start.1 = ((s8[4356096]{0:T(1024)(128)(4,1)}), s8[4194304]{0:T(1024)(128)(4,1)S(1)}, s32[]{:S(2)}) async-start(s8[4356096]{0:T(1024)(128)(4,1)} %bitcast.31), calls=%async_computation.7 | async-start | bytes 8388608
  30.6 2.5 copy-start.1
  30.6 4.1 copy-start.6
  226.9 239.5 %reduce-scatter.3.cloned.1.call-start = ((), (), s32[]{:S(2)}) async-start(), calls=%async_computation.4 | async-start | bytes 6082560 | tf_op jit(solution)/shard_map/reduce_scatter | solution.py:886
  242.4 0.7 copy-start.3
  243.2 133.6 %copy-start.4 = (f32[1,3072]{1,0:T(1,128)S(1)}, f32[1,3072]{1,0:T(1,128)}, u32[]{:S(2)}) copy-start(f32[1,3072]{1,0:T(1,128)} %get-tuple-element.39) | copy-start | bytes 36868
  378.2 74.4 %copy-start = (bf16[2,1,709,768]{3,2,1,0:T(8,128)(2,1)S(1)}, bf16[2,1,709,768]{3,2,1,0:T(8,128)(2,1)}, u32[]{:S(2)}) copy-start(bf16[2,1,709,768]{3,2,1,0:T(8,128)(2,1)} %get-tuple-element.71) | copy-start | bytes 6534148
  469.4 7.3 %copy-start.2 = (f32[24,2304]{1,0:T(8,128)S(1)}, f32[24,2304]{1,0:T(8,128)}, u32[]{:S(2)}) copy-start(f32[24,2304]{1,0:T(8,128)} %get-tuple-element.110) | copy-start | bytes 663556
Sparse Core Ops, SparseCore 0:
  12.2 85.5 all-gather.3
  100.7 62.2 all-gather.5
  227.0 105.7 reduce-scatter.4
  339.3 127.0 reduce-scatter.2

commit v4 on v3

--- a/solution.py
+++ b/solution.py
@@ -474,63 +474,100 @@
     return jnp.concatenate([pieces[2], pieces[0], pieces[1]], axis=1).T * SCALE
 
 
-def branch_up_grads(attended, d_branch, low, d_upper):
+def weight_grads(attended, d_branch, low, d_upper, active, d_ffn, devices):
     rows, width = attended.shape
-    parts = 1 + d_upper.shape[1] // width
-
-    def kernel(a_ref, b_ref, l_ref, u_ref, out_ref, turned_ref):
-        part = pl.program_id(0)
-
-        @pl.when(part == 0)
+    own, fold = width // devices, d_upper.shape[1] // width
+    share = devices // fold
+    steps = 1 + 2 * fold
+
+    def kernel(a_ref, b_ref, l_ref, u_ref, g_ref, f_ref, out_ref, turned_ref, stage_ref, sems):
+        step = pl.program_id(0)
+        slot = step % 2
+
+        def flat_copy(where, spot):
+            cols = pl.ds(pl.multiple_of(where * width, width), width)
+            return pltpu.make_async_copy(
+                stage_ref.at[spot], out_ref.at[:, :, cols], sems.at[spot, 0]
+            )
+
+        def fold_copy(where, spot, part):
+            block = where - 1 - fold
+            cols = pl.ds((1 + fold + part) * width, width)
+            return pltpu.make_async_copy(
+                stage_ref.at[spot].reshape(share, fold, own, width).at[:, part],
+                out_ref.at[pl.ds(block * share, share), :, cols],
+                sems.at[spot, part],
+            )
+
+        def wait_for(where, spot):
+            @pl.when(where <= fold)
+            def _():
+                flat_copy(where, spot).wait()
+
+            @pl.when(where > fold)
+            def _():
+                for part in range(fold):
+                    fold_copy(where, spot, part).wait()
+
+        @pl.when(step >= 2)
         def _():
-            out_ref[...] = dot(a_ref[...].T, b_ref[...]).astype(BF16)
+            wait_for(step - 2, slot)
+
+        def put(value):
+            stage_ref[slot] = value.astype(BF16).reshape(devices, own, width)
+
+        @pl.when(step == 0)
+        def _():
+            put(dot(a_ref[...].T, b_ref[...]))
             turned_ref[...] = l_ref[...].T
 
-        @pl.when(part > 0)
+        @pl.when((step > 0) & (step <= fold))
         def _():
-            out_ref[...] = dot(turned_ref[...], u_ref[...]).astype(BF16)
+            put(dot(turned_ref[...], u_ref[...]))
+
+        @pl.when(step > fold)
+        def _():
+            put(dot(g_ref[...].T, f_ref[...]))
+
+        @pl.when(step <= fold)
+        def _():
+            flat_copy(step, slot).start()
+
+        @pl.when(step > fold)
+        def _():
+            for part in range(fold):
+                fold_copy(step, slot, part).start()
+
+        @pl.when(step == steps - 1)
+        def _():
+            wait_for(step - 1, 1 - slot)
+            wait_for(step, slot)
 
     return pl.pallas_call(
         kernel,
-        out_shape=jax.ShapeDtypeStruct((width, parts * width), BF16),
-        grid=(parts,),
+        out_shape=jax.ShapeDtypeStruct((devices, own, (1 + 2 * fold) * width), BF16),
+        grid=(steps,),
         in_specs=[
             resident((rows, width)),
             resident((rows, width)),
             resident((rows, width)),
-            pl.BlockSpec((rows, width), lambda p: (0, jnp.maximum(p - 1, 0))),
+            pl.BlockSpec((rows, width), lambda p: (0, jnp.clip(p - 1, 0, fold - 1))),
+            pl.BlockSpec((rows, width), lambda p: (0, jnp.clip(p - 1 - fold, 0, fold - 1))),
+            resident((rows, width)),
         ],
-        out_specs=pl.BlockSpec((width, width), lambda p: (0, p)),
-        scratch_shapes=[pltpu.VMEM((width, rows), BF16)],
+        out_specs=pl.BlockSpec(memory_space=pl.ANY),
+        scratch_shapes=[
+            pltpu.VMEM((width, rows), BF16),
+            pltpu.VMEM((2, devices, own, width), BF16),
+            pltpu.SemaphoreType.DMA((2, fold)),
+        ],
         compiler_params=params(1),
         cost_estimate=pl.CostEstimate(
-            flops=2 * rows * width * width * parts, transcendentals=0,
-            bytes_accessed=2 * rows * width * (parts + 3),
-        ),
-        name="branch_up_grads",
-    )(attended, d_branch, low, d_upper)
-
-
-def down_grads(active, d_ffn):
-    rows, width = d_ffn.shape
-    parts = active.shape[1] // width
-
-    def kernel(g_ref, f_ref, out_ref):
-        out_ref[...] = dot(g_ref[...].T, f_ref[...]).astype(BF16)
-
-    return pl.pallas_call(
-        kernel,
-        out_shape=jax.ShapeDtypeStruct((parts * width, width), BF16),
-        grid=(parts,),
-        in_specs=[pl.BlockSpec((rows, width), lambda p: (0, p)), resident((rows, width))],
-        out_specs=pl.BlockSpec((width, width), lambda p: (p, 0)),
-        compiler_params=params(1),
-        cost_estimate=pl.CostEstimate(
-            flops=2 * rows * width * width * parts, transcendentals=0,
-            bytes_accessed=2 * rows * width * (parts + 2),
-        ),
-        name="down_grads",
-    )(active, d_ffn)
+            flops=2 * rows * width * width * steps, transcendentals=0,
+            bytes_accessed=2 * rows * width * (steps + 3),
+        ),
+        name="weight_grads",
+    )(attended, d_branch, low, d_upper, active, d_ffn)
 
 
 ORDERS = ((3, 1, 2, 0), (3, 2, 1, 0), (3, 1, 2, 0))
@@ -836,7 +873,7 @@
     return sums[0:2], sums[2:4], d_biases, up_sum, d_table
 
 
-def local_step(lengths, pos_buckets, box_buckets, layer_input, cotangent, w_mixed, w_down, vectors, up_row, table):
+def local_step(devices, lengths, pos_buckets, box_buckets, layer_input, cotangent, w_mixed, w_down, vectors, up_row, table):
     heads, width = table.shape[1], layer_input.shape[3]
     docs, rows = layer_input.shape[0], layer_input.shape[2]
     bias = bias_rows(lengths, table_entries(table), pos_buckets, box_buckets, heads)
@@ -849,13 +886,14 @@
     def flat(item):
         return item.reshape(-1, item.shape[-1])
 
-    d_down = down_grads(flat(active), flat(d_ffn))
-    d_branch_up = branch_up_grads(flat(attended), flat(d_branch), flat(low), flat(d_upper))
+    d_weights = weight_grads(
+        flat(attended), flat(d_branch), flat(low), flat(d_upper), flat(active), flat(d_ffn), devices
+    )
     d_mixed, bins = attend_back(qkv, probs, d_attended, pos_buckets, box_buckets)
     packed = jnp.concatenate(
         [sums.reshape(-1, LANES), up_sum.reshape(-1, LANES), bins], axis=0
     )
-    return result, d_branch_up, d_down, (w_mixed, flat(tok), flat(d_mixed), d_one, packed, rows)
+    return result, d_weights, (w_mixed, flat(tok), flat(d_mixed), d_one, packed, rows)
 
 
 def body(
@@ -878,12 +916,16 @@
     small = w_mixed[:, 4 * width + hidden :].astype(F32)
     vectors = small[:, :8].T
     up_row = small[:, 8 : 8 + hidden // width].reshape(1, hidden)
-    result, d_branch_up, d_down, rest = local_step(
-        text_lengths[:, 0], pos_buckets, box_buckets, layer_input, cotangent, w_mixed, w_down,
+    devices = width // own
+    result, d_weights, rest = local_step(
+        devices, text_lengths[:, 0], pos_buckets, box_buckets, layer_input, cotangent, w_mixed, w_down,
         vectors, up_row, table,
     )
-    d_down = lax.psum_scatter(d_down, axes, scatter_dimension=0, tiled=True).astype(F32)
-    d_branch_up = lax.psum_scatter(d_branch_up, axes, scatter_dimension=0, tiled=True).astype(F32)
+    d_weights = lax.psum_scatter(
+        d_weights.reshape(width, -1), axes, scatter_dimension=0, tiled=True
+    ).astype(F32)
+    d_down = [d_weights[:, first : first + width] for first in range(width + hidden, width + 2 * hidden, width)]
+    d_down = jnp.concatenate(d_down, axis=0)
     d_qkv, packed, input_grad = tail(
         *rest, split_mesh(lax.axis_size("dp"), lax.axis_size("fsdp"))
     )
@@ -897,7 +939,7 @@
     table_rows = rel_tables.shape[0]
     d_table = lax.dynamic_slice_in_dim(d_table, lax.axis_index("fsdp") * table_rows, table_rows, 0)
     return (
-        result, jnp.transpose(input_grad, (0, 2, 1, 3)), d_qkv, d_branch_up[:, :width], d_branch_up[:, width:], d_down,
+        result, jnp.transpose(input_grad, (0, 2, 1, 3)), d_qkv, d_weights[:, :width], d_weights[:, width : width + hidden], d_down,
         d_gains, d_shifts, d_biases, up_sum, d_table,
     )
 

time: 492 us -> 468 us (0.951)
  Pallas kernels: 406 us -> 387 us
    pallas_call x1, Pallas kernels: 72.7 us -> 55.8 us  [tail(): pl.pallas_call(partial(tail_kernel, dims), out_shape=(jax.ShapeDtypeStruc...]
    pallas_call x2 -> x1, Pallas kernels: 27.2 us -> 25.3 us  [weight_grads(): pl.pallas_call(kernel, out_shape=jax.ShapeDtypeStruct((devices, own, (1 +...]
  transfers between devices with their start and end apart: 4 -> 3, of which waited for: 2 -> 1; matrix products, arithmetic and copies ran while one was open for 7% -> 6% of each run, Pallas kernels for 71% -> 67%
where the time goes in v4:
time: 468 us; the launch traced here: 461 us
  Pallas kernels  387 us (83%)
  local copies, waits for them, and re-layouts  39 us (8%)
  between operations  14.3 us (3%)
  other arithmetic  8.56 us (2%)
  blocking collectives  6.2 us (1%)
  waiting for transfers between devices  5.42 us (1%)
    pallas_call x1, Pallas kernels, attend_back(): pl.pallas_call(partial(attend_back_kernel, rows), out_shape=(jax.ShapeDty...  134 us
    pallas_call x1, Pallas kernels, bias_rows(): pl.pallas_call(partial(bias_kernel, rows), out_shape=jax.ShapeDtypeStruct...  69.5 us
    pallas_call x1, Pallas kernels, tail(): pl.pallas_call(partial(tail_kernel, dims), out_shape=(jax.ShapeDtypeStruc...  55.8 us
    pallas_call x1, Pallas kernels, dense(): pl.pallas_call(partial(dense_kernel, rows), out_shape=(jax.ShapeDtypeStru...  52.2 us
    pallas_call x1, Pallas kernels, attend(): pl.pallas_call(attend_kernel, out_shape=(jax.ShapeDtypeStruct((docs, head...  40.7 us
    unnamed x28, local copies, waits for them, and re-layouts  29.5 us
    pallas_call x1, Pallas kernels, weight_grads(): pl.pallas_call(kernel, out_shape=jax.ShapeDtypeStruct((devices, own, (1 +...  25.3 us
    pallas_call x1, Pallas kernels, project(): pl.pallas_call(partial(project_kernel, rows), out_shape=(jax.ShapeDtypeSt...  9.91 us
  transfers between devices with their start and end apart: 3, of which 1 were waited for; matrix products, arithmetic and copies ran while one was open for 6% of the time, Pallas kernels for 67%

profile of v4, /device:TPU:0, one launch (start us, length us, event | category | flops | bytes accessed | tf_op | source)
XLA Modules:
  0.0 460.7 jit_solution(7381859305840499303)
XLA Ops:
  10.3 1.7 pad_maximum_fusion
  12.9 3.3 copy.61.x_ref
  16.2 6.2 %all-gather = bf16[4,40,12]{1,2,0:T(8,128)(2,1)S(1)} all-gather(bf16[1,40,12]{1,2,0:T(8,128)(2,1)S(1)} %bitcast.43), channel_id=1, replica_groups=mesh['dp'=8,'fsdp'=4] {'fsdp'}, dimensions={0}, use_global_device_ids=true | all-gather | bytes 4800 | tf_op jit(solution)/shard_map/all_gather | solution.py:906
  22.5 8.1 %copy.60.box_ref = s32[2,1,2,709,709]{4,3,2,1,0:T(8,128)} copy(s32[2,1,2,709,709]{4,2,3,1,0:T(2,128)} %param.17) | data formatting | bytes 16085792 | tf_op args[3]
  30.6 2.3 copy.59.pos_ref
  33.1 1.6 copy.62.cot_ref
  35.4 69.5 %bias_rows.1.bias_ref = f32[2,12,768,768]{3,2,1,0:T(8,128)} custom-call(s32[2]{0:T(128)} %bitcast.44, f32[24,128]{1,0:T(8,128)} %pad_maximum_fusion.3.tab_ref, s32[2,1,709,709]{3,2,1,0:T(8,128)} %copy.59.pos_ref, s32[2,1,2,709,709]{4,3,2,1,0:T(8,128)} %copy.60.box_ref), custom_call_target="tpu_custom_call" | custom-call | flops 36193032 | bytes 70778880 | tf_op jit(solution)/shard_map/bias_rows/pallas_call | solution.py:97
  104.9 1.0 slice_convert_fusion
  106.8 0.9 reshape.74.upb_ref
  107.6 9.9 %project.1 = (bf16[2,768,2304]{2,1,0:T(8,128)(2,1)}, bf16[2,768,768]{2,1,0:T(8,128)(2,1)}) custom-call(bf16[2,1,709,768]{3,2,1,0:T(8,128)(2,1)} %copy.61.x_ref, bf16[768,6272]{1,0:T(8,128)(2,1)} %all-gather.4.cloned.1.call-done.w_ref.wo_ref.wu_ref, f32[8,768]{1,0:T(8,128)} %copy.57.vec_ref), custom_call_target="tpu_custom_call" | custom-call | tf_op jit(solution)/shard_map/project/pallas_call | solution.py:132
  117.5 40.7 %attend.1 = (bf16[2,12,768,768]{3,2,1,0:T(8,128)(2,1)}, bf16[2,768,768]{2,1,0:T(8,128)(2,1)}) custom-call(bf16[2,768,2304]{2,1,0:T(8,128)(2,1)} %get-tuple-element.30.q_ref.k_ref.v_ref, bf16[2,768,2304]{2,1,0:T(8,128)(2,1)} %get-tuple-element.30.q_ref.k_ref.v_ref, bf16[2,768,2304]{2,1,0:T(8,128)(2,1)} %get-tuple-element.30.q_ref.k_ref.v_ref, ...), custom_call_target="tpu_custom_call" | custom-call | tf_op jit(solution)/shard_map/attend/pallas_call | solution.py:176
  158.3 4.7 %all-gather.6.cloned.1.call-done.wd_ref = bf16[3072,768]{1,0:T(8,128)(2,1)} async-done(((bf16[96,768]{1,0:T(8,128)(2,1)}), bf16[3072,768]{1,0:T(8,128)(2,1)}) %all-gather.6.cloned.1.call-update) | async-done | bytes 4718608 | tf_op jit(solution)/shard_map/all_gather | solution.py:915
  163.0 52.2 %dense.1 = (bf16[2,1,709,768]{3,2,1,0:T(8,128)(2,1)}, f32[2,768,768]{2,1,0:T(8,128)}, bf16[2,768,768]{2,1,0:T(8,128)(2,1)}, bf16[2,768,3072]{2,1,0:T(8,128)(2,1)...) custom-call(bf16[2,1,709,768]{3,2,1,0:T(8,128)(2,1)} %copy.61.x_ref,, ...), custom_call_target="tpu_custom_call" | custom-call | tf_op jit(solution)/shard_map/dense/pallas_call | solution.py:277
  215.1 25.3 %weight_grads.1 = bf16[32,24,6912]{2,1,0:T(8,128)(2,1)} custom-call(bf16[1536,768]{1,0:T(8,128)(2,1)} %bitcast.36, bf16[1536,768]{1,0:T(8,128)(2,1)} %bitcast.49, bf16[1536,768]{1,0:T(8,128)(2,1)} %bitcast.47, bf16[1536,3072]{1,0:T(8,128)(2,1)} %bitcast.46, bf16[1536,3072]{1,0:T(8,128)(2,1)} %bitcast.45, bf16[1536,768]{1,0:T(8,128)(2,1)} %bitcast.48), custom_call_target="tpu_custom_call" | custom-call | flops 16307453952 | bytes 28311552 | tf_op jit(solution)/shard_map/weight_grads/pallas_call | solution.py:546
  241.2 133.7 %attend_back.1 = (bf16[2,768,2304]{2,1,0:T(8,128)(2,1)}, f32[64,128]{1,0:T(8,128)}) custom-call(bf16[2,768,2304]{2,1,0:T(8,128)(2,1)} %get-tuple-element.30.q_ref.k_ref.v_ref, bf16[2,768,2304]{2,1,0:T(8,128)(2,1)} %get-tuple-element.30.q_ref.k_ref.v_ref, bf16[2,768,2304]{2,1,0:T(8,128)(2,1)} %get-tuple-element.30.q_ref.k_ref.v_ref, ...), custom_call_target="tpu_custom_call" | custom-call | tf_op jit(solution)/shard_map/attend_back/pallas_call | solution.py:428
  374.9 1.4 pad_maximum_fusion.2.small_ref
  376.3 55.8 %tail.1 = (f32[24,2304]{1,0:T(8,128)}, f32[280,128]{1,0:T(8,128)}, f32[2,709,1,768]{3,2,1,0:T(1,128)}) custom-call(bf16[768,6272]{1,0:T(8,128)(2,1)} %all-gather.4.cloned.1.call-done.w_ref.wo_ref.wu_ref, bf16[1536,768]{1,0:T(8,128)(2,1)} %bitcast.35, bf16[1536,2304]{1,0:T(8,128)(2,1)} %bitcast.31, f32[2,768,768]{2,1,0:T(8,128)} %get-tuple-element.37.one_ref, ...), custom_call_target="tpu_custom_call" | custom-call | tf_op jit(solution)/shard_map/tail/pallas_call | solution.py:848
  432.1 0.9 slice.125
  433.8 3.0 copy.66
  438.1 0.8 fusion.12
  438.9 0.8 fusion.11
  441.8 1.5 fusion.10
  444.1 1.6 slice.145
  445.7 7.3 %copy.69 = f32[2,1,709,768]{3,1,2,0:T(1,128)} copy(f32[2,1,709,768]{3,1,2,0:T(1,128)} %bitcast.32) | data formatting | bytes 8712192
  (54 shorter events, 12.2 us)
Async XLA Ops:
  7.2 9.0 %copy-start.5 = (bf16[40,12]{0,1:T(8,128)(2,1)S(1)}, bf16[40,12]{0,1:T(8,128)(2,1)}, u32[]{:S(2)}) copy-start(bf16[40,12]{0,1:T(8,128)(2,1)} %param.26) | copy-start | bytes 2884
  7.2 97.7 %all-gather.4.cloned.1.call-start = ((), (), s32[]{:S(2)}) async-start(), calls=%async_computation.1 | async-start | bytes 9934848 | tf_op jit(solution)/shard_map/all_gather | solution.py:912
  12.1 150.9 %all-gather.6.cloned.1.call-start = ((), (), s32[]{:S(2)}) async-start(), calls=%async_computation.2 | async-start | bytes 4866048 | tf_op jit(solution)/shard_map/all_gather | solution.py:915
  12.9 429.0 %reduce-scatter.2.cloned.1.call-start = ((), (), s32[]{:S(2)}) async-start(), calls=%async_computation.3 | async-start | bytes 10948608 | tf_op jit(solution)/shard_map/reduce_scatter | solution.py:924
  12.9 17.7 %slice-start = ((s8[4356096]{0:T(1024)(128)(4,1)}), s8[161792]{0:T(1024)(128)(4,1)S(1)}, s32[]{:S(2)}) async-start(s8[4356096]{0:T(1024)(128)(4,1)} %bitcast.33), calls=%async_computation.4 | async-start | bytes 323584
  22.5 8.1 %slice-start.1 = ((s8[4356096]{0:T(1024)(128)(4,1)}), s8[4194304]{0:T(1024)(128)(4,1)S(1)}, s32[]{:S(2)}) async-start(s8[4356096]{0:T(1024)(128)(4,1)} %bitcast.33), calls=%async_computation.5 | async-start | bytes 8388608
  30.6 2.5 copy-start.1
  33.1 1.6 copy-start.6
  240.5 0.7 copy-start.3
  241.2 133.7 %copy-start.4 = (f32[1,3072]{1,0:T(1,128)S(1)}, f32[1,3072]{1,0:T(1,128)}, u32[]{:S(2)}) copy-start(f32[1,3072]{1,0:T(1,128)} %get-tuple-element.39) | copy-start | bytes 36868
  376.3 57.5 %copy-start = (bf16[2,1,709,768]{3,2,1,0:T(8,128)(2,1)S(1)}, bf16[2,1,709,768]{3,2,1,0:T(8,128)(2,1)}, u32[]{:S(2)}) copy-start(bf16[2,1,709,768]{3,2,1,0:T(8,128)(2,1)} %get-tuple-element.71) | copy-start | bytes 6534148
  445.7 7.3 %copy-start.2 = (f32[24,2304]{1,0:T(8,128)S(1)}, f32[24,2304]{1,0:T(8,128)}, u32[]{:S(2)}) copy-start(f32[24,2304]{1,0:T(8,128)} %get-tuple-element.115) | copy-start | bytes 663556
Sparse Core Ops, SparseCore 0:
  12.2 85.5 all-gather.3
  100.7 62.2 all-gather.5
  240.6 140.7 reduce-scatter.1

commit v5 on v4

--- a/solution.py
+++ b/solution.py
@@ -118,7 +118,7 @@
 def project_kernel(rows, x_ref, w_ref, vec_ref, out_ref, tok_ref):
     width = x_ref.shape[3]
     block = live_rows(x_ref[0, 0], rows, pl.program_id(1) * x_ref.shape[2])
-    tok_ref[0] = block
+    tok_ref[...] = block.T
     queries = dot(block, w_ref[:, :width]) + vec_ref[4:5, :]
     out_ref[0, :, :width] = queries.astype(BF16) * BF16(SCALE)
     out_ref[0, :, width : 2 * width] = dot(block, w_ref[:, width : 2 * width]).astype(BF16)
@@ -133,7 +133,7 @@
         partial(project_kernel, rows),
         out_shape=(
             jax.ShapeDtypeStruct((docs, padded, 3 * width), BF16),
-            jax.ShapeDtypeStruct((docs, padded, width), BF16),
+            jax.ShapeDtypeStruct((width, docs * padded), BF16),
         ),
         grid=(docs, padded // DENSE_BLOCK),
         in_specs=[
@@ -143,7 +143,7 @@
         ],
         out_specs=(
             pl.BlockSpec((1, DENSE_BLOCK, 3 * width), lambda d, i: (d, i, 0)),
-            pl.BlockSpec((1, DENSE_BLOCK, width), lambda d, i: (d, i, 0)),
+            pl.BlockSpec((width, DENSE_BLOCK), lambda d, i: (0, d * (padded // DENSE_BLOCK) + i)),
         ),
         compiler_params=params(2),
         name="project",
@@ -307,7 +307,7 @@
 
 
 def attend_back_kernel(
-    rows, q_ref, k_ref, v_ref, probs_ref, do_ref, pos_ref, box_ref, dm_ref, bins_ref,
+    rows, q_ref, k_ref, v_ref, probs_ref, do_ref, pos_ref, box_ref, dm_ref, bins_ref, line_ref,
     dk_ref, dv_ref, ds_ref, acc_ref, picks_ref,
 ):
     block, width = pl.program_id(1), q_ref.shape[2]
@@ -317,6 +317,7 @@
     @pl.when((pl.program_id(0) == 0) & (block == 0))
     def _():
         acc_ref[...] = jnp.zeros_like(acc_ref)
+        line_ref[...] = jnp.zeros_like(line_ref)
         ds_ref[...] = jnp.zeros_like(ds_ref)
 
     @pl.when(block == 0)
@@ -420,6 +421,7 @@
         dm_ref[0, :, width : 2 * width] = dk_ref[...].astype(BF16).T
         dm_ref[0, :, 2 * width :] = dv_ref[...].astype(BF16).T
         bins_ref[...] = jnp.sum(acc_ref[...], axis=0)
+        line_ref[...] += dot(jnp.ones((16, padded), BF16), dm_ref[0])[0:8]
 
 
 def attend_back(qkv, probs, d_attended, pos_buckets, box_buckets):
@@ -430,6 +432,7 @@
         out_shape=(
             jax.ShapeDtypeStruct((docs, padded, 3 * width), BF16),
             jax.ShapeDtypeStruct((64, LANES), F32),
+            jax.ShapeDtypeStruct((8, 3 * width), F32),
         ),
         grid=(docs, padded // BLOCK),
         in_specs=[
@@ -444,6 +447,7 @@
         out_specs=(
             pl.BlockSpec((1, padded, 3 * width), lambda d, i: (d, 0, 0)),
             pl.BlockSpec((64, LANES), lambda d, i: (0, 0)),
+            pl.BlockSpec((8, 3 * width), lambda d, i: (0, 0)),
         ),
         scratch_shapes=[
             pltpu.VMEM((width, padded), F32),
@@ -570,7 +574,9 @@
     )(attended, d_branch, low, d_upper, active, d_ffn)
 
 
-ORDERS = ((3, 1, 2, 0), (3, 2, 1, 0), (3, 1, 2, 0))
+ORDERS = ((3, 1, 2, 0), (3, 2, 1, 0)) * 3
+MATRICES = 3
+TABLE_LINES = 64
 MESH = pl.DeviceIdType.MESH
 
 
@@ -581,11 +587,12 @@
 def tail_kernel(
     dims, w_ref, tok_ref, mixed_ref, one_ref, small_ref, grad_ref, sums_ref, input_ref, *scratch
 ):
-    parts, width = len(ORDERS), tok_ref.shape[1]
+    parts, width = len(ORDERS), tok_ref.shape[0]
+    cut = MATRICES * width // parts
     holders = [scratch[8 * part : 8 * part + 4] for part in range(parts)]
     inboxes = [scratch[8 * part + 4 : 8 * part + 8] for part in range(parts)]
     (
-        tok, turned, mixed, weights, kept, stage, own_sums, got_sums,
+        turned, mixed, weights, kept, stage, own_sums, got_sums,
         send_sems, recv_sems, load_sems, keep_sems, store_sems,
     ) = scratch[8 * parts :]
     deep, across, along, cores = dims
@@ -593,15 +600,15 @@
     mine = (dp // across, dp % across, fsdp // cores, fsdp % cores)
     docs, padded = one_ref.shape[0], one_ref.shape[1]
     rows, block = input_ref.shape[1], kept.shape[1]
-    own_lines = small_ref.shape[0]
+    own_lines = sums_ref.shape[0] - TABLE_LINES
 
     def peer(axis, step):
         place = list(mine)
         place[axis] = (place[axis] + step) % dims[axis]
         return place[axis], (place[0] * across + place[1], place[2] * cores + place[3])
 
-    loads = [pltpu.make_async_copy(tok_ref, tok, load_sems.at[0])]
-    for part in range(parts):
+    loads = [pltpu.make_async_copy(tok_ref, turned, load_sems.at[0])]
+    for part in range(MATRICES):
         loads.append(
             pltpu.make_async_copy(
                 mixed_ref.at[:, pl.ds(part * width, width)], mixed.at[part], load_sems.at[1 + part]
@@ -609,7 +616,7 @@
         )
     loads.append(
         pltpu.make_async_copy(
-            w_ref.at[:, pl.ds(0, parts * width)], weights, load_sems.at[1 + parts]
+            w_ref.at[:, pl.ds(0, MATRICES * width)], weights, load_sems.at[1 + MATRICES]
         )
     )
     for load in loads:
@@ -670,7 +677,7 @@
         left = [item for item in axes if item != axis]
         count = dims[axis] - 1
         if not left:
-            grad_ref[:, part * width : (part + 1) * width] = joined(
+            grad_ref[:, part * cut : (part + 1) * cut] = joined(
                 source[mine[axis]], [box[slot] for slot in range(count)]
             )
             return
@@ -693,27 +700,39 @@
         send(part, level + 1)
 
     small_order = (3, 1, 2, 0)
+    own_bins = deep * own_lines
 
     def small_send(level):
-        axis = small_order[level]
-        first = sum(dims[item] - 1 for item in small_order[:level])
+        axis, lane = small_order[level], 4 * parts + level
+        if level < 3:
+            launch(lane, axis, lambda place: own_sums.at[level], lambda slot: got_sums.at[level, slot])
+            return
         launch(
-            4 * parts + level, axis,
-            lambda place: own_sums.at[level], lambda slot: got_sums.at[first + slot],
+            lane, axis,
+            lambda place: own_sums.at[3, pl.ds(pl.multiple_of(place * own_lines, 8), own_lines)],
+            lambda slot: got_sums.at[3, slot, pl.ds(0, own_lines)],
         )
+        launch(
+            lane + 1, axis,
+            lambda place: own_sums.at[3, pl.ds(own_bins, TABLE_LINES)],
+            lambda slot: got_sums.at[3, slot, pl.ds(own_bins, TABLE_LINES)],
+        )
 
     def small_join(level):
-        land(4 * parts + level)
-        axis = small_order[level]
-        first = sum(dims[item] - 1 for item in small_order[:level])
-        total = joined(
-            own_sums[level], [got_sums[first + slot] for slot in range(dims[axis] - 1)]
+        axis, lane = small_order[level], 4 * parts + level
+        land(lane)
+        slots = range(dims[axis] - 1)
+        if level < 3:
+            own_sums[level + 1] = joined(own_sums[level], [got_sums[level, slot] for slot in slots])
+            small_send(level + 1)
+            return
+        land(lane + 1)
+        here = pl.ds(pl.multiple_of(mine[0] * own_lines, 8), own_lines)
+        sums_ref[0:own_lines] = joined(
+            own_sums[3, here], [got_sums[3, slot, 0:own_lines] for slot in slots]
         )
-        if level == 3:
-            sums_ref[...] = total
-        else:
-            own_sums[level + 1] = total
-            small_send(level + 1)
+        last = slice(own_bins, own_bins + TABLE_LINES)
+        sums_ref[own_lines:] = joined(own_sums[3, last], [got_sums[3, slot, last] for slot in slots])
 
     spans = [(doc, first) for doc in range(docs) for first in range(0, padded, block)]
 
@@ -735,7 +754,7 @@
     def input_step(step):
         doc, first = spans[step]
         if step == 0:
-            loads[1 + parts].wait()
+            loads[1 + MATRICES].wait()
             keep(0).start()
         if step + 1 < len(spans):
             keep(step + 1).start()
@@ -744,7 +763,7 @@
             store(step - 2).wait()
         at = pl.ds(doc * padded + first, block)
         total = kept[step % 2]
-        for part in range(parts):
+        for part in range(MATRICES):
             total = total + dot_nt(
                 mixed[part, at, :], weights[:, part * width : (part + 1) * width]
             )
@@ -752,47 +771,48 @@
         store(step).start()
 
     loads[0].wait()
-    turned[...] = tok[...].T
-    ones = jnp.ones((16, tok.shape[0]), BF16)
-    own_sums[0, 0:own_lines] = small_ref[...]
-
-    def multiply(part):
-        loads[1 + part].wait()
-        rest = holders[part][0].shape
-        block_rows = dot(turned[...], mixed[part]).astype(BF16)
-        holders[part][0][...] = block_rows.reshape(rest)
-        line = dot(ones, mixed[part])[0:8]
-        share = 8 * width // LANES // 8
-        for chunk in range(share):
-            own_sums[0, pl.ds(own_lines + (part * share + chunk) * 8, 8)] = line[
-                :, chunk * LANES : (chunk + 1) * LANES
-            ]
-        send(part, 0)
+    own_sums[0] = small_ref[...]
+    small_send(0)
+
+    def multiply(matrix):
+        loads[1 + matrix].wait()
+        for part in range(matrix * parts // MATRICES, (matrix + 1) * parts // MATRICES):
+            first = part * cut - matrix * width
+            block_rows = dot(turned[...], mixed[matrix, :, first : first + cut]).astype(BF16)
+            holders[part][0][...] = block_rows.reshape(holders[part][0].shape)
+            send(part, 0)
 
     multiply(0)
+    small_join(0)
     multiply(1)
+    join(0, 0)
+    join(1, 0)
     multiply(2)
-    small_send(0)
-    join(0, 0)
+    small_join(1)
+    join(2, 0)
+    join(3, 0)
+    join(0, 1)
+    join(1, 1)
+    join(4, 0)
+    join(5, 0)
+    small_join(2)
     input_step(0)
-    join(1, 0)
-    join(0, 1)
-    small_join(0)
-    join(2, 0)
-    join(1, 1)
+    join(2, 1)
+    join(3, 1)
+    join(0, 2)
+    join(1, 2)
     input_step(1)
-    join(0, 2)
-    small_join(1)
-    join(2, 1)
-    join(1, 2)
+    join(4, 1)
+    join(5, 1)
+    join(2, 2)
+    join(3, 2)
     input_step(2)
-    small_join(2)
-    join(2, 2)
+    small_join(3)
+    join(4, 2)
+    join(5, 2)
     input_step(3)
-    join(0, 3)
-    join(1, 3)
-    join(2, 3)
-    small_join(3)
+    for part in range(parts):
+        join(part, 3)
     for step in range(max(len(spans) - 2, 0), len(spans)):
         store(step).wait()
 
@@ -807,9 +827,10 @@
 def tail(w_mixed, tok, d_mixed, d_one, small, rows, dims):
     docs, padded, width = d_one.shape
     parts = len(ORDERS)
+    cut = MATRICES * width // parts
     devices = dims[0] * dims[1] * dims[2] * dims[3]
     own = width // devices
-    lines = small.shape[0] + parts * 8 * width // LANES
+    lines = (small.shape[0] - TABLE_LINES) // dims[0] + TABLE_LINES
     any_space = pl.BlockSpec(memory_space=pl.ANY)
     vmem = pl.BlockSpec(memory_space=pltpu.VMEM)
     scratch = []
@@ -818,12 +839,12 @@
         for level in range(4):
             axes = remaining(part, level)
             axis = ORDERS[part][level]
-            scratch.append(pltpu.VMEM(tuple(dims[item] for item in axes) + (own, width), BF16))
+            scratch.append(pltpu.VMEM(tuple(dims[item] for item in axes) + (own, cut), BF16))
             boxes.append(
                 pltpu.VMEM(
                     (max(dims[axis] - 1, 1),)
                     + tuple(dims[item] for item in axes if item != axis)
-                    + (own, width),
+                    + (own, cut),
                     BF16,
                 )
             )
@@ -831,24 +852,23 @@
     most = max(max(dims) - 1, 1)
     flat = docs * padded
     scratch += [
-        pltpu.VMEM((flat, width), BF16),
         pltpu.VMEM((width, flat), BF16),
-        pltpu.VMEM((parts, flat, width), BF16),
-        pltpu.VMEM((width, parts * width), BF16),
+        pltpu.VMEM((MATRICES, flat, width), BF16),
+        pltpu.VMEM((width, MATRICES * width), BF16),
         pltpu.VMEM((2, DENSE_BLOCK, width), F32),
         pltpu.VMEM((2, DENSE_BLOCK, 1, width), F32),
-        pltpu.VMEM((4, lines, LANES), F32),
-        pltpu.VMEM((sum(dims) - 4, lines, LANES), F32),
-        pltpu.SemaphoreType.DMA((4 * parts + 4, most)),
-        pltpu.SemaphoreType.DMA((4 * parts + 4, most)),
-        pltpu.SemaphoreType.DMA((parts + 2,)),
+        pltpu.VMEM((4,) + small.shape, F32),
+        pltpu.VMEM((4, most) + small.shape, F32),
+        pltpu.SemaphoreType.DMA((4 * parts + 5, most)),
+        pltpu.SemaphoreType.DMA((4 * parts + 5, most)),
+        pltpu.SemaphoreType.DMA((MATRICES + 2,)),
         pltpu.SemaphoreType.DMA((2,)),
         pltpu.SemaphoreType.DMA((2,)),
     ]
     return pl.pallas_call(
         partial(tail_kernel, dims),
         out_shape=(
-            jax.ShapeDtypeStruct((own, parts * width), F32),
+            jax.ShapeDtypeStruct((own, MATRICES * width), F32),
             jax.ShapeDtypeStruct((lines, LANES), F32),
             jax.ShapeDtypeStruct((docs, rows, 1, width), F32),
         ),
@@ -862,18 +882,25 @@
     )(w_mixed, tok, d_mixed, d_one, small)
 
 
-def small_results(packed, width, hidden, heads):
-    lines, more = 8 * width // LANES, hidden // LANES
-    sums = packed[:lines].reshape(8, width)
-    up_sum = packed[lines : lines + more].reshape(hidden)
-    d_table = table_grad(packed[lines + more : lines + more + 64], heads)
-    mixed = packed[lines + more + 64 :].reshape(3, width // LANES, 8, LANES)[:, :, 0]
-    mixed = mixed.reshape(3, width)
-    d_biases = jnp.concatenate([mixed[0:1], mixed[2:3], sums[6:8]], axis=0)
-    return sums[0:2], sums[2:4], d_biases, up_sum, d_table
-
-
-def local_step(devices, lengths, pos_buckets, box_buckets, layer_input, cotangent, w_mixed, w_down, vectors, up_row, table):
+def packed_sums(sums, up_sum, bins, deep):
+    width, hidden = sums.shape[1], up_sum.shape[1]
+    sums = jnp.transpose(sums.reshape(8, deep, width // deep), (1, 0, 2)).reshape(deep, -1)
+    lines = jnp.concatenate([sums, up_sum.reshape(deep, hidden // deep)], axis=1)
+    share = pl.cdiv(lines.shape[1], 8 * LANES) * 8 * LANES
+    lines = jnp.pad(lines, ((0, 0), (0, share - lines.shape[1])))
+    return jnp.concatenate([lines.reshape(-1, LANES), bins], axis=0)
+
+
+def small_results(packed, width, hidden, heads, deep, own, rank):
+    flat = packed[:-TABLE_LINES].reshape(-1)
+    count, more = 8 * width // deep, hidden // deep
+    sums = lax.dynamic_slice_in_dim(flat[:count].reshape(8, -1), rank * own, own, 1)
+    fold = hidden // width * own
+    up_sum = lax.dynamic_slice_in_dim(flat[count : count + more], rank * fold, fold, 0)
+    return sums, up_sum, table_grad(packed[-TABLE_LINES:], heads)
+
+
+def local_step(dims, lengths, pos_buckets, box_buckets, layer_input, cotangent, w_mixed, w_down, vectors, up_row, table):
     heads, width = table.shape[1], layer_input.shape[3]
     docs, rows = layer_input.shape[0], layer_input.shape[2]
     bias = bias_rows(lengths, table_entries(table), pos_buckets, box_buckets, heads)
@@ -887,13 +914,14 @@
         return item.reshape(-1, item.shape[-1])
 
     d_weights = weight_grads(
-        flat(attended), flat(d_branch), flat(low), flat(d_upper), flat(active), flat(d_ffn), devices
-    )
-    d_mixed, bins = attend_back(qkv, probs, d_attended, pos_buckets, box_buckets)
-    packed = jnp.concatenate(
-        [sums.reshape(-1, LANES), up_sum.reshape(-1, LANES), bins], axis=0
-    )
-    return result, d_weights, (w_mixed, flat(tok), flat(d_mixed), d_one, packed, rows)
+        flat(attended), flat(d_branch), flat(low), flat(d_upper), flat(active), flat(d_ffn), dims[0] * dims[1] * dims[2] * dims[3]
+    )
+    d_mixed, bins, line = attend_back(qkv, probs, d_attended, pos_buckets, box_buckets)
+    sums = jnp.concatenate(
+        [sums[:4], line[:1, :width], line[:1, 2 * width :], sums[6:]], axis=0
+    )
+    packed = packed_sums(sums, up_sum, bins, dims[0])
+    return result, d_weights, (w_mixed, tok, flat(d_mixed), d_one, packed, rows, dims)
 
 
 def body(
@@ -916,9 +944,9 @@
     small = w_mixed[:, 4 * width + hidden :].astype(F32)
     vectors = small[:, :8].T
     up_row = small[:, 8 : 8 + hidden // width].reshape(1, hidden)
-    devices = width // own
+    dims = split_mesh(lax.axis_size("dp"), lax.axis_size("fsdp"))
     result, d_weights, rest = local_step(
-        devices, text_lengths[:, 0], pos_buckets, box_buckets, layer_input, cotangent, w_mixed, w_down,
+        dims, text_lengths[:, 0], pos_buckets, box_buckets, layer_input, cotangent, w_mixed, w_down,
         vectors, up_row, table,
     )
     d_weights = lax.psum_scatter(
@@ -926,21 +954,14 @@
     ).astype(F32)
     d_down = [d_weights[:, first : first + width] for first in range(width + hidden, width + 2 * hidden, width)]
     d_down = jnp.concatenate(d_down, axis=0)
-    d_qkv, packed, input_grad = tail(
-        *rest, split_mesh(lax.axis_size("dp"), lax.axis_size("fsdp"))
-    )
-    d_gains, d_shifts, d_biases, up_sum, d_table = small_results(packed, width, hidden, heads)
-    place = lax.axis_index(axes)
-    d_gains, d_shifts, d_biases = (
-        lax.dynamic_slice_in_dim(item, place * own, own, 1)
-        for item in (d_gains, d_shifts, d_biases)
-    )
-    up_sum = lax.dynamic_slice_in_dim(up_sum, place * up_bias.shape[0], up_bias.shape[0], 0)
+    d_qkv, packed, input_grad = tail(*rest)
+    rank = lax.axis_index(axes) % (width // own // dims[0])
+    sums, up_sum, d_table = small_results(packed, width, hidden, heads, dims[0], own, rank)
     table_rows = rel_tables.shape[0]
     d_table = lax.dynamic_slice_in_dim(d_table, lax.axis_index("fsdp") * table_rows, table_rows, 0)
     return (
         result, jnp.transpose(input_grad, (0, 2, 1, 3)), d_qkv, d_weights[:, :width], d_weights[:, width : width + hidden], d_down,
-        d_gains, d_shifts, d_biases, up_sum, d_table,
+        sums[0:2], sums[2:4], sums[4:8], up_sum, d_table,
     )
 
 

time: 468 us -> 450 us (0.962)
  Pallas kernels: 387 us -> 370 us
    pallas_call x1, Pallas kernels: 55.8 us -> 38.1 us  [tail(): pl.pallas_call(partial(tail_kernel, dims), out_shape=(jax.ShapeDtypeStruc...]
    unnamed x28 -> x30, local copies, waits for them, and re-layouts: 29.5 us -> 29.5 us
  transfers between devices with their start and end apart: 3 -> 3, of which waited for: 1 -> 1; matrix products, arithmetic and copies ran while one was open for 6% -> 7% of each run, Pallas kernels for 67% -> 66%
where the time goes in v5:
time: 450 us; the launch traced here: 442 us
  Pallas kernels  370 us (82%)
  local copies, waits for them, and re-layouts  39.5 us (9%)
  between operations  14.4 us (3%)
  other arithmetic  7.13 us (2%)
  blocking collectives  6.2 us (1%)
  waiting for transfers between devices  5.27 us (1%)
    pallas_call x1, Pallas kernels, attend_back(): pl.pallas_call(partial(attend_back_kernel, rows), out_shape=(jax.ShapeDty...  134 us
    pallas_call x1, Pallas kernels, bias_rows(): pl.pallas_call(partial(bias_kernel, rows), out_shape=jax.ShapeDtypeStruct...  69.5 us
    pallas_call x1, Pallas kernels, dense(): pl.pallas_call(partial(dense_kernel, rows), out_shape=(jax.ShapeDtypeStru...  52.2 us
    pallas_call x1, Pallas kernels, attend(): pl.pallas_call(attend_kernel, out_shape=(jax.ShapeDtypeStruct((docs, head...  40.8 us
    pallas_call x1, Pallas kernels, tail(): pl.pallas_call(partial(tail_kernel, dims), out_shape=(jax.ShapeDtypeStruc...  38.1 us
    unnamed x30, local copies, waits for them, and re-layouts  29.5 us
    pallas_call x1, Pallas kernels, weight_grads(): pl.pallas_call(kernel, out_shape=jax.ShapeDtypeStruct((devices, own, (1 +...  25.2 us
    pallas_call x1, Pallas kernels, project(): pl.pallas_call(partial(project_kernel, rows), out_shape=(jax.ShapeDtypeSt...  9.98 us
  transfers between devices with their start and end apart: 3, of which 1 were waited for; matrix products, arithmetic and copies ran while one was open for 7% of the time, Pallas kernels for 66%

profile of v5, /device:TPU:0, one launch (start us, length us, event | category | flops | bytes accessed | tf_op | source)
XLA Modules:
  0.0 442.3 jit_solution(3261868434102310717)
XLA Ops:
  8.7 0.8 copy.57
  10.3 1.7 pad_maximum_fusion
  12.9 3.3 copy.63.x_ref
  16.2 6.2 %all-gather = bf16[4,40,12]{1,2,0:T(8,128)(2,1)S(1)} all-gather(bf16[1,40,12]{1,2,0:T(8,128)(2,1)S(1)} %bitcast.35), channel_id=1, replica_groups=mesh['dp'=8,'fsdp'=4] {'fsdp'}, dimensions={0}, use_global_device_ids=true | all-gather | bytes 4800 | tf_op jit(solution)/shard_map/all_gather | solution.py:934
  22.5 8.1 %copy.62.box_ref = s32[2,1,2,709,709]{4,3,2,1,0:T(8,128)} copy(s32[2,1,2,709,709]{4,2,3,1,0:T(2,128)} %param.17) | data formatting | bytes 16085792 | tf_op args[3]
  30.6 2.3 copy.61.pos_ref
  33.1 1.6 copy.64.cot_ref
  35.4 69.5 %bias_rows.1.bias_ref = f32[2,12,768,768]{3,2,1,0:T(8,128)} custom-call(s32[2]{0:T(128)} %bitcast.36, f32[24,128]{1,0:T(8,128)} %pad_maximum_fusion.4.tab_ref, s32[2,1,709,709]{3,2,1,0:T(8,128)} %copy.61.pos_ref, s32[2,1,2,709,709]{4,3,2,1,0:T(8,128)} %copy.62.box_ref), custom_call_target="tpu_custom_call" | custom-call | flops 36193032 | bytes 70778880 | tf_op jit(solution)/shard_map/bias_rows/pallas_call | solution.py:97
  104.9 1.0 slice_convert_fusion
  106.8 0.9 reshape.72.upb_ref
  107.7 10.0 %project.1 = (bf16[2,768,2304]{2,1,0:T(8,128)(2,1)}, bf16[768,1536]{1,0:T(8,128)(2,1)}) custom-call(bf16[2,1,709,768]{3,2,1,0:T(8,128)(2,1)} %copy.63.x_ref, bf16[768,6272]{1,0:T(8,128)(2,1)} %all-gather.4.cloned.1.call-done.w_ref.wo_ref.wu_ref, f32[8,768]{1,0:T(8,128)} %copy.59.vec_ref), custom_call_target="tpu_custom_call" | custom-call | tf_op jit(solution)/shard_map/project/pallas_call | solution.py:132
  117.7 40.8 %attend.1 = (bf16[2,12,768,768]{3,2,1,0:T(8,128)(2,1)}, bf16[2,768,768]{2,1,0:T(8,128)(2,1)}) custom-call(bf16[2,768,2304]{2,1,0:T(8,128)(2,1)} %get-tuple-element.31.q_ref.k_ref.v_ref, bf16[2,768,2304]{2,1,0:T(8,128)(2,1)} %get-tuple-element.31.q_ref.k_ref.v_ref, bf16[2,768,2304]{2,1,0:T(8,128)(2,1)} %get-tuple-element.31.q_ref.k_ref.v_ref, ...), custom_call_target="tpu_custom_call" | custom-call | tf_op jit(solution)/shard_map/attend/pallas_call | solution.py:176
  158.4 4.5 %all-gather.6.cloned.1.call-done.wd_ref = bf16[3072,768]{1,0:T(8,128)(2,1)} async-done(((bf16[96,768]{1,0:T(8,128)(2,1)}), bf16[3072,768]{1,0:T(8,128)(2,1)}) %all-gather.6.cloned.1.call-update) | async-done | bytes 4718608 | tf_op jit(solution)/shard_map/all_gather | solution.py:943
  163.0 52.2 %dense.1 = (bf16[2,1,709,768]{3,2,1,0:T(8,128)(2,1)}, f32[2,768,768]{2,1,0:T(8,128)}, bf16[2,768,768]{2,1,0:T(8,128)(2,1)}, bf16[2,768,3072]{2,1,0:T(8,128)(2,1)...) custom-call(bf16[2,1,709,768]{3,2,1,0:T(8,128)(2,1)} %copy.63.x_ref,, ...), custom_call_target="tpu_custom_call" | custom-call | tf_op jit(solution)/shard_map/dense/pallas_call | solution.py:277
  215.2 25.2 %weight_grads.1 = bf16[32,24,6912]{2,1,0:T(8,128)(2,1)} custom-call(bf16[1536,768]{1,0:T(8,128)(2,1)} %bitcast.29, bf16[1536,768]{1,0:T(8,128)(2,1)} %bitcast.41, bf16[1536,768]{1,0:T(8,128)(2,1)} %bitcast.39, bf16[1536,3072]{1,0:T(8,128)(2,1)} %bitcast.38, bf16[1536,3072]{1,0:T(8,128)(2,1)} %bitcast.37, bf16[1536,768]{1,0:T(8,128)(2,1)} %bitcast.40), custom_call_target="tpu_custom_call" | custom-call | flops 16307453952 | bytes 28311552 | tf_op jit(solution)/shard_map/weight_grads/pallas_call | solution.py:550
  241.2 133.9 %attend_back.1 = (bf16[2,768,2304]{2,1,0:T(8,128)(2,1)}, f32[64,128]{1,0:T(8,128)}, f32[8,2304]{1,0:T(8,128)}) custom-call(bf16[2,768,2304]{2,1,0:T(8,128)(2,1)} %get-tuple-element.31.q_ref.k_ref.v_ref, bf16[2,768,2304]{2,1,0:T(8,128)(2,1)} %get-tuple-element.31.q_ref.k_ref.v_ref, bf16[2,768,2304]{2,1,0:T(8,128)(2,1)} %get-tuple-element.31.q_ref.k_ref.v_ref, ...), custom_call_target="tpu_custom_call" | custom-call | tf_op jit(solution)/shard_map/attend_back/pallas_call | solution.py:430
  375.1 0.8 fusion.9
  377.3 1.4 pad_maximum_fusion.2.small_ref
  378.7 38.1 %tail.1 = (f32[24,2304]{1,0:T(8,128)}, f32[88,128]{1,0:T(8,128)}, f32[2,709,1,768]{3,2,1,0:T(1,128)}) custom-call(bf16[768,6272]{1,0:T(8,128)(2,1)} %all-gather.4.cloned.1.call-done.w_ref.wo_ref.wu_ref, bf16[768,1536]{1,0:T(8,128)(2,1)} %get-tuple-element.34.tok_ref, bf16[1536,2304]{1,0:T(8,128)(2,1)} %bitcast.25, f32[2,768,768]{2,1,0:T(8,128)} %get-tuple-element.38.one_ref, ...), custom_call_target="tpu_custom_call" | custom-call | tf_op jit(solution)/shard_map/tail/pallas_call | solution.py:868
  416.8 0.8 slice.116
  418.3 3.0 copy.69
  423.4 1.5 fusion.8
  425.7 1.6 slice.134
  427.3 7.3 %copy.72 = f32[2,1,709,768]{3,1,2,0:T(1,128)} copy(f32[2,1,709,768]{3,1,2,0:T(1,128)} %bitcast.26) | data formatting | bytes 8712192
  (64 shorter events, 11.5 us)
Async XLA Ops:
  7.2 9.0 %copy-start.6 = (bf16[40,12]{0,1:T(8,128)(2,1)S(1)}, bf16[40,12]{0,1:T(8,128)(2,1)}, u32[]{:S(2)}) copy-start(bf16[40,12]{0,1:T(8,128)(2,1)} %param.26) | copy-start | bytes 2884
  7.2 97.8 %all-gather.4.cloned.1.call-start = ((), (), s32[]{:S(2)}) async-start(), calls=%async_computation.1 | async-start | bytes 9934848 | tf_op jit(solution)/shard_map/all_gather | solution.py:940
  12.1 150.9 %all-gather.6.cloned.1.call-start = ((), (), s32[]{:S(2)}) async-start(), calls=%async_computation.2 | async-start | bytes 4866048 | tf_op jit(solution)/shard_map/all_gather | solution.py:943
  12.9 410.6 %reduce-scatter.2.cloned.1.call-start = ((), (), s32[]{:S(2)}) async-start(), calls=%async_computation.3 | async-start | bytes 10948608 | tf_op jit(solution)/shard_map/reduce_scatter | solution.py:952
  12.9 17.7 %slice-start = ((s8[4356096]{0:T(1024)(128)(4,1)}), s8[161792]{0:T(1024)(128)(4,1)S(1)}, s32[]{:S(2)}) async-start(s8[4356096]{0:T(1024)(128)(4,1)} %bitcast.27), calls=%async_computation.4 | async-start | bytes 323584
  22.5 8.1 %slice-start.1 = ((s8[4356096]{0:T(1024)(128)(4,1)}), s8[4194304]{0:T(1024)(128)(4,1)S(1)}, s32[]{:S(2)}) async-start(s8[4356096]{0:T(1024)(128)(4,1)} %bitcast.27), calls=%async_computation.5 | async-start | bytes 8388608
  30.6 2.5 copy-start.1
  33.1 1.6 copy-start.7
  240.4 0.7 copy-start.4
  241.1 135.4 %copy-start.5 = (f32[1,3072]{1,0:T(1,128)S(1)}, f32[1,3072]{1,0:T(1,128)}, u32[]{:S(2)}) copy-start(f32[1,3072]{1,0:T(1,128)} %get-tuple-element.41) | copy-start | bytes 36868
  378.7 39.6 %copy-start = (bf16[2,1,709,768]{3,2,1,0:T(8,128)(2,1)S(1)}, bf16[2,1,709,768]{3,2,1,0:T(8,128)(2,1)}, u32[]{:S(2)}) copy-start(bf16[2,1,709,768]{3,2,1,0:T(8,128)(2,1)} %get-tuple-element.73) | copy-start | bytes 6534148
  416.8 4.5 %copy-start.3 = (f32[88,128]{1,0:T(8,128)S(1)}, f32[88,128]{1,0:T(8,128)}, u32[]{:S(2)}) copy-start(f32[88,128]{1,0:T(8,128)} %get-tuple-element.50) | copy-start | bytes 135172
  427.3 7.3 %copy-start.2 = (f32[24,2304]{1,0:T(8,128)S(1)}, f32[24,2304]{1,0:T(8,128)}, u32[]{:S(2)}) copy-start(f32[24,2304]{1,0:T(8,128)} %get-tuple-element.114) | copy-start | bytes 663556
Sparse Core Ops, SparseCore 0:
  12.2 85.5 all-gather.3
  100.7 62.2 all-gather.5
  240.5 140.5 reduce-scatter.1

commit v6 on v5

--- a/solution.py
+++ b/solution.py
@@ -150,7 +150,7 @@
     )(layer_input, w_mixed, vectors)
 
 
-def attend_kernel(q_ref, k_ref, v_ref, bias_ref, probs_ref, out_ref):
+def attend_kernel(q_ref, k_ref, v_ref, bias_ref, probs_ref, out_ref, turned_ref):
     lane = lax.broadcasted_iota(jnp.int32, (1, LANES), 1)
     for pair in range(q_ref.shape[2] // LANES):
         cols = slice(pair * LANES, (pair + 1) * LANES)
@@ -167,7 +167,9 @@
             probs_ref[0, head] = probs
             part = dot(probs, jnp.where(keep, values, BF16(0)))
             total = part if half == 0 else total + part
-        out_ref[0, :, cols] = total.astype(BF16)
+        low = total.astype(BF16)
+        out_ref[0, :, cols] = low
+        turned_ref[cols, :] = low.T
 
 
 def attend(qkv, bias):
@@ -178,6 +180,7 @@
         out_shape=(
             jax.ShapeDtypeStruct((docs, heads, padded, padded), BF16),
             jax.ShapeDtypeStruct((docs, padded, width), BF16),
+            jax.ShapeDtypeStruct((width, docs * padded), BF16),
         ),
         grid=(docs, padded // BLOCK),
         in_specs=[
@@ -189,6 +192,7 @@
         out_specs=(
             pl.BlockSpec((1, heads, BLOCK, padded), lambda d, i: (d, 0, i, 0)),
             pl.BlockSpec((1, BLOCK, width), lambda d, i: (d, i, 0)),
+            pl.BlockSpec((width, BLOCK), lambda d, i: (0, d * (padded // BLOCK) + i)),
         ),
         compiler_params=params(2),
         name="attend",
@@ -212,7 +216,7 @@
 
 def dense_kernel(
     rows, x_ref, o_ref, cot_ref, wo_ref, wu_ref, wd_ref, vec_ref, upb_ref,
-    y_ref, dr_ref, h_ref, g_ref, du_ref, df_ref, db_ref, do_ref, sums_ref, upsum_ref,
+    y_ref, dr_ref, left_ref, du_ref, df_ref, db_ref, do_ref, sums_ref, upsum_ref,
     slope_ref,
 ):
     width, hidden = wu_ref.shape
@@ -228,7 +232,7 @@
     normed_one, inv_one = norm(tok + dot(o_ref[0], wo_ref[...]) + vec[6:7])
     state = normed_one * vec[0:1] + vec[2:3]
     low = state.astype(BF16)
-    h_ref[0] = low
+    left_ref[0:width, :] = low.T
     second = state + vec[7:8]
     for part in range(hidden // width):
         cols = slice(part * width, (part + 1) * width)
@@ -236,7 +240,7 @@
         cdf = 0.5 * (1.0 + lax.erf(upper * (0.5**0.5)))
         slope_ref[:, cols] = cdf + upper * (jnp.exp(-0.5 * upper * upper) * 0.3989422804014327)
         active = (upper * cdf).astype(BF16)
-        g_ref[0, :, cols] = active
+        left_ref[(part + 1) * width : (part + 2) * width, :] = active.T
         second = second + dot(active, wd_ref[cols, :])
     normed_two, inv_two = norm(second)
     y_ref[0, 0] = (normed_two * vec[1:2] + vec[3:4]).astype(BF16)
@@ -271,6 +275,11 @@
     narrow = pl.BlockSpec((1, DENSE_BLOCK, width), lambda d, i: (d, i, 0))
     wide = pl.BlockSpec((1, DENSE_BLOCK, hidden), lambda d, i: (d, i, 0))
 
+    def turned(lines):
+        return pl.BlockSpec(
+            (lines, DENSE_BLOCK), lambda d, i: (0, d * (padded // DENSE_BLOCK) + i)
+        )
+
     def rows_of(columns, dtype):
         return jax.ShapeDtypeStruct((docs, padded, columns), dtype)
 
@@ -279,8 +288,7 @@
         out_shape=(
             jax.ShapeDtypeStruct(layer_input.shape, BF16),
             rows_of(width, F32),
-            rows_of(width, BF16),
-            rows_of(hidden, BF16),
+            jax.ShapeDtypeStruct((width + hidden, docs * padded), BF16),
             rows_of(hidden, BF16),
             rows_of(width, BF16),
             rows_of(width, BF16),
@@ -296,7 +304,7 @@
             resident(vectors.shape), resident(up_row.shape),
         ],
         out_specs=(
-            ragged, narrow, narrow, wide, wide, narrow, narrow, narrow,
+            ragged, narrow, turned(width + hidden), wide, narrow, narrow, narrow,
             pl.BlockSpec((8, width), lambda d, i: (0, 0)),
             pl.BlockSpec((1, hidden), lambda d, i: (0, 0)),
         ),
@@ -353,7 +361,7 @@
             dv_ref[lines, :] += dot(turned_g[part, :], low)
         dm_ref[0, own, cols] = (total * SCALE).astype(BF16)
 
-    group = 32
+    group = 64
     low_bins = lax.broadcasted_iota(jnp.int32, (HALF, LANES), 0).astype(BF16)
 
     def hits(picks, bins):
@@ -478,24 +486,33 @@
     return jnp.concatenate([pieces[2], pieces[0], pieces[1]], axis=1).T * SCALE
 
 
-def weight_grads(attended, d_branch, low, d_upper, active, d_ffn, devices):
-    rows, width = attended.shape
+def weight_grads(attended, d_branch, left, d_upper, d_ffn, devices):
+    width, rows = attended.shape
     own, fold = width // devices, d_upper.shape[1] // width
     share = devices // fold
     steps = 1 + 2 * fold
 
-    def kernel(a_ref, b_ref, l_ref, u_ref, g_ref, f_ref, out_ref, turned_ref, stage_ref, sems):
+    def kernel(
+        l_ref, u_ref, a_ref, b_ref, f_ref, out_ref,
+        attended_ref, branch_ref, ffn_ref, stage_ref, sems, load_sems,
+    ):
         step = pl.program_id(0)
         slot = step % 2
-
-        def flat_copy(where, spot):
-            cols = pl.ds(pl.multiple_of(where * width, width), width)
+        loads = [
+            pltpu.make_async_copy(source, target, load_sems.at[place])
+            for place, (source, target) in enumerate(
+                ((f_ref, ffn_ref), (a_ref, attended_ref), (b_ref, branch_ref))
+            )
+        ]
+
+        def flat_copy(part, spot):
+            cols = pl.ds(pl.multiple_of(part * width, width), width)
             return pltpu.make_async_copy(
                 stage_ref.at[spot], out_ref.at[:, :, cols], sems.at[spot, 0]
             )
 
         def fold_copy(where, spot, part):
-            block = where - 1 - fold
+            block = where - fold
             cols = pl.ds((1 + fold + part) * width, width)
             return pltpu.make_async_copy(
                 stage_ref.at[spot].reshape(share, fold, own, width).at[:, part],
@@ -504,66 +521,71 @@
             )
 
         def wait_for(where, spot):
-            @pl.when(where <= fold)
+            @pl.when(where < fold)
             def _():
-                flat_copy(where, spot).wait()
-
-            @pl.when(where > fold)
+                flat_copy(where + 1, spot).wait()
+
+            @pl.when((where >= fold) & (where < 2 * fold))
             def _():
                 for part in range(fold):
                     fold_copy(where, spot, part).wait()
 
+        @pl.when(step == 0)
+        def _():
+            for load in loads:
+                load.start()
+
         @pl.when(step >= 2)
         def _():
             wait_for(step - 2, slot)
 
         def put(value):
-            stage_ref[slot] = value.astype(BF16).reshape(devices, own, width)
-
-        @pl.when(step == 0)
+            stage_ref[slot] = value.reshape(devices, own, width).astype(BF16)
+
+        @pl.when(step < fold)
         def _():
-            put(dot(a_ref[...].T, b_ref[...]))
-            turned_ref[...] = l_ref[...].T
-
-        @pl.when((step > 0) & (step <= fold))
+            put(dot(l_ref[...], u_ref[...]))
+            flat_copy(step + 1, slot).start()
+
+        @pl.when(step == fold)
         def _():
-            put(dot(turned_ref[...], u_ref[...]))
-
-        @pl.when(step > fold)
+            loads[0].wait()
+
+        @pl.when((step >= fold) & (step < 2 * fold))
         def _():
-            put(dot(g_ref[...].T, f_ref[...]))
-
-        @pl.when(step <= fold)
-        def _():
-            flat_copy(step, slot).start()
-
-        @pl.when(step > fold)
-        def _():
+            put(dot(l_ref[...], ffn_ref[...]))
             for part in range(fold):
                 fold_copy(step, slot, part).start()
 
-        @pl.when(step == steps - 1)
+        @pl.when(step == 2 * fold)
         def _():
+            loads[1].wait()
+            loads[2].wait()
+            put(dot(attended_ref[...], branch_ref[...]))
+            flat_copy(0, slot).start()
             wait_for(step - 1, 1 - slot)
-            wait_for(step, slot)
-
+            flat_copy(0, slot).wait()
+
+    away = pl.BlockSpec(memory_space=pl.ANY)
     return pl.pallas_call(
         kernel,
         out_shape=jax.ShapeDtypeStruct((devices, own, (1 + 2 * fold) * width), BF16),
         grid=(steps,),
         in_specs=[
-            resident((rows, width)),
-            resident((rows, width)),
-            resident((rows, width)),
-            pl.BlockSpec((rows, width), lambda p: (0, jnp.clip(p - 1, 0, fold - 1))),
-            pl.BlockSpec((rows, width), lambda p: (0, jnp.clip(p - 1 - fold, 0, fold - 1))),
-            resident((rows, width)),
+            pl.BlockSpec((width, rows), lambda p: (jnp.clip(p - fold + 1, 0, fold), 0)),
+            pl.BlockSpec((rows, width), lambda p: (0, jnp.minimum(p, fold - 1))),
+            away,
+            away,
+            away,
         ],
-        out_specs=pl.BlockSpec(memory_space=pl.ANY),
+        out_specs=away,
         scratch_shapes=[
             pltpu.VMEM((width, rows), BF16),
+            pltpu.VMEM((rows, width), BF16),
+            pltpu.VMEM((rows, width), BF16),
             pltpu.VMEM((2, devices, own, width), BF16),
             pltpu.SemaphoreType.DMA((2, fold)),
+            pltpu.SemaphoreType.DMA((3,)),
         ],
         compiler_params=params(1),
         cost_estimate=pl.CostEstimate(
@@ -571,7 +593,7 @@
             bytes_accessed=2 * rows * width * (steps + 3),
         ),
         name="weight_grads",
-    )(attended, d_branch, low, d_upper, active, d_ffn)
+    )(left, d_upper, attended, d_branch, d_ffn)
 
 
 ORDERS = ((3, 1, 2, 0), (3, 2, 1, 0)) * 3
@@ -778,8 +800,8 @@
         loads[1 + matrix].wait()
         for part in range(matrix * parts // MATRICES, (matrix + 1) * parts // MATRICES):
             first = part * cut - matrix * width
-            block_rows = dot(turned[...], mixed[matrix, :, first : first + cut]).astype(BF16)
-            holders[part][0][...] = block_rows.reshape(holders[part][0].shape)
+            block_rows = dot(turned[...], mixed[matrix, :, first : first + cut])
+            holders[part][0][...] = block_rows.reshape(holders[part][0].shape).astype(BF16)
             send(part, 0)
 
     multiply(0)
@@ -882,6 +904,36 @@
     )(w_mixed, tok, d_mixed, d_one, small)
 
 
+def handed_on(rows_out):
+    docs, pieces = rows_out.shape[0], 4
+
+    def kernel(in_ref, out_ref, sems):
+        copies = []
+        for doc in range(docs):
+            count = rows_out.shape[1]
+            edges = [count * piece // pieces for piece in range(pieces + 1)]
+            for piece in range(pieces):
+                at = pl.ds(edges[piece], edges[piece + 1] - edges[piece])
+                copies.append(
+                    pltpu.make_async_copy(
+                        in_ref.at[doc, at], out_ref.at[doc, at], sems.at[doc, piece]
+                    )
+                )
+        for copy in copies:
+            copy.start()
+        for copy in copies:
+            copy.wait()
+
+    return pl.pallas_call(
+        kernel,
+        out_shape=jax.ShapeDtypeStruct(rows_out.shape, rows_out.dtype),
+        in_specs=[pl.BlockSpec(memory_space=pl.ANY)],
+        out_specs=pl.BlockSpec(memory_space=pl.ANY),
+        scratch_shapes=[pltpu.SemaphoreType.DMA((docs, pieces))],
+        name="handed_on",
+    )(rows_out)
+
+
 def packed_sums(sums, up_sum, bins, deep):
     width, hidden = sums.shape[1], up_sum.shape[1]
     sums = jnp.transpose(sums.reshape(8, deep, width // deep), (1, 0, 2)).reshape(deep, -1)
@@ -905,8 +957,8 @@
     docs, rows = layer_input.shape[0], layer_input.shape[2]
     bias = bias_rows(lengths, table_entries(table), pos_buckets, box_buckets, heads)
     qkv, tok = project(layer_input, w_mixed, vectors)
-    probs, attended = attend(qkv, bias)
-    result, d_one, low, active, d_upper, d_ffn, d_branch, d_attended, sums, up_sum = dense(
+    probs, attended, turned = attend(qkv, bias)
+    result, d_one, left, d_upper, d_ffn, d_branch, d_attended, sums, up_sum = dense(
         layer_input, attended, cotangent, w_mixed, w_down, vectors, up_row
     )
 
@@ -914,7 +966,7 @@
         return item.reshape(-1, item.shape[-1])
 
     d_weights = weight_grads(
-        flat(attended), flat(d_branch), flat(low), flat(d_upper), flat(active), flat(d_ffn), dims[0] * dims[1] * dims[2] * dims[3]
+        turned, flat(d_branch), left, flat(d_upper), flat(d_ffn), dims[0] * dims[1] * dims[2] * dims[3]
     )
     d_mixed, bins, line = attend_back(qkv, probs, d_attended, pos_buckets, box_buckets)
     sums = jnp.concatenate(
@@ -960,7 +1012,7 @@
     table_rows = rel_tables.shape[0]
     d_table = lax.dynamic_slice_in_dim(d_table, lax.axis_index("fsdp") * table_rows, table_rows, 0)
     return (
-        result, jnp.transpose(input_grad, (0, 2, 1, 3)), d_qkv, d_weights[:, :width], d_weights[:, width : width + hidden], d_down,
+        result, jnp.transpose(handed_on(input_grad), (0, 2, 1, 3)), d_qkv, d_weights[:, :width], d_weights[:, width : width + hidden], d_down,
         sums[0:2], sums[2:4], sums[4:8], up_sum, d_table,
     )
 

time: 450 us -> 579 us (1.29)
  Pallas kernels: 370 us -> 508 us
  local copies, waits for them, and re-layouts: 39.5 us -> 31.4 us
    pallas_call x0 -> x1, Pallas kernels: none -> 133 us  [handed_on(): pl.pallas_call(kernel, out_shape=jax.ShapeDtypeStruct(rows_out.shape, row...]
    unnamed x30 -> x29, local copies, waits for them, and re-layouts: 29.5 us -> 22.2 us
    pallas_call x1, Pallas kernels: 134 us -> 141 us  [attend_back(): pl.pallas_call(partial(attend_back_kernel, rows), out_shape=(jax.ShapeDty...]
  transfers between devices with their start and end apart: 3 -> 3, of which waited for: 1 -> 1; matrix products, arithmetic and copies ran while one was open for 7% -> 5% of each run, Pallas kernels for 66% -> 76%
where the time goes in v6:
time: 579 us; the launch traced here: 572 us
  Pallas kernels  508 us (88%)
  local copies, waits for them, and re-layouts  31.4 us (5%)
  between operations  14.4 us (2%)
  other arithmetic  7.13 us (1%)
  blocking collectives  6.2 us (1%)
    pallas_call x1, Pallas kernels, attend_back(): pl.pallas_call(partial(attend_back_kernel, rows), out_shape=(jax.ShapeDty...  141 us
    pallas_call x1, Pallas kernels, handed_on(): pl.pallas_call(kernel, out_shape=jax.ShapeDtypeStruct(rows_out.shape, row...  133 us
    pallas_call x1, Pallas kernels, bias_rows(): pl.pallas_call(partial(bias_kernel, rows), out_shape=jax.ShapeDtypeStruct...  69.5 us
    pallas_call x1, Pallas kernels, dense(): pl.pallas_call(partial(dense_kernel, rows), out_shape=(jax.ShapeDtypeStru...  51.9 us
    pallas_call x1, Pallas kernels, attend(): pl.pallas_call(attend_kernel, out_shape=(jax.ShapeDtypeStruct((docs, head...  41.4 us
    pallas_call x1, Pallas kernels, tail(): pl.pallas_call(partial(tail_kernel, dims), out_shape=(jax.ShapeDtypeStruc...  38.1 us
    pallas_call x1, Pallas kernels, weight_grads(): pl.pallas_call(kernel, out_shape=jax.ShapeDtypeStruct((devices, own, (1 +...  22.3 us
    unnamed x29, local copies, waits for them, and re-layouts  22.2 us
  transfers between devices with their start and end apart: 3, of which 1 were waited for; matrix products, arithmetic and copies ran while one was open for 5% of the time, Pallas kernels for 76%

profile of v6, /device:TPU:0, one launch (start us, length us, event | category | flops | bytes accessed | tf_op | source)
XLA Modules:
  0.0 571.5 jit_solution(14489476250696588816)
XLA Ops:
  8.7 0.8 copy.57
  9.5 0.7 reshape.62
  10.3 1.7 pad_maximum_fusion
  12.9 3.3 copy.63.x_ref
  16.2 6.2 %all-gather = bf16[4,40,12]{1,2,0:T(8,128)(2,1)S(1)} all-gather(bf16[1,40,12]{1,2,0:T(8,128)(2,1)S(1)} %bitcast.31), channel_id=1, replica_groups=mesh['dp'=8,'fsdp'=4] {'fsdp'}, dimensions={0}, use_global_device_ids=true | all-gather | bytes 4800 | tf_op jit(solution)/shard_map/all_gather | solution.py:986
  22.5 8.1 %copy.62.box_ref = s32[2,1,2,709,709]{4,3,2,1,0:T(8,128)} copy(s32[2,1,2,709,709]{4,2,3,1,0:T(2,128)} %param.17) | data formatting | bytes 16085792 | tf_op args[3]
  30.6 2.3 copy.61.pos_ref
  33.1 1.6 copy.64.cot_ref
  35.4 69.5 %bias_rows.1.bias_ref = f32[2,12,768,768]{3,2,1,0:T(8,128)} custom-call(s32[2]{0:T(128)} %bitcast.32, f32[24,128]{1,0:T(8,128)} %pad_maximum_fusion.4.tab_ref, s32[2,1,709,709]{3,2,1,0:T(8,128)} %copy.61.pos_ref, s32[2,1,2,709,709]{4,3,2,1,0:T(8,128)} %copy.62.box_ref), custom_call_target="tpu_custom_call" | custom-call | flops 36193032 | bytes 70778880 | tf_op jit(solution)/shard_map/bias_rows/pallas_call | solution.py:97
  104.9 1.0 slice_convert_fusion
  106.8 0.9 reshape.63.upb_ref
  107.7 10.0 %project.1 = (bf16[2,768,2304]{2,1,0:T(8,128)(2,1)}, bf16[768,1536]{1,0:T(8,128)(2,1)}) custom-call(bf16[2,1,709,768]{3,2,1,0:T(8,128)(2,1)} %copy.63.x_ref, bf16[768,6272]{1,0:T(8,128)(2,1)} %all-gather.4.cloned.1.call-done.w_ref.wo_ref.wu_ref, f32[8,768]{1,0:T(8,128)} %copy.59.vec_ref), custom_call_target="tpu_custom_call" | custom-call | tf_op jit(solution)/shard_map/project/pallas_call | solution.py:132
  117.7 41.4 %attend.1 = (bf16[2,12,768,768]{3,2,1,0:T(8,128)(2,1)}, bf16[2,768,768]{2,1,0:T(8,128)(2,1)}, bf16[768,1536]{1,0:T(8,128)(2,1)}) custom-call(bf16[2,768,2304]{2,1,0:T(8,128)(2,1)} %get-tuple-element.31.q_ref.k_ref.v_ref, bf16[2,768,2304]{2,1,0:T(8,128)(2,1)} %get-tuple-element.31.q_ref.k_ref.v_ref, ...), custom_call_target="tpu_custom_call" | custom-call | tf_op jit(solution)/shard_map/attend/pallas_call | solution.py:178
  159.1 3.9 all-gather.6.cloned.1.call-done.wd_ref
  163.0 51.9 %dense.1 = (bf16[2,1,709,768]{3,2,1,0:T(8,128)(2,1)}, f32[2,768,768]{2,1,0:T(8,128)}, bf16[3840,1536]{1,0:T(8,128)(2,1)}, bf16[2,768,3072]{2,1,0:T(8,128)(2,1)},...) custom-call(bf16[2,1,709,768]{3,2,1,0:T(8,128)(2,1)} %copy.63.x_ref,, ...), custom_call_target="tpu_custom_call" | custom-call | tf_op jit(solution)/shard_map/dense/pallas_call | solution.py:286
  214.8 22.3 %weight_grads.1 = bf16[32,24,6912]{2,1,0:T(8,128)(2,1)} custom-call(bf16[3840,1536]{1,0:T(8,128)(2,1)} %get-tuple-element.45.l_ref, bf16[1536,3072]{1,0:T(8,128)(2,1)} %bitcast.33, bf16[768,1536]{1,0:T(8,128)(2,1)} %get-tuple-element.47.a_ref, bf16[1536,768]{1,0:T(8,128)(2,1)} %bitcast.35, bf16[1536,768]{1,0:T(8,128)(2,1)} %bitcast.34), custom_call_target="tpu_custom_call" | custom-call | flops 16307453952 | bytes 28311552 | tf_op jit(solution)/shard_map/weight_grads/pallas_call | solution.py:570
  237.9 141.2 %attend_back.1 = (bf16[2,768,2304]{2,1,0:T(8,128)(2,1)}, f32[64,128]{1,0:T(8,128)}, f32[8,2304]{1,0:T(8,128)}) custom-call(bf16[2,768,2304]{2,1,0:T(8,128)(2,1)} %get-tuple-element.31.q_ref.k_ref.v_ref, bf16[2,768,2304]{2,1,0:T(8,128)(2,1)} %get-tuple-element.31.q_ref.k_ref.v_ref, bf16[2,768,2304]{2,1,0:T(8,128)(2,1)} %get-tuple-element.31.q_ref.k_ref.v_ref, ...), custom_call_target="tpu_custom_call" | custom-call | tf_op jit(solution)/shard_map/attend_back/pallas_call | solution.py:438
  379.2 0.8 fusion.9
  381.4 1.4 pad_maximum_fusion.2.small_ref
  382.8 38.1 %tail.1 = (f32[24,2304]{1,0:T(8,128)}, f32[88,128]{1,0:T(8,128)}, f32[2,709,1,768]{3,2,1,0:T(1,128)}) custom-call(bf16[768,6272]{1,0:T(8,128)(2,1)} %all-gather.4.cloned.1.call-done.w_ref.wo_ref.wu_ref, bf16[768,1536]{1,0:T(8,128)(2,1)} %get-tuple-element.34.tok_ref, bf16[1536,2304]{1,0:T(8,128)(2,1)} %bitcast.22, f32[2,768,768]{2,1,0:T(8,128)} %get-tuple-element.38.one_ref, ...), custom_call_target="tpu_custom_call" | custom-call | tf_op jit(solution)/shard_map/tail/pallas_call | solution.py:890
  421.0 133.1 %handed_on.1 = f32[2,709,1,768]{3,2,1,0:T(1,128)} custom-call(f32[2,709,1,768]{3,2,1,0:T(1,128)} %get-tuple-element.43.in_ref), custom_call_target="tpu_custom_call" | custom-call | tf_op jit(solution)/shard_map/handed_on/pallas_call | solution.py:927
  554.9 3.0 copy.69
  560.0 1.5 fusion.8
  562.2 1.6 slice.134
  (64 shorter events, 10.7 us)
Async XLA Ops:
  7.2 9.0 %copy-start.6 = (bf16[40,12]{0,1:T(8,128)(2,1)S(1)}, bf16[40,12]{0,1:T(8,128)(2,1)}, u32[]{:S(2)}) copy-start(bf16[40,12]{0,1:T(8,128)(2,1)} %param.26) | copy-start | bytes 2884
  7.2 97.8 %all-gather.4.cloned.1.call-start = ((), (), s32[]{:S(2)}) async-start(), calls=%async_computation.1 | async-start | bytes 9934848 | tf_op jit(solution)/shard_map/all_gather | solution.py:992
  12.1 150.9 %all-gather.6.cloned.1.call-start = ((), (), s32[]{:S(2)}) async-start(), calls=%async_computation.2 | async-start | bytes 4866048 | tf_op jit(solution)/shard_map/all_gather | solution.py:995
  12.9 547.1 %reduce-scatter.2.cloned.1.call-start = ((), (), s32[]{:S(2)}) async-start(), calls=%async_computation.3 | async-start | bytes 10948608 | tf_op jit(solution)/shard_map/reduce_scatter | solution.py:1004
  12.9 17.7 %slice-start = ((s8[4356096]{0:T(1024)(128)(4,1)}), s8[161792]{0:T(1024)(128)(4,1)S(1)}, s32[]{:S(2)}) async-start(s8[4356096]{0:T(1024)(128)(4,1)} %bitcast.24), calls=%async_computation.4 | async-start | bytes 323584
  22.5 8.1 %slice-start.1 = ((s8[4356096]{0:T(1024)(128)(4,1)}), s8[4194304]{0:T(1024)(128)(4,1)S(1)}, s32[]{:S(2)}) async-start(s8[4356096]{0:T(1024)(128)(4,1)} %bitcast.24), calls=%async_computation.5 | async-start | bytes 8388608
  30.6 2.5 copy-start.1
  33.1 1.6 copy-start.7
  237.2 0.7 copy-start.4
  237.9 142.8 %copy-start.5 = (f32[1,3072]{1,0:T(1,128)S(1)}, f32[1,3072]{1,0:T(1,128)}, u32[]{:S(2)}) copy-start(f32[1,3072]{1,0:T(1,128)} %get-tuple-element.41) | copy-start | bytes 36868
  420.9 133.2 %copy-start.3 = (f32[88,128]{1,0:T(8,128)S(1)}, f32[88,128]{1,0:T(8,128)}, u32[]{:S(2)}) copy-start(f32[88,128]{1,0:T(8,128)} %get-tuple-element.50) | copy-start | bytes 135172
  421.0 133.9 %copy-start = (bf16[2,1,709,768]{3,2,1,0:T(8,128)(2,1)S(1)}, bf16[2,1,709,768]{3,2,1,0:T(8,128)(2,1)}, u32[]{:S(2)}) copy-start(bf16[2,1,709,768]{3,2,1,0:T(8,128)(2,1)} %get-tuple-element.73) | copy-start | bytes 6534148
  554.1 9.7 %copy-start.2 = (f32[24,2304]{1,0:T(8,128)S(1)}, f32[24,2304]{1,0:T(8,128)}, u32[]{:S(2)}) copy-start(f32[24,2304]{1,0:T(8,128)} %get-tuple-element.114) | copy-start | bytes 663556
Sparse Core Ops, SparseCore 0:
  12.2 85.5 all-gather.3
  100.7 62.2 all-gather.5
  237.3 140.6 reduce-scatter.1

commit v7 on v6

--- a/solution.py
+++ b/solution.py
@@ -361,7 +361,7 @@
             dv_ref[lines, :] += dot(turned_g[part, :], low)
         dm_ref[0, own, cols] = (total * SCALE).astype(BF16)
 
-    group = 64
+    group = 32
     low_bins = lax.broadcasted_iota(jnp.int32, (HALF, LANES), 0).astype(BF16)
 
     def hits(picks, bins):
@@ -905,23 +905,28 @@
 
 
 def handed_on(rows_out):
-    docs, pieces = rows_out.shape[0], 4
-
-    def kernel(in_ref, out_ref, sems):
-        copies = []
+    docs, count, unused, width = rows_out.shape
+    pieces = 4
+    edges = [count * piece // pieces for piece in range(pieces + 1)]
+
+    def kernel(in_ref, out_ref, held_ref, in_sems, out_sems):
+        arrivals, departures = [], []
         for doc in range(docs):
-            count = rows_out.shape[1]
-            edges = [count * piece // pieces for piece in range(pieces + 1)]
             for piece in range(pieces):
                 at = pl.ds(edges[piece], edges[piece + 1] - edges[piece])
-                copies.append(
-                    pltpu.make_async_copy(
-                        in_ref.at[doc, at], out_ref.at[doc, at], sems.at[doc, piece]
-                    )
+                held = held_ref.at[doc, at]
+                arrivals.append(
+                    pltpu.make_async_copy(in_ref.at[doc, at], held, in_sems.at[doc, piece])
                 )
-        for copy in copies:
+                departures.append(
+                    pltpu.make_async_copy(held, out_ref.at[doc, at], out_sems.at[doc, piece])
+                )
+        for copy in arrivals:
             copy.start()
-        for copy in copies:
+        for arrival, departure in zip(arrivals, departures):
+            arrival.wait()
+            departure.start()
+        for copy in departures:
             copy.wait()
 
     return pl.pallas_call(
@@ -929,7 +934,12 @@
         out_shape=jax.ShapeDtypeStruct(rows_out.shape, rows_out.dtype),
         in_specs=[pl.BlockSpec(memory_space=pl.ANY)],
         out_specs=pl.BlockSpec(memory_space=pl.ANY),
-        scratch_shapes=[pltpu.SemaphoreType.DMA((docs, pieces))],
+        scratch_shapes=[
+            pltpu.VMEM(rows_out.shape, rows_out.dtype),
+            pltpu.SemaphoreType.DMA((docs, pieces)),
+            pltpu.SemaphoreType.DMA((docs, pieces)),
+        ],
+        compiler_params=pltpu.CompilerParams(vmem_limit_bytes=VMEM_LIMIT),
         name="handed_on",
     )(rows_out)
 

time: 579 us -> 443 us (0.77)
  Pallas kernels: 508 us -> 371 us
    pallas_call x1, Pallas kernels: 133 us -> 3.9 us  [handed_on(): pl.pallas_call(kernel, out_shape=jax.ShapeDtypeStruct(rows_out.shape, row...]
    pallas_call x1, Pallas kernels: 141 us -> 134 us  [attend_back(): pl.pallas_call(partial(attend_back_kernel, rows), out_shape=(jax.ShapeDty...]
  transfers between devices with their start and end apart: 3 -> 3, of which waited for: 1 -> 1; matrix products, arithmetic and copies ran while one was open for 5% -> 6% of each run, Pallas kernels for 76% -> 68%
where the time goes in v7:
time: 443 us; the launch traced here: 435 us
  Pallas kernels  371 us (84%)
  local copies, waits for them, and re-layouts  31.4 us (7%)
  between operations  14.3 us (3%)
  other arithmetic  7.13 us (2%)
  blocking collectives  6.2 us (1%)
  waiting for transfers between devices  4.6 us (1%)
    pallas_call x1, Pallas kernels, attend_back(): pl.pallas_call(partial(attend_back_kernel, rows), out_shape=(jax.ShapeDty...  134 us
    pallas_call x1, Pallas kernels, bias_rows(): pl.pallas_call(partial(bias_kernel, rows), out_shape=jax.ShapeDtypeStruct...  69.5 us
    pallas_call x1, Pallas kernels, dense(): pl.pallas_call(partial(dense_kernel, rows), out_shape=(jax.ShapeDtypeStru...  52.1 us
    pallas_call x1, Pallas kernels, attend(): pl.pallas_call(attend_kernel, out_shape=(jax.ShapeDtypeStruct((docs, head...  41.4 us
    pallas_call x1, Pallas kernels, tail(): pl.pallas_call(partial(tail_kernel, dims), out_shape=(jax.ShapeDtypeStruc...  37.9 us
    pallas_call x1, Pallas kernels, weight_grads(): pl.pallas_call(kernel, out_shape=jax.ShapeDtypeStruct((devices, own, (1 +...  22.3 us
    unnamed x29, local copies, waits for them, and re-layouts  22.2 us
    pallas_call x1, Pallas kernels, project(): pl.pallas_call(partial(project_kernel, rows), out_shape=(jax.ShapeDtypeSt...  9.97 us
  transfers between devices with their start and end apart: 3, of which 1 were waited for; matrix products, arithmetic and copies ran while one was open for 6% of the time, Pallas kernels for 68%

profile of v7, /device:TPU:0, one launch (start us, length us, event | category | flops | bytes accessed | tf_op | source)
XLA Modules:
  0.0 434.8 jit_solution(11188683295911149656)
XLA Ops:
  8.7 0.8 copy.57
  9.5 0.7 reshape.62
  10.3 1.7 pad_maximum_fusion
  12.9 3.3 copy.63.x_ref
  16.2 6.2 %all-gather = bf16[4,40,12]{1,2,0:T(8,128)(2,1)S(1)} all-gather(bf16[1,40,12]{1,2,0:T(8,128)(2,1)S(1)} %bitcast.31), channel_id=1, replica_groups=mesh['dp'=8,'fsdp'=4] {'fsdp'}, dimensions={0}, use_global_device_ids=true | all-gather | bytes 4800 | tf_op jit(solution)/shard_map/all_gather | solution.py:996
  22.5 8.1 %copy.62.box_ref = s32[2,1,2,709,709]{4,3,2,1,0:T(8,128)} copy(s32[2,1,2,709,709]{4,2,3,1,0:T(2,128)} %param.17) | data formatting | bytes 16085792 | tf_op args[3]
  30.6 2.3 copy.61.pos_ref
  33.1 1.6 copy.64.cot_ref
  35.4 69.5 %bias_rows.1.bias_ref = f32[2,12,768,768]{3,2,1,0:T(8,128)} custom-call(s32[2]{0:T(128)} %bitcast.32, f32[24,128]{1,0:T(8,128)} %pad_maximum_fusion.4.tab_ref, s32[2,1,709,709]{3,2,1,0:T(8,128)} %copy.61.pos_ref, s32[2,1,2,709,709]{4,3,2,1,0:T(8,128)} %copy.62.box_ref), custom_call_target="tpu_custom_call" | custom-call | flops 36193032 | bytes 70778880 | tf_op jit(solution)/shard_map/bias_rows/pallas_call | solution.py:97
  104.9 1.0 slice_convert_fusion
  106.8 0.9 reshape.63.upb_ref
  107.7 10.0 %project.1 = (bf16[2,768,2304]{2,1,0:T(8,128)(2,1)}, bf16[768,1536]{1,0:T(8,128)(2,1)}) custom-call(bf16[2,1,709,768]{3,2,1,0:T(8,128)(2,1)} %copy.63.x_ref, bf16[768,6272]{1,0:T(8,128)(2,1)} %all-gather.4.cloned.1.call-done.w_ref.wo_ref.wu_ref, f32[8,768]{1,0:T(8,128)} %copy.59.vec_ref), custom_call_target="tpu_custom_call" | custom-call | tf_op jit(solution)/shard_map/project/pallas_call | solution.py:132
  117.7 41.4 %attend.1 = (bf16[2,12,768,768]{3,2,1,0:T(8,128)(2,1)}, bf16[2,768,768]{2,1,0:T(8,128)(2,1)}, bf16[768,1536]{1,0:T(8,128)(2,1)}) custom-call(bf16[2,768,2304]{2,1,0:T(8,128)(2,1)} %get-tuple-element.31.q_ref.k_ref.v_ref, bf16[2,768,2304]{2,1,0:T(8,128)(2,1)} %get-tuple-element.31.q_ref.k_ref.v_ref, ...), custom_call_target="tpu_custom_call" | custom-call | tf_op jit(solution)/shard_map/attend/pallas_call | solution.py:178
  159.1 3.9 all-gather.6.cloned.1.call-done.wd_ref
  163.0 52.1 %dense.1 = (bf16[2,1,709,768]{3,2,1,0:T(8,128)(2,1)}, f32[2,768,768]{2,1,0:T(8,128)}, bf16[3840,1536]{1,0:T(8,128)(2,1)}, bf16[2,768,3072]{2,1,0:T(8,128)(2,1)},...) custom-call(bf16[2,1,709,768]{3,2,1,0:T(8,128)(2,1)} %copy.63.x_ref,, ...), custom_call_target="tpu_custom_call" | custom-call | tf_op jit(solution)/shard_map/dense/pallas_call | solution.py:286
  215.0 22.3 %weight_grads.1 = bf16[32,24,6912]{2,1,0:T(8,128)(2,1)} custom-call(bf16[3840,1536]{1,0:T(8,128)(2,1)} %get-tuple-element.45.l_ref, bf16[1536,3072]{1,0:T(8,128)(2,1)} %bitcast.33, bf16[768,1536]{1,0:T(8,128)(2,1)} %get-tuple-element.47.a_ref, bf16[1536,768]{1,0:T(8,128)(2,1)} %bitcast.35, bf16[1536,768]{1,0:T(8,128)(2,1)} %bitcast.34), custom_call_target="tpu_custom_call" | custom-call | flops 16307453952 | bytes 28311552 | tf_op jit(solution)/shard_map/weight_grads/pallas_call | solution.py:570
  238.1 133.9 %attend_back.1 = (bf16[2,768,2304]{2,1,0:T(8,128)(2,1)}, f32[64,128]{1,0:T(8,128)}, f32[8,2304]{1,0:T(8,128)}) custom-call(bf16[2,768,2304]{2,1,0:T(8,128)(2,1)} %get-tuple-element.31.q_ref.k_ref.v_ref, bf16[2,768,2304]{2,1,0:T(8,128)(2,1)} %get-tuple-element.31.q_ref.k_ref.v_ref, bf16[2,768,2304]{2,1,0:T(8,128)(2,1)} %get-tuple-element.31.q_ref.k_ref.v_ref, ...), custom_call_target="tpu_custom_call" | custom-call | tf_op jit(solution)/shard_map/attend_back/pallas_call | solution.py:438
  372.0 0.8 fusion.9
  374.3 1.4 pad_maximum_fusion.2.small_ref
  375.7 37.9 %tail.1 = (f32[24,2304]{1,0:T(8,128)}, f32[88,128]{1,0:T(8,128)}, f32[2,709,1,768]{3,2,1,0:T(1,128)}) custom-call(bf16[768,6272]{1,0:T(8,128)(2,1)} %all-gather.4.cloned.1.call-done.w_ref.wo_ref.wu_ref, bf16[768,1536]{1,0:T(8,128)(2,1)} %get-tuple-element.34.tok_ref, bf16[1536,2304]{1,0:T(8,128)(2,1)} %bitcast.22, f32[2,768,768]{2,1,0:T(8,128)} %get-tuple-element.38.one_ref, ...), custom_call_target="tpu_custom_call" | custom-call | tf_op jit(solution)/shard_map/tail/pallas_call | solution.py:890
  413.6 3.9 handed_on.1
  418.3 3.0 copy.69
  423.4 1.5 fusion.8
  425.6 1.6 slice.134
  (64 shorter events, 10.7 us)
Async XLA Ops:
  7.2 9.0 %copy-start.6 = (bf16[40,12]{0,1:T(8,128)(2,1)S(1)}, bf16[40,12]{0,1:T(8,128)(2,1)}, u32[]{:S(2)}) copy-start(bf16[40,12]{0,1:T(8,128)(2,1)} %param.26) | copy-start | bytes 2884
  7.2 97.8 %all-gather.4.cloned.1.call-start = ((), (), s32[]{:S(2)}) async-start(), calls=%async_computation.1 | async-start | bytes 9934848 | tf_op jit(solution)/shard_map/all_gather | solution.py:1002
  12.1 150.9 %all-gather.6.cloned.1.call-start = ((), (), s32[]{:S(2)}) async-start(), calls=%async_computation.2 | async-start | bytes 4866048 | tf_op jit(solution)/shard_map/all_gather | solution.py:1005
  12.9 410.5 %reduce-scatter.2.cloned.1.call-start = ((), (), s32[]{:S(2)}) async-start(), calls=%async_computation.3 | async-start | bytes 10948608 | tf_op jit(solution)/shard_map/reduce_scatter | solution.py:1014
  12.9 17.7 %slice-start = ((s8[4356096]{0:T(1024)(128)(4,1)}), s8[161792]{0:T(1024)(128)(4,1)S(1)}, s32[]{:S(2)}) async-start(s8[4356096]{0:T(1024)(128)(4,1)} %bitcast.24), calls=%async_computation.4 | async-start | bytes 323584
  22.5 8.1 %slice-start.1 = ((s8[4356096]{0:T(1024)(128)(4,1)}), s8[4194304]{0:T(1024)(128)(4,1)S(1)}, s32[]{:S(2)}) async-start(s8[4356096]{0:T(1024)(128)(4,1)} %bitcast.24), calls=%async_computation.5 | async-start | bytes 8388608
  30.6 2.5 copy-start.1
  33.1 1.6 copy-start.7
  237.3 0.7 copy-start.4
  238.1 135.4 %copy-start.5 = (f32[1,3072]{1,0:T(1,128)S(1)}, f32[1,3072]{1,0:T(1,128)}, u32[]{:S(2)}) copy-start(f32[1,3072]{1,0:T(1,128)} %get-tuple-element.41) | copy-start | bytes 36868
  413.6 3.9 copy-start.3
  413.6 4.7 %copy-start = (bf16[2,1,709,768]{3,2,1,0:T(8,128)(2,1)S(1)}, bf16[2,1,709,768]{3,2,1,0:T(8,128)(2,1)}, u32[]{:S(2)}) copy-start(bf16[2,1,709,768]{3,2,1,0:T(8,128)(2,1)} %get-tuple-element.73) | copy-start | bytes 6534148
  417.5 9.7 %copy-start.2 = (f32[24,2304]{1,0:T(8,128)S(1)}, f32[24,2304]{1,0:T(8,128)}, u32[]{:S(2)}) copy-start(f32[24,2304]{1,0:T(8,128)} %get-tuple-element.114) | copy-start | bytes 663556
Sparse Core Ops, SparseCore 0:
  12.2 85.5 all-gather.3
  100.7 62.2 all-gather.5
  237.5 140.7 reduce-scatter.1

commit v8 on v7

--- a/solution.py
+++ b/solution.py
@@ -315,7 +315,7 @@
 
 
 def attend_back_kernel(
-    rows, q_ref, k_ref, v_ref, probs_ref, do_ref, pos_ref, box_ref, dm_ref, bins_ref, line_ref,
+    rows, q_ref, k_ref, v_ref, probs_ref, do_ref, o_ref, pos_ref, box_ref, dm_ref, bins_ref, line_ref,
     dk_ref, dv_ref, ds_ref, acc_ref, picks_ref,
 ):
     block, width = pl.program_id(1), q_ref.shape[2]
@@ -339,6 +339,7 @@
         queries, key_rows, values = q_ref[0, :, cols], k_ref[0, :, cols], v_ref[0, :, cols]
         grads = do_ref[0, :, cols]
         turned_q, turned_g = queries.T, grads.T
+        shared = grads.astype(F32) * o_ref[0, :, cols].astype(F32)
         total = None
         for half in range(2):
             head = 2 * pair + half
@@ -348,7 +349,7 @@
             low = probs_ref[0, head]
             probs = low.astype(F32)
             dprobs = dot_nt(jnp.where(keep, grads, BF16(0)), values)
-            delta = jnp.sum(probs * dprobs, axis=-1, keepdims=True)
+            delta = jnp.sum(jnp.where(keep, shared, 0.0), axis=-1, keepdims=True)
             dscore = probs * (dprobs - delta)
             for chunk in range(padded // LANES):
                 ds_ref[chunk, pl.ds(head, BLOCK, stride=16), :] = dscore[
@@ -432,7 +433,7 @@
         line_ref[...] += dot(jnp.ones((16, padded), BF16), dm_ref[0])[0:8]
 
 
-def attend_back(qkv, probs, d_attended, pos_buckets, box_buckets):
+def attend_back(qkv, probs, d_attended, attended, pos_buckets, box_buckets):
     docs, padded, width = qkv.shape[0], qkv.shape[1], qkv.shape[2] // 3
     heads, rows = probs.shape[1], pos_buckets.shape[2]
     return pl.pallas_call(
@@ -448,6 +449,7 @@
             pl.BlockSpec((1, padded, width), lambda d, i: (d, 0, 1)),
             pl.BlockSpec((1, padded, width), lambda d, i: (d, 0, 2)),
             pl.BlockSpec((1, heads, BLOCK, padded), lambda d, i: (d, 0, i, 0)),
+            pl.BlockSpec((1, BLOCK, width), lambda d, i: (d, i, 0)),
             pl.BlockSpec((1, BLOCK, width), lambda d, i: (d, i, 0)),
             pl.BlockSpec((1, 1, BLOCK, padded), lambda d, i: (d, 0, i, 0)),
             pl.BlockSpec((1, 1, 2, BLOCK, padded), lambda d, i: (d, 0, 0, i, 0)),
@@ -466,7 +468,7 @@
         ],
         compiler_params=params(2),
         name="attend_back",
-    )(qkv, qkv, qkv, probs, d_attended, pos_buckets, box_buckets)
+    )(qkv, qkv, qkv, probs, d_attended, attended, pos_buckets, box_buckets)
 
 
 def table_entries(table):
@@ -978,7 +980,7 @@
     d_weights = weight_grads(
         turned, flat(d_branch), left, flat(d_upper), flat(d_ffn), dims[0] * dims[1] * dims[2] * dims[3]
     )
-    d_mixed, bins, line = attend_back(qkv, probs, d_attended, pos_buckets, box_buckets)
+    d_mixed, bins, line = attend_back(qkv, probs, d_attended, attended, pos_buckets, box_buckets)
     sums = jnp.concatenate(
         [sums[:4], line[:1, :width], line[:1, 2 * width :], sums[6:]], axis=0
     )
@@ -996,7 +998,11 @@
     table = lax.all_gather(rel_tables, "fsdp", axis=0, tiled=True)
     heads = table.shape[1]
     small = jnp.concatenate(
-        [norm_gains.T, norm_shifts.T, proj_biases.T, up_bias.reshape(own, hidden // width)], axis=1
+        [
+            jnp.concatenate([norm_gains, norm_shifts, proj_biases], axis=0).T,
+            up_bias.reshape(own, hidden // width),
+        ],
+        axis=1,
     )
     small = jnp.pad(small, ((0, 0), (0, LANES - small.shape[1])))
     w_mixed = lax.all_gather(

time: 443 us -> 428 us (0.966)
  Pallas kernels: 371 us -> 357 us
    pallas_call x1, Pallas kernels: 134 us -> 120 us  [attend_back(): pl.pallas_call(partial(attend_back_kernel, rows), out_shape=(jax.ShapeDty...]
    unnamed x29 -> x26, local copies, waits for them, and re-layouts: 22.2 us -> 20 us
  transfers between devices with their start and end apart: 3 -> 3, of which waited for: 1 -> 1; matrix products, arithmetic and copies ran while one was open for 6% -> 7% of each run, Pallas kernels for 68% -> 67%
where the time goes in v8:
time: 428 us; the launch traced here: 420 us
  Pallas kernels  357 us (83%)
  local copies, waits for them, and re-layouts  29.4 us (7%)
  between operations  14.2 us (3%)
  other arithmetic  7.84 us (2%)
  blocking collectives  6.2 us (1%)
  waiting for transfers between devices  4.94 us (1%)
    pallas_call x1, Pallas kernels, attend_back(): pl.pallas_call(partial(attend_back_kernel, rows), out_shape=(jax.ShapeDty...  120 us
    pallas_call x1, Pallas kernels, bias_rows(): pl.pallas_call(partial(bias_kernel, rows), out_shape=jax.ShapeDtypeStruct...  69.5 us
    pallas_call x1, Pallas kernels, dense(): pl.pallas_call(partial(dense_kernel, rows), out_shape=(jax.ShapeDtypeStru...  51.8 us
    pallas_call x1, Pallas kernels, attend(): pl.pallas_call(attend_kernel, out_shape=(jax.ShapeDtypeStruct((docs, head...  41.5 us
    pallas_call x1, Pallas kernels, tail(): pl.pallas_call(partial(tail_kernel, dims), out_shape=(jax.ShapeDtypeStruc...  38 us
    pallas_call x1, Pallas kernels, weight_grads(): pl.pallas_call(kernel, out_shape=jax.ShapeDtypeStruct((devices, own, (1 +...  22.7 us
    unnamed x26, local copies, waits for them, and re-layouts  20 us
    pallas_call x1, Pallas kernels, project(): pl.pallas_call(partial(project_kernel, rows), out_shape=(jax.ShapeDtypeSt...  10 us
  transfers between devices with their start and end apart: 3, of which 1 were waited for; matrix products, arithmetic and copies ran while one was open for 7% of the time, Pallas kernels for 67%

profile of v8, /device:TPU:0, one launch (start us, length us, event | category | flops | bytes accessed | tf_op | source)
XLA Modules:
  0.0 420.0 jit_solution(1372716765297845596)
XLA Ops:
  8.0 0.8 reshape.62
  8.9 1.7 pad_maximum_fusion
  11.4 3.3 copy.61.x_ref
  14.7 6.2 %all-gather = bf16[4,40,12]{1,2,0:T(8,128)(2,1)S(1)} all-gather(bf16[1,40,12]{1,2,0:T(8,128)(2,1)S(1)} %bitcast.27), channel_id=1, replica_groups=mesh['dp'=8,'fsdp'=4] {'fsdp'}, dimensions={0}, use_global_device_ids=true | all-gather | bytes 4800 | tf_op jit(solution)/shard_map/all_gather | solution.py:998
  21.0 8.2 %copy.60.box_ref = s32[2,1,2,709,709]{4,3,2,1,0:T(8,128)} copy(s32[2,1,2,709,709]{4,2,3,1,0:T(2,128)} %param.17) | data formatting | bytes 16085792 | tf_op args[3]
  29.2 2.3 copy.59.pos_ref
  31.7 1.6 copy.62.cot_ref
  34.0 69.5 %bias_rows.1.bias_ref = f32[2,12,768,768]{3,2,1,0:T(8,128)} custom-call(s32[2]{0:T(128)} %bitcast.28, f32[24,128]{1,0:T(8,128)} %pad_maximum_fusion.4.tab_ref, s32[2,1,709,709]{3,2,1,0:T(8,128)} %copy.59.pos_ref, s32[2,1,2,709,709]{4,3,2,1,0:T(8,128)} %copy.60.box_ref), custom_call_target="tpu_custom_call" | custom-call | flops 36193032 | bytes 70778880 | tf_op jit(solution)/shard_map/bias_rows/pallas_call | solution.py:97
  103.6 1.0 slice_convert_fusion
  104.7 0.7 copy.57.vec_ref
  105.5 0.9 reshape.63.upb_ref
  106.3 10.0 %project.1 = (bf16[2,768,2304]{2,1,0:T(8,128)(2,1)}, bf16[768,1536]{1,0:T(8,128)(2,1)}) custom-call(bf16[2,1,709,768]{3,2,1,0:T(8,128)(2,1)} %copy.61.x_ref, bf16[768,6272]{1,0:T(8,128)(2,1)} %all-gather.4.cloned.1.call-done.w_ref.wo_ref.wu_ref, f32[8,768]{1,0:T(8,128)} %copy.57.vec_ref), custom_call_target="tpu_custom_call" | custom-call | tf_op jit(solution)/shard_map/project/pallas_call | solution.py:132
  116.3 41.5 %attend.1 = (bf16[2,12,768,768]{3,2,1,0:T(8,128)(2,1)}, bf16[2,768,768]{2,1,0:T(8,128)(2,1)}, bf16[768,1536]{1,0:T(8,128)(2,1)}) custom-call(bf16[2,768,2304]{2,1,0:T(8,128)(2,1)} %get-tuple-element.31.q_ref.k_ref.v_ref, bf16[2,768,2304]{2,1,0:T(8,128)(2,1)} %get-tuple-element.31.q_ref.k_ref.v_ref, ...), custom_call_target="tpu_custom_call" | custom-call | tf_op jit(solution)/shard_map/attend/pallas_call | solution.py:178
  157.8 4.2 %all-gather.6.cloned.1.call-done.wd_ref = bf16[3072,768]{1,0:T(8,128)(2,1)} async-done(((bf16[96,768]{1,0:T(8,128)(2,1)}), bf16[3072,768]{1,0:T(8,128)(2,1)}) %all-gather.6.cloned.1.call-update) | async-done | bytes 4718608 | tf_op jit(solution)/shard_map/all_gather | solution.py:1011
  162.1 51.8 %dense.1 = (bf16[2,1,709,768]{3,2,1,0:T(8,128)(2,1)}, f32[2,768,768]{2,1,0:T(8,128)}, bf16[3840,1536]{1,0:T(8,128)(2,1)}, bf16[2,768,3072]{2,1,0:T(8,128)(2,1)},...) custom-call(bf16[2,1,709,768]{3,2,1,0:T(8,128)(2,1)} %copy.61.x_ref,, ...), custom_call_target="tpu_custom_call" | custom-call | tf_op jit(solution)/shard_map/dense/pallas_call | solution.py:286
  213.9 22.7 %weight_grads.1 = bf16[32,24,6912]{2,1,0:T(8,128)(2,1)} custom-call(bf16[3840,1536]{1,0:T(8,128)(2,1)} %get-tuple-element.45.l_ref, bf16[1536,3072]{1,0:T(8,128)(2,1)} %bitcast.29, bf16[768,1536]{1,0:T(8,128)(2,1)} %get-tuple-element.47.a_ref, bf16[1536,768]{1,0:T(8,128)(2,1)} %bitcast.31, bf16[1536,768]{1,0:T(8,128)(2,1)} %bitcast.30), custom_call_target="tpu_custom_call" | custom-call | flops 16307453952 | bytes 28311552 | tf_op jit(solution)/shard_map/weight_grads/pallas_call | solution.py:572
  237.3 119.9 %attend_back.1 = (bf16[2,768,2304]{2,1,0:T(8,128)(2,1)}, f32[64,128]{1,0:T(8,128)}, f32[8,2304]{1,0:T(8,128)}) custom-call(bf16[2,768,2304]{2,1,0:T(8,128)(2,1)} %get-tuple-element.31.q_ref.k_ref.v_ref, bf16[2,768,2304]{2,1,0:T(8,128)(2,1)} %get-tuple-element.31.q_ref.k_ref.v_ref, bf16[2,768,2304]{2,1,0:T(8,128)(2,1)} %get-tuple-element.31.q_ref.k_ref.v_ref, ...), custom_call_target="tpu_custom_call" | custom-call | tf_op jit(solution)/shard_map/attend_back/pallas_call | solution.py:439
  357.3 0.8 fusion.5
  359.5 1.4 pad_maximum_fusion.2.small_ref
  360.9 38.0 %tail.1 = (f32[24,2304]{1,0:T(8,128)}, f32[88,128]{1,0:T(8,128)}, f32[2,709,1,768]{3,2,1,0:T(1,128)}) custom-call(bf16[768,6272]{1,0:T(8,128)(2,1)} %all-gather.4.cloned.1.call-done.w_ref.wo_ref.wu_ref, bf16[768,1536]{1,0:T(8,128)(2,1)} %get-tuple-element.34.tok_ref, bf16[1536,2304]{1,0:T(8,128)(2,1)} %bitcast.20, f32[2,768,768]{2,1,0:T(8,128)} %get-tuple-element.38.one_ref, ...), custom_call_target="tpu_custom_call" | custom-call | tf_op jit(solution)/shard_map/tail/pallas_call | solution.py:892
  398.9 3.9 handed_on.1
  403.6 3.0 copy.67
  408.7 1.5 fusion.4
  410.9 1.6 slice.134
  (63 shorter events, 9.3 us)
Async XLA Ops:
  7.2 7.6 %copy-start.6 = (bf16[40,12]{0,1:T(8,128)(2,1)S(1)}, bf16[40,12]{0,1:T(8,128)(2,1)}, u32[]{:S(2)}) copy-start(bf16[40,12]{0,1:T(8,128)(2,1)} %param.26) | copy-start | bytes 2884
  7.2 96.4 %all-gather.4.cloned.1.call-start = ((), (), s32[]{:S(2)}) async-start(), calls=%async_computation.1 | async-start | bytes 9934848 | tf_op jit(solution)/shard_map/all_gather | solution.py:1008
  10.6 151.4 %all-gather.6.cloned.1.call-start = ((), (), s32[]{:S(2)}) async-start(), calls=%async_computation.2 | async-start | bytes 4866048 | tf_op jit(solution)/shard_map/all_gather | solution.py:1011
  11.4 397.3 %reduce-scatter.2.cloned.1.call-start = ((), (), s32[]{:S(2)}) async-start(), calls=%async_computation.3 | async-start | bytes 10948608 | tf_op jit(solution)/shard_map/reduce_scatter | solution.py:1020
  11.4 17.8 %slice-start = ((s8[4356096]{0:T(1024)(128)(4,1)}), s8[161792]{0:T(1024)(128)(4,1)S(1)}, s32[]{:S(2)}) async-start(s8[4356096]{0:T(1024)(128)(4,1)} %bitcast.22), calls=%async_computation.4 | async-start | bytes 323584
  21.0 8.2 %slice-start.1 = ((s8[4356096]{0:T(1024)(128)(4,1)}), s8[4194304]{0:T(1024)(128)(4,1)S(1)}, s32[]{:S(2)}) async-start(s8[4356096]{0:T(1024)(128)(4,1)} %bitcast.22), calls=%async_computation.5 | async-start | bytes 8388608
  29.2 2.5 copy-start.1
  31.7 1.6 copy-start.7
  236.6 0.7 copy-start.4
  237.3 121.4 %copy-start.5 = (f32[1,3072]{1,0:T(1,128)S(1)}, f32[1,3072]{1,0:T(1,128)}, u32[]{:S(2)}) copy-start(f32[1,3072]{1,0:T(1,128)} %get-tuple-element.41) | copy-start | bytes 36868
  398.9 3.9 copy-start.3
  398.9 4.7 %copy-start = (bf16[2,1,709,768]{3,2,1,0:T(8,128)(2,1)S(1)}, bf16[2,1,709,768]{3,2,1,0:T(8,128)(2,1)}, u32[]{:S(2)}) copy-start(bf16[2,1,709,768]{3,2,1,0:T(8,128)(2,1)} %get-tuple-element.73) | copy-start | bytes 6534148
  402.8 9.7 %copy-start.2 = (f32[24,2304]{1,0:T(8,128)S(1)}, f32[24,2304]{1,0:T(8,128)}, u32[]{:S(2)}) copy-start(f32[24,2304]{1,0:T(8,128)} %get-tuple-element.114) | copy-start | bytes 663556
Sparse Core Ops, SparseCore 0:
  11.4 85.4 all-gather.3
  99.8 62.2 all-gather.5
  236.7 140.5 reduce-scatter.1

commit v9 on v8

--- a/solution.py
+++ b/solution.py
@@ -600,7 +600,6 @@
 
 ORDERS = ((3, 1, 2, 0), (3, 2, 1, 0)) * 3
 MATRICES = 3
-TABLE_LINES = 64
 MESH = pl.DeviceIdType.MESH
 
 
@@ -609,7 +608,8 @@
 
 
 def tail_kernel(
-    dims, w_ref, tok_ref, mixed_ref, one_ref, small_ref, grad_ref, sums_ref, input_ref, *scratch
+    dims, w_ref, tok_ref, mixed_ref, one_ref, dense_ref, up_ref, line_ref, bins_ref,
+    grad_ref, sums_ref, input_ref, *scratch
 ):
     parts, width = len(ORDERS), tok_ref.shape[0]
     cut = MATRICES * width // parts
@@ -624,7 +624,6 @@
     mine = (dp // across, dp % across, fsdp // cores, fsdp % cores)
     docs, padded = one_ref.shape[0], one_ref.shape[1]
     rows, block = input_ref.shape[1], kept.shape[1]
-    own_lines = sums_ref.shape[0] - TABLE_LINES
 
     def peer(axis, step):
         place = list(mine)
@@ -724,7 +723,14 @@
         send(part, level + 1)
 
     small_order = (3, 1, 2, 0)
-    own_bins = deep * own_lines
+    chunks = width // LANES
+    span = 8 * min(2, chunks)
+    rest = sums_ref.shape[0] - span
+
+    def window(place):
+        return pl.ds(pl.multiple_of(8 * window_start(place, width, deep), 8), span)
+
+    tail_lines = pl.ds(8 * chunks, rest)
 
     def small_send(level):
         axis, lane = small_order[level], 4 * parts + level
@@ -733,13 +739,13 @@
             return
         launch(
             lane, axis,
-            lambda place: own_sums.at[3, pl.ds(pl.multiple_of(place * own_lines, 8), own_lines)],
-            lambda slot: got_sums.at[3, slot, pl.ds(0, own_lines)],
+            lambda place: own_sums.at[3, window(place)],
+            lambda slot: got_sums.at[3, slot, pl.ds(0, span)],
         )
         launch(
             lane + 1, axis,
-            lambda place: own_sums.at[3, pl.ds(own_bins, TABLE_LINES)],
-            lambda slot: got_sums.at[3, slot, pl.ds(own_bins, TABLE_LINES)],
+            lambda place: own_sums.at[3, tail_lines],
+            lambda slot: got_sums.at[3, slot, tail_lines],
         )
 
     def small_join(level):
@@ -751,12 +757,12 @@
             small_send(level + 1)
             return
         land(lane + 1)
-        here = pl.ds(pl.multiple_of(mine[0] * own_lines, 8), own_lines)
-        sums_ref[0:own_lines] = joined(
-            own_sums[3, here], [got_sums[3, slot, 0:own_lines] for slot in slots]
+        sums_ref[0:span] = joined(
+            own_sums[3, window(mine[0])], [got_sums[3, slot, 0:span] for slot in slots]
         )
-        last = slice(own_bins, own_bins + TABLE_LINES)
-        sums_ref[own_lines:] = joined(own_sums[3, last], [got_sums[3, slot, last] for slot in slots])
+        sums_ref[span:] = joined(
+            own_sums[3, tail_lines], [got_sums[3, slot, tail_lines] for slot in slots]
+        )
 
     spans = [(doc, first) for doc in range(docs) for first in range(0, padded, block)]
 
@@ -795,7 +801,18 @@
         store(step).start()
 
     loads[0].wait()
-    own_sums[0] = small_ref[...]
+    place = lax.broadcasted_iota(jnp.int32, (8, width), 0)
+    eight = jnp.where(
+        place == 4, line_ref[:, :width],
+        jnp.where(place == 5, line_ref[:, 2 * width :], dense_ref[...]),
+    )
+    for chunk in range(chunks):
+        own_sums[0, 8 * chunk : 8 * chunk + 8] = eight[:, chunk * LANES : (chunk + 1) * LANES]
+    ups = up_ref.shape[1] // LANES
+    for chunk in range(ups):
+        at = 8 * chunks + chunk
+        own_sums[0, at : at + 1] = up_ref[:, chunk * LANES : (chunk + 1) * LANES]
+    own_sums[0, 8 * chunks + ups :] = bins_ref[...]
     small_send(0)
 
     def multiply(matrix):
@@ -848,13 +865,20 @@
     return dp // across, across, fsdp // cores, cores
 
 
-def tail(w_mixed, tok, d_mixed, d_one, small, rows, dims):
+def window_start(place, width, deep):
+    chunks = width // LANES
+    return jnp.minimum(place * (width // deep) // LANES, max(chunks - 2, 0))
+
+
+def tail(w_mixed, tok, d_mixed, d_one, sums, up_sum, line, bins, rows, dims):
     docs, padded, width = d_one.shape
     parts = len(ORDERS)
     cut = MATRICES * width // parts
     devices = dims[0] * dims[1] * dims[2] * dims[3]
     own = width // devices
-    lines = (small.shape[0] - TABLE_LINES) // dims[0] + TABLE_LINES
+    more = up_sum.shape[1] // LANES + bins.shape[0]
+    small = (8 * width // LANES + more, LANES)
+    lines = 8 * min(2, width // LANES) + more
     any_space = pl.BlockSpec(memory_space=pl.ANY)
     vmem = pl.BlockSpec(memory_space=pltpu.VMEM)
     scratch = []
@@ -881,8 +905,8 @@
         pltpu.VMEM((width, MATRICES * width), BF16),
         pltpu.VMEM((2, DENSE_BLOCK, width), F32),
         pltpu.VMEM((2, DENSE_BLOCK, 1, width), F32),
-        pltpu.VMEM((4,) + small.shape, F32),
-        pltpu.VMEM((4, most) + small.shape, F32),
+        pltpu.VMEM((4,) + small, F32),
+        pltpu.VMEM((4, most) + small, F32),
         pltpu.SemaphoreType.DMA((4 * parts + 5, most)),
         pltpu.SemaphoreType.DMA((4 * parts + 5, most)),
         pltpu.SemaphoreType.DMA((MATRICES + 2,)),
@@ -896,14 +920,14 @@
             jax.ShapeDtypeStruct((lines, LANES), F32),
             jax.ShapeDtypeStruct((docs, rows, 1, width), F32),
         ),
-        in_specs=[any_space, any_space, any_space, any_space, vmem],
+        in_specs=[any_space] * 4 + [vmem] * 4,
         out_specs=(vmem, vmem, any_space),
         scratch_shapes=scratch,
         compiler_params=pltpu.CompilerParams(
             collective_id=0, has_side_effects=True, vmem_limit_bytes=VMEM_LIMIT
         ),
         name="tail",
-    )(w_mixed, tok, d_mixed, d_one, small)
+    )(w_mixed, tok, d_mixed, d_one, sums, up_sum, line, bins)
 
 
 def handed_on(rows_out):
@@ -946,22 +970,16 @@
     )(rows_out)
 
 
-def packed_sums(sums, up_sum, bins, deep):
-    width, hidden = sums.shape[1], up_sum.shape[1]
-    sums = jnp.transpose(sums.reshape(8, deep, width // deep), (1, 0, 2)).reshape(deep, -1)
-    lines = jnp.concatenate([sums, up_sum.reshape(deep, hidden // deep)], axis=1)
-    share = pl.cdiv(lines.shape[1], 8 * LANES) * 8 * LANES
-    lines = jnp.pad(lines, ((0, 0), (0, share - lines.shape[1])))
-    return jnp.concatenate([lines.reshape(-1, LANES), bins], axis=0)
-
-
-def small_results(packed, width, hidden, heads, deep, own, rank):
-    flat = packed[:-TABLE_LINES].reshape(-1)
-    count, more = 8 * width // deep, hidden // deep
-    sums = lax.dynamic_slice_in_dim(flat[:count].reshape(8, -1), rank * own, own, 1)
+def small_results(packed, width, hidden, heads, deep, own, place):
+    span, more = 8 * min(2, width // LANES), hidden // LANES
+    sums = jnp.transpose(packed[:span].reshape(-1, 8, LANES), (1, 0, 2)).reshape(8, -1)
+    depth = place * own // (width // deep)
+    first = place * own - LANES * window_start(depth, width, deep)
+    sums = lax.dynamic_slice_in_dim(sums, first, own, 1)
     fold = hidden // width * own
-    up_sum = lax.dynamic_slice_in_dim(flat[count : count + more], rank * fold, fold, 0)
-    return sums, up_sum, table_grad(packed[-TABLE_LINES:], heads)
+    up_sum = packed[span : span + more].reshape(hidden)
+    up_sum = lax.dynamic_slice_in_dim(up_sum, place * fold, fold, 0)
+    return sums, up_sum, table_grad(packed[span + more :], heads)
 
 
 def local_step(dims, lengths, pos_buckets, box_buckets, layer_input, cotangent, w_mixed, w_down, vectors, up_row, table):
@@ -981,11 +999,7 @@
         turned, flat(d_branch), left, flat(d_upper), flat(d_ffn), dims[0] * dims[1] * dims[2] * dims[3]
     )
     d_mixed, bins, line = attend_back(qkv, probs, d_attended, attended, pos_buckets, box_buckets)
-    sums = jnp.concatenate(
-        [sums[:4], line[:1, :width], line[:1, 2 * width :], sums[6:]], axis=0
-    )
-    packed = packed_sums(sums, up_sum, bins, dims[0])
-    return result, d_weights, (w_mixed, tok, flat(d_mixed), d_one, packed, rows, dims)
+    return result, d_weights, (w_mixed, tok, flat(d_mixed), d_one, sums, up_sum, line, bins, rows, dims)
 
 
 def body(
@@ -1023,8 +1037,9 @@
     d_down = [d_weights[:, first : first + width] for first in range(width + hidden, width + 2 * hidden, width)]
     d_down = jnp.concatenate(d_down, axis=0)
     d_qkv, packed, input_grad = tail(*rest)
-    rank = lax.axis_index(axes) % (width // own // dims[0])
-    sums, up_sum, d_table = small_results(packed, width, hidden, heads, dims[0], own, rank)
+    sums, up_sum, d_table = small_results(
+        packed, width, hidden, heads, dims[0], own, lax.axis_index(axes)
+    )
     table_rows = rel_tables.shape[0]
     d_table = lax.dynamic_slice_in_dim(d_table, lax.axis_index("fsdp") * table_rows, table_rows, 0)
     return (

time: 428 us -> 423 us (0.988)
    unnamed x26 -> x22, local copies, waits for them, and re-layouts: 20 us -> 19.3 us
  transfers between devices with their start and end apart: 3 -> 3, of which waited for: 1 -> 1; matrix products, arithmetic and copies ran while one was open for 7% -> 6% of each run, Pallas kernels for 67% -> 68%
where the time goes in v9:
time: 423 us; the launch traced here: 415 us
  Pallas kernels  357 us (84%)
  local copies, waits for them, and re-layouts  27.1 us (6%)
  between operations  14.2 us (3%)
  blocking collectives  6.2 us (1%)
  other arithmetic  5.73 us (1%)
  waiting for transfers between devices  4.94 us (1%)
    pallas_call x1, Pallas kernels, attend_back(): pl.pallas_call(partial(attend_back_kernel, rows), out_shape=(jax.ShapeDty...  120 us
    pallas_call x1, Pallas kernels, bias_rows(): pl.pallas_call(partial(bias_kernel, rows), out_shape=jax.ShapeDtypeStruct...  69.5 us
    pallas_call x1, Pallas kernels, dense(): pl.pallas_call(partial(dense_kernel, rows), out_shape=(jax.ShapeDtypeStru...  51.8 us
    pallas_call x1, Pallas kernels, attend(): pl.pallas_call(attend_kernel, out_shape=(jax.ShapeDtypeStruct((docs, head...  41.5 us
    pallas_call x1, Pallas kernels, tail(): pl.pallas_call(partial(tail_kernel, dims), out_shape=(jax.ShapeDtypeStruc...  37.9 us
    pallas_call x1, Pallas kernels, weight_grads(): pl.pallas_call(kernel, out_shape=jax.ShapeDtypeStruct((devices, own, (1 +...  22.7 us
    unnamed x22, local copies, waits for them, and re-layouts  19.3 us
    pallas_call x1, Pallas kernels, project(): pl.pallas_call(partial(project_kernel, rows), out_shape=(jax.ShapeDtypeSt...  10 us
  transfers between devices with their start and end apart: 3, of which 1 were waited for; matrix products, arithmetic and copies ran while one was open for 6% of the time, Pallas kernels for 68%

profile of v9, /device:TPU:0, one launch (start us, length us, event | category | flops | bytes accessed | tf_op | source)
XLA Modules:
  0.0 415.4 jit_solution(18262716531173297234)
XLA Ops:
  7.2 0.7 pad_maximum_fusion.3
  8.0 0.8 reshape.52
  8.9 1.7 pad_maximum_fusion
  11.4 3.3 copy.59.x_ref
  14.7 6.2 %all-gather = bf16[4,40,12]{1,2,0:T(8,128)(2,1)S(1)} all-gather(bf16[1,40,12]{1,2,0:T(8,128)(2,1)S(1)} %bitcast.31), channel_id=1, replica_groups=mesh['dp'=8,'fsdp'=4] {'fsdp'}, dimensions={0}, use_global_device_ids=true | all-gather | bytes 4800 | tf_op jit(solution)/shard_map/all_gather | solution.py:1012
  21.0 8.2 %copy.58.box_ref = s32[2,1,2,709,709]{4,3,2,1,0:T(8,128)} copy(s32[2,1,2,709,709]{4,2,3,1,0:T(2,128)} %param.17) | data formatting | bytes 16085792 | tf_op args[3]
  29.2 2.3 copy.57.pos_ref
  31.7 1.6 copy.60.cot_ref
  34.0 69.5 %bias_rows.1.bias_ref = f32[2,12,768,768]{3,2,1,0:T(8,128)} custom-call(s32[2]{0:T(128)} %bitcast.32, f32[24,128]{1,0:T(8,128)} %pad_maximum_fusion.2.tab_ref, s32[2,1,709,709]{3,2,1,0:T(8,128)} %copy.57.pos_ref, s32[2,1,2,709,709]{4,3,2,1,0:T(8,128)} %copy.58.box_ref), custom_call_target="tpu_custom_call" | custom-call | flops 36193032 | bytes 70778880 | tf_op jit(solution)/shard_map/bias_rows/pallas_call | solution.py:97
  103.6 1.0 slice_convert_fusion
  104.7 0.7 copy.55.vec_ref
  105.5 0.9 reshape.53.upb_ref
  106.3 10.0 %project.1 = (bf16[2,768,2304]{2,1,0:T(8,128)(2,1)}, bf16[768,1536]{1,0:T(8,128)(2,1)}) custom-call(bf16[2,1,709,768]{3,2,1,0:T(8,128)(2,1)} %copy.59.x_ref, bf16[768,6272]{1,0:T(8,128)(2,1)} %all-gather.4.cloned.1.call-done.w_ref.wo_ref.wu_ref, f32[8,768]{1,0:T(8,128)} %copy.55.vec_ref), custom_call_target="tpu_custom_call" | custom-call | tf_op jit(solution)/shard_map/project/pallas_call | solution.py:132
  116.3 41.5 %attend.1 = (bf16[2,12,768,768]{3,2,1,0:T(8,128)(2,1)}, bf16[2,768,768]{2,1,0:T(8,128)(2,1)}, bf16[768,1536]{1,0:T(8,128)(2,1)}) custom-call(bf16[2,768,2304]{2,1,0:T(8,128)(2,1)} %get-tuple-element.31.q_ref.k_ref.v_ref, bf16[2,768,2304]{2,1,0:T(8,128)(2,1)} %get-tuple-element.31.q_ref.k_ref.v_ref, ...), custom_call_target="tpu_custom_call" | custom-call | tf_op jit(solution)/shard_map/attend/pallas_call | solution.py:178
  157.8 4.2 %all-gather.6.cloned.1.call-done.wd_ref = bf16[3072,768]{1,0:T(8,128)(2,1)} async-done(((bf16[96,768]{1,0:T(8,128)(2,1)}), bf16[3072,768]{1,0:T(8,128)(2,1)}) %all-gather.6.cloned.1.call-update) | async-done | bytes 4718608 | tf_op jit(solution)/shard_map/all_gather | solution.py:1025
  162.1 51.8 %dense.1 = (bf16[2,1,709,768]{3,2,1,0:T(8,128)(2,1)}, f32[2,768,768]{2,1,0:T(8,128)}, bf16[3840,1536]{1,0:T(8,128)(2,1)}, bf16[2,768,3072]{2,1,0:T(8,128)(2,1)},...) custom-call(bf16[2,1,709,768]{3,2,1,0:T(8,128)(2,1)} %copy.59.x_ref,, ...), custom_call_target="tpu_custom_call" | custom-call | tf_op jit(solution)/shard_map/dense/pallas_call | solution.py:286
  213.9 22.7 %weight_grads.1 = bf16[32,24,6912]{2,1,0:T(8,128)(2,1)} custom-call(bf16[3840,1536]{1,0:T(8,128)(2,1)} %get-tuple-element.45.l_ref, bf16[1536,3072]{1,0:T(8,128)(2,1)} %bitcast.33, bf16[768,1536]{1,0:T(8,128)(2,1)} %get-tuple-element.47.a_ref, bf16[1536,768]{1,0:T(8,128)(2,1)} %bitcast.35, bf16[1536,768]{1,0:T(8,128)(2,1)} %bitcast.34), custom_call_target="tpu_custom_call" | custom-call | flops 16307453952 | bytes 28311552 | tf_op jit(solution)/shard_map/weight_grads/pallas_call | solution.py:572
  236.7 119.7 %attend_back.1 = (bf16[2,768,2304]{2,1,0:T(8,128)(2,1)}, f32[64,128]{1,0:T(8,128)}, f32[8,2304]{1,0:T(8,128)}) custom-call(bf16[2,768,2304]{2,1,0:T(8,128)(2,1)} %get-tuple-element.31.q_ref.k_ref.v_ref, bf16[2,768,2304]{2,1,0:T(8,128)(2,1)} %get-tuple-element.31.q_ref.k_ref.v_ref, bf16[2,768,2304]{2,1,0:T(8,128)(2,1)} %get-tuple-element.31.q_ref.k_ref.v_ref, ...), custom_call_target="tpu_custom_call" | custom-call | tf_op jit(solution)/shard_map/attend_back/pallas_call | solution.py:439
  356.4 37.9 %tail.1 = (f32[24,2304]{1,0:T(8,128)}, f32[104,128]{1,0:T(8,128)}, f32[2,709,1,768]{3,2,1,0:T(1,128)}) custom-call(bf16[768,6272]{1,0:T(8,128)(2,1)} %all-gather.4.cloned.1.call-done.w_ref.wo_ref.wu_ref, bf16[768,1536]{1,0:T(8,128)(2,1)} %get-tuple-element.34.tok_ref, bf16[1536,2304]{1,0:T(8,128)(2,1)} %bitcast.25, ...), custom_call_target="tpu_custom_call" | custom-call | tf_op jit(solution)/shard_map/tail/pallas_call | solution.py:916
  394.3 3.9 handed_on.1
  399.0 3.0 copy.64
  404.0 1.5 fusion.4
  405.5 0.7 pad_maximum_fusion.1
  406.3 1.6 slice.110
  (45 shorter events, 5.6 us)
Async XLA Ops:
  7.2 7.6 %copy-start.4 = (bf16[40,12]{0,1:T(8,128)(2,1)S(1)}, bf16[40,12]{0,1:T(8,128)(2,1)}, u32[]{:S(2)}) copy-start(bf16[40,12]{0,1:T(8,128)(2,1)} %param.26) | copy-start | bytes 2884
  7.2 96.4 %all-gather.4.cloned.1.call-start = ((), (), s32[]{:S(2)}) async-start(), calls=%async_computation.1 | async-start | bytes 9934848 | tf_op jit(solution)/shard_map/all_gather | solution.py:1022
  10.6 151.4 %all-gather.6.cloned.1.call-start = ((), (), s32[]{:S(2)}) async-start(), calls=%async_computation.2 | async-start | bytes 4866048 | tf_op jit(solution)/shard_map/all_gather | solution.py:1025
  11.4 392.7 %reduce-scatter.2.cloned.1.call-start = ((), (), s32[]{:S(2)}) async-start(), calls=%async_computation.3 | async-start | bytes 10948608 | tf_op jit(solution)/shard_map/reduce_scatter | solution.py:1034
  11.4 17.8 %slice-start = ((s8[4356096]{0:T(1024)(128)(4,1)}), s8[161792]{0:T(1024)(128)(4,1)S(1)}, s32[]{:S(2)}) async-start(s8[4356096]{0:T(1024)(128)(4,1)} %bitcast.27), calls=%async_computation.4 | async-start | bytes 323584
  21.0 8.2 %slice-start.1 = ((s8[4356096]{0:T(1024)(128)(4,1)}), s8[4194304]{0:T(1024)(128)(4,1)S(1)}, s32[]{:S(2)}) async-start(s8[4356096]{0:T(1024)(128)(4,1)} %bitcast.27), calls=%async_computation.5 | async-start | bytes 8388608
  29.2 2.5 copy-start.1
  31.7 1.6 copy-start.5
  394.3 3.9 copy-start.3
  394.3 4.6 %copy-start = (bf16[2,1,709,768]{3,2,1,0:T(8,128)(2,1)S(1)}, bf16[2,1,709,768]{3,2,1,0:T(8,128)(2,1)}, u32[]{:S(2)}) copy-start(bf16[2,1,709,768]{3,2,1,0:T(8,128)(2,1)} %get-tuple-element.73) | copy-start | bytes 6534148
  398.3 9.7 %copy-start.2 = (f32[24,2304]{1,0:T(8,128)S(1)}, f32[24,2304]{1,0:T(8,128)}, u32[]{:S(2)}) copy-start(f32[24,2304]{1,0:T(8,128)} %get-tuple-element.112) | copy-start | bytes 663556
Sparse Core Ops, SparseCore 0:
  11.4 85.4 all-gather.3
  99.8 62.2 all-gather.5
  236.7 143.9 reduce-scatter.1

commit v10 on v9

--- a/solution.py
+++ b/solution.py
@@ -930,12 +930,17 @@
     )(w_mixed, tok, d_mixed, d_one, sums, up_sum, line, bins)
 
 
-def handed_on(rows_out):
+def handed_on(rows_out, d_weights, d_qkv):
     docs, count, unused, width = rows_out.shape
+    own, fold = d_weights.shape[0], (d_weights.shape[1] // width - 1) // 2
+    hidden = fold * width
     pieces = 4
     edges = [count * piece // pieces for piece in range(pieces + 1)]
 
-    def kernel(in_ref, out_ref, held_ref, in_sems, out_sems):
+    def kernel(
+        in_ref, w_ref, q_ref, out_ref, branch_ref, up_ref, down_ref, qkv_ref,
+        held_ref, in_sems, out_sems,
+    ):
         arrivals, departures = [], []
         for doc in range(docs):
             for piece in range(pieces):
@@ -949,17 +954,30 @@
                 )
         for copy in arrivals:
             copy.start()
+        branch_ref[...] = w_ref[:, :width].astype(F32)
+        up_ref[...] = w_ref[:, width : width + hidden].astype(F32)
         for arrival, departure in zip(arrivals, departures):
             arrival.wait()
             departure.start()
+        for part in range(fold):
+            first = width + hidden + part * width
+            down_ref[part * own : (part + 1) * own, :] = w_ref[:, first : first + width].astype(F32)
+        qkv_ref[...] = q_ref[...]
         for copy in departures:
             copy.wait()
 
+    away, near = pl.BlockSpec(memory_space=pl.ANY), pl.BlockSpec(memory_space=pltpu.VMEM)
     return pl.pallas_call(
         kernel,
-        out_shape=jax.ShapeDtypeStruct(rows_out.shape, rows_out.dtype),
-        in_specs=[pl.BlockSpec(memory_space=pl.ANY)],
-        out_specs=pl.BlockSpec(memory_space=pl.ANY),
+        out_shape=(
+            jax.ShapeDtypeStruct(rows_out.shape, rows_out.dtype),
+            jax.ShapeDtypeStruct((own, width), F32),
+            jax.ShapeDtypeStruct((own, hidden), F32),
+            jax.ShapeDtypeStruct((fold * own, width), F32),
+            jax.ShapeDtypeStruct(d_qkv.shape, F32),
+        ),
+        in_specs=[away, near, near],
+        out_specs=(away, near, near, near, near),
         scratch_shapes=[
             pltpu.VMEM(rows_out.shape, rows_out.dtype),
             pltpu.SemaphoreType.DMA((docs, pieces)),
@@ -967,7 +985,7 @@
         ],
         compiler_params=pltpu.CompilerParams(vmem_limit_bytes=VMEM_LIMIT),
         name="handed_on",
-    )(rows_out)
+    )(rows_out, d_weights, d_qkv)
 
 
 def small_results(packed, width, hidden, heads, deep, own, place):
@@ -1033,17 +1051,16 @@
     )
     d_weights = lax.psum_scatter(
         d_weights.reshape(width, -1), axes, scatter_dimension=0, tiled=True
-    ).astype(F32)
-    d_down = [d_weights[:, first : first + width] for first in range(width + hidden, width + 2 * hidden, width)]
-    d_down = jnp.concatenate(d_down, axis=0)
+    )
     d_qkv, packed, input_grad = tail(*rest)
+    input_grad, d_out, d_up, d_down, d_qkv = handed_on(input_grad, d_weights, d_qkv)
     sums, up_sum, d_table = small_results(
         packed, width, hidden, heads, dims[0], own, lax.axis_index(axes)
     )
     table_rows = rel_tables.shape[0]
     d_table = lax.dynamic_slice_in_dim(d_table, lax.axis_index("fsdp") * table_rows, table_rows, 0)
     return (
-        result, jnp.transpose(handed_on(input_grad), (0, 2, 1, 3)), d_qkv, d_weights[:, :width], d_weights[:, width : width + hidden], d_down,
+        result, jnp.transpose(input_grad, (0, 2, 1, 3)), d_qkv, d_out, d_up, d_down,
         sums[0:2], sums[2:4], sums[4:8], up_sum, d_table,
     )
 

time: 423 us -> 421 us (level)
    unnamed x22 -> x19, local copies, waits for them, and re-layouts: 19.3 us -> 18.6 us
  transfers between devices with their start and end apart: 3 -> 3, of which waited for: 1 -> 1; matrix products, arithmetic and copies ran while one was open for 6% -> 6% of each run, Pallas kernels for 68% -> 67%
where the time goes in v10:
time: 421 us; the launch traced here: 414 us
  Pallas kernels  359 us (85%)
  local copies, waits for them, and re-layouts  24 us (6%)
  between operations  14.2 us (3%)
  blocking collectives  6.2 us (1%)
  waiting for transfers between devices  5.07 us (1%)
  other arithmetic  4.99 us (1%)
    pallas_call x1, Pallas kernels, attend_back(): pl.pallas_call(partial(attend_back_kernel, rows), out_shape=(jax.ShapeDty...  120 us
    pallas_call x1, Pallas kernels, bias_rows(): pl.pallas_call(partial(bias_kernel, rows), out_shape=jax.ShapeDtypeStruct...  69.5 us
    pallas_call x1, Pallas kernels, dense(): pl.pallas_call(partial(dense_kernel, rows), out_shape=(jax.ShapeDtypeStru...  51.9 us
    pallas_call x1, Pallas kernels, attend(): pl.pallas_call(attend_kernel, out_shape=(jax.ShapeDtypeStruct((docs, head...  41.4 us
    pallas_call x1, Pallas kernels, tail(): pl.pallas_call(partial(tail_kernel, dims), out_shape=(jax.ShapeDtypeStruc...  38.1 us
    pallas_call x1, Pallas kernels, weight_grads(): pl.pallas_call(kernel, out_shape=jax.ShapeDtypeStruct((devices, own, (1 +...  22.7 us
    unnamed x19, local copies, waits for them, and re-layouts  18.6 us
    pallas_call x1, Pallas kernels, project(): pl.pallas_call(partial(project_kernel, rows), out_shape=(jax.ShapeDtypeSt...  10 us
  transfers between devices with their start and end apart: 3, of which 1 were waited for; matrix products, arithmetic and copies ran while one was open for 6% of the time, Pallas kernels for 67%

profile of v10, /device:TPU:0, one launch (start us, length us, event | category | flops | bytes accessed | tf_op | source)
XLA Modules:
  0.0 413.5 jit_solution(9284835204318482637)
XLA Ops:
  7.2 0.7 pad_maximum_fusion.2
  8.0 0.8 reshape.52
  8.9 1.7 pad_maximum_fusion
  10.7 0.7 all-gather.6.cloned.1.call-update
  11.4 3.3 copy.59.x_ref
  14.7 6.2 %all-gather = bf16[4,40,12]{1,2,0:T(8,128)(2,1)S(1)} all-gather(bf16[1,40,12]{1,2,0:T(8,128)(2,1)S(1)} %bitcast.30), channel_id=1, replica_groups=mesh['dp'=8,'fsdp'=4] {'fsdp'}, dimensions={0}, use_global_device_ids=true | all-gather | bytes 4800 | tf_op jit(solution)/shard_map/all_gather | solution.py:1030
  21.0 8.2 %copy.58.box_ref = s32[2,1,2,709,709]{4,3,2,1,0:T(8,128)} copy(s32[2,1,2,709,709]{4,2,3,1,0:T(2,128)} %param.17) | data formatting | bytes 16085792 | tf_op args[3]
  29.2 2.3 copy.57.pos_ref
  31.7 1.6 copy.60.cot_ref
  34.0 69.5 %bias_rows.1.bias_ref = f32[2,12,768,768]{3,2,1,0:T(8,128)} custom-call(s32[2]{0:T(128)} %bitcast.31, f32[24,128]{1,0:T(8,128)} %pad_maximum_fusion.1.tab_ref, s32[2,1,709,709]{3,2,1,0:T(8,128)} %copy.57.pos_ref, s32[2,1,2,709,709]{4,3,2,1,0:T(8,128)} %copy.58.box_ref), custom_call_target="tpu_custom_call" | custom-call | flops 36193032 | bytes 70778880 | tf_op jit(solution)/shard_map/bias_rows/pallas_call | solution.py:97
  103.5 1.0 slice_convert_fusion
  104.7 0.7 copy.55.vec_ref
  105.5 0.9 reshape.53.upb_ref
  106.3 10.0 %project.1 = (bf16[2,768,2304]{2,1,0:T(8,128)(2,1)}, bf16[768,1536]{1,0:T(8,128)(2,1)}) custom-call(bf16[2,1,709,768]{3,2,1,0:T(8,128)(2,1)} %copy.59.x_ref, bf16[768,6272]{1,0:T(8,128)(2,1)} %all-gather.4.cloned.1.call-done.w_ref.wo_ref.wu_ref, f32[8,768]{1,0:T(8,128)} %copy.55.vec_ref), custom_call_target="tpu_custom_call" | custom-call | tf_op jit(solution)/shard_map/project/pallas_call | solution.py:132
  116.3 41.4 %attend.1 = (bf16[2,12,768,768]{3,2,1,0:T(8,128)(2,1)}, bf16[2,768,768]{2,1,0:T(8,128)(2,1)}, bf16[768,1536]{1,0:T(8,128)(2,1)}) custom-call(bf16[2,768,2304]{2,1,0:T(8,128)(2,1)} %get-tuple-element.36.q_ref.k_ref.v_ref, bf16[2,768,2304]{2,1,0:T(8,128)(2,1)} %get-tuple-element.36.q_ref.k_ref.v_ref, ...), custom_call_target="tpu_custom_call" | custom-call | tf_op jit(solution)/shard_map/attend/pallas_call | solution.py:178
  157.7 4.3 %all-gather.6.cloned.1.call-done.wd_ref = bf16[3072,768]{1,0:T(8,128)(2,1)} async-done(((bf16[96,768]{1,0:T(8,128)(2,1)}), bf16[3072,768]{1,0:T(8,128)(2,1)}) %all-gather.6.cloned.1.call-update) | async-done | bytes 4718608 | tf_op jit(solution)/shard_map/all_gather | solution.py:1043
  162.1 51.9 %dense.1 = (bf16[2,1,709,768]{3,2,1,0:T(8,128)(2,1)}, f32[2,768,768]{2,1,0:T(8,128)}, bf16[3840,1536]{1,0:T(8,128)(2,1)}, bf16[2,768,3072]{2,1,0:T(8,128)(2,1)},...) custom-call(bf16[2,1,709,768]{3,2,1,0:T(8,128)(2,1)} %copy.59.x_ref,, ...), custom_call_target="tpu_custom_call" | custom-call | tf_op jit(solution)/shard_map/dense/pallas_call | solution.py:286
  213.9 22.7 %weight_grads.1 = bf16[32,24,6912]{2,1,0:T(8,128)(2,1)} custom-call(bf16[3840,1536]{1,0:T(8,128)(2,1)} %get-tuple-element.49.l_ref, bf16[1536,3072]{1,0:T(8,128)(2,1)} %bitcast.32, bf16[768,1536]{1,0:T(8,128)(2,1)} %get-tuple-element.51.a_ref, bf16[1536,768]{1,0:T(8,128)(2,1)} %bitcast.35, bf16[1536,768]{1,0:T(8,128)(2,1)} %bitcast.34), custom_call_target="tpu_custom_call" | custom-call | flops 16307453952 | bytes 28311552 | tf_op jit(solution)/shard_map/weight_grads/pallas_call | solution.py:572
  236.7 119.7 %attend_back.1 = (bf16[2,768,2304]{2,1,0:T(8,128)(2,1)}, f32[64,128]{1,0:T(8,128)}, f32[8,2304]{1,0:T(8,128)}) custom-call(bf16[2,768,2304]{2,1,0:T(8,128)(2,1)} %get-tuple-element.36.q_ref.k_ref.v_ref, bf16[2,768,2304]{2,1,0:T(8,128)(2,1)} %get-tuple-element.36.q_ref.k_ref.v_ref, bf16[2,768,2304]{2,1,0:T(8,128)(2,1)} %get-tuple-element.36.q_ref.k_ref.v_ref, ...), custom_call_target="tpu_custom_call" | custom-call | tf_op jit(solution)/shard_map/attend_back/pallas_call | solution.py:439
  356.4 38.1 %tail.1 = (f32[24,2304]{1,0:T(8,128)}, f32[104,128]{1,0:T(8,128)}, f32[2,709,1,768]{3,2,1,0:T(1,128)}) custom-call(bf16[768,6272]{1,0:T(8,128)(2,1)} %all-gather.4.cloned.1.call-done.w_ref.wo_ref.wu_ref, bf16[768,1536]{1,0:T(8,128)(2,1)} %get-tuple-element.39.tok_ref, bf16[1536,2304]{1,0:T(8,128)(2,1)} %bitcast.25, ...), custom_call_target="tpu_custom_call" | custom-call | tf_op jit(solution)/shard_map/tail/pallas_call | solution.py:916
  394.5 0.8 slice_bitcast_fusion.2
  395.9 3.0 copy.64
  399.8 0.7 fusion.2
  401.0 5.7 %handed_on.1 = (f32[2,709,1,768]{3,2,1,0:T(1,128)}, f32[24,768]{1,0:T(8,128)}, f32[24,3072]{1,0:T(8,128)}, f32[96,768]{1,0:T(8,128)}, f32[24,2304]{1,0:T(8,128)}) custom-call(f32[2,709,1,768]{3,2,1,0:T(1,128)} %get-tuple-element.48.in_ref, bf16[24,6912]{1,0:T(8,128)(2,1)} %reduce-scatter.2.cloned.1.call-done.w_ref, f32[24,2304]{1,0:T(8,128)} %get-tuple-element.54.q_ref), custom_call_target="tpu_custom_call" | custom-call | tf_op jit(solution)/shard_map/handed_on/pallas_call | solution.py:970
  (39 shorter events, 3.6 us)
Async XLA Ops:
  7.2 7.5 %copy-start.3 = (bf16[40,12]{0,1:T(8,128)(2,1)S(1)}, bf16[40,12]{0,1:T(8,128)(2,1)}, u32[]{:S(2)}) copy-start(bf16[40,12]{0,1:T(8,128)(2,1)} %param.26) | copy-start | bytes 2884
  7.2 96.4 %all-gather.4.cloned.1.call-start = ((), (), s32[]{:S(2)}) async-start(), calls=%async_computation.1 | async-start | bytes 9934848 | tf_op jit(solution)/shard_map/all_gather | solution.py:1040
  10.6 151.4 %all-gather.6.cloned.1.call-start = ((), (), s32[]{:S(2)}) async-start(), calls=%async_computation.2 | async-start | bytes 4866048 | tf_op jit(solution)/shard_map/all_gather | solution.py:1043
  11.4 389.6 %reduce-scatter.2.cloned.1.call-start = ((), (), s32[]{:S(2)}) async-start(), calls=%async_computation.3 | async-start | bytes 10948608 | tf_op jit(solution)/shard_map/reduce_scatter | solution.py:1052
  11.4 17.8 %slice-start = ((s8[4356096]{0:T(1024)(128)(4,1)}), s8[161792]{0:T(1024)(128)(4,1)S(1)}, s32[]{:S(2)}) async-start(s8[4356096]{0:T(1024)(128)(4,1)} %bitcast.26), calls=%async_computation.4 | async-start | bytes 323584
  21.0 8.2 %slice-start.1 = ((s8[4356096]{0:T(1024)(128)(4,1)}), s8[4194304]{0:T(1024)(128)(4,1)S(1)}, s32[]{:S(2)}) async-start(s8[4356096]{0:T(1024)(128)(4,1)} %bitcast.26), calls=%async_computation.5 | async-start | bytes 8388608
  29.2 2.5 copy-start.1
  31.7 1.6 copy-start.4
  356.4 39.5 %copy-start = (bf16[2,1,709,768]{3,2,1,0:T(8,128)(2,1)S(1)}, bf16[2,1,709,768]{3,2,1,0:T(8,128)(2,1)}, u32[]{:S(2)}) copy-start(bf16[2,1,709,768]{3,2,1,0:T(8,128)(2,1)} %get-tuple-element.83) | copy-start | bytes 6534148
  394.5 4.5 %copy-start.2 = (f32[104,128]{1,0:T(8,128)S(1)}, f32[104,128]{1,0:T(8,128)}, u32[]{:S(2)}) copy-start(f32[104,128]{1,0:T(8,128)} %get-tuple-element.60) | copy-start | bytes 159748
Sparse Core Ops, SparseCore 0:
  11.4 85.4 all-gather.3
  99.8 62.2 all-gather.5
  236.8 144.0 reduce-scatter.1

commit v11 on v10

--- a/solution.py
+++ b/solution.py
@@ -609,7 +609,7 @@
 
 def tail_kernel(
     dims, w_ref, tok_ref, mixed_ref, one_ref, dense_ref, up_ref, line_ref, bins_ref,
-    grad_ref, sums_ref, input_ref, *scratch
+    grad_ref, sums_ref, ups_ref, table_ref, input_ref, *scratch
 ):
     parts, width = len(ORDERS), tok_ref.shape[0]
     cut = MATRICES * width // parts
@@ -724,8 +724,9 @@
 
     small_order = (3, 1, 2, 0)
     chunks = width // LANES
-    span = 8 * min(2, chunks)
-    rest = sums_ref.shape[0] - span
+    span = sums_ref.shape[0]
+    ups = ups_ref.shape[0]
+    rest = ups + table_ref.shape[0]
 
     def window(place):
         return pl.ds(pl.multiple_of(8 * window_start(place, width, deep), 8), span)
@@ -757,12 +758,12 @@
             small_send(level + 1)
             return
         land(lane + 1)
-        sums_ref[0:span] = joined(
+        sums_ref[...] = joined(
             own_sums[3, window(mine[0])], [got_sums[3, slot, 0:span] for slot in slots]
         )
-        sums_ref[span:] = joined(
-            own_sums[3, tail_lines], [got_sums[3, slot, tail_lines] for slot in slots]
-        )
+        others = joined(own_sums[3, tail_lines], [got_sums[3, slot, tail_lines] for slot in slots])
+        ups_ref[...] = others[:ups]
+        table_ref[...] = others[ups:]
 
     spans = [(doc, first) for doc in range(docs) for first in range(0, padded, block)]
 
@@ -808,7 +809,6 @@
     )
     for chunk in range(chunks):
         own_sums[0, 8 * chunk : 8 * chunk + 8] = eight[:, chunk * LANES : (chunk + 1) * LANES]
-    ups = up_ref.shape[1] // LANES
     for chunk in range(ups):
         at = 8 * chunks + chunk
         own_sums[0, at : at + 1] = up_ref[:, chunk * LANES : (chunk + 1) * LANES]
@@ -917,11 +917,13 @@
         partial(tail_kernel, dims),
         out_shape=(
             jax.ShapeDtypeStruct((own, MATRICES * width), F32),
-            jax.ShapeDtypeStruct((lines, LANES), F32),
+            jax.ShapeDtypeStruct((lines - more, LANES), F32),
+            jax.ShapeDtypeStruct((more - bins.shape[0], LANES), F32),
+            jax.ShapeDtypeStruct(bins.shape, F32),
             jax.ShapeDtypeStruct((docs, rows, 1, width), F32),
         ),
         in_specs=[any_space] * 4 + [vmem] * 4,
-        out_specs=(vmem, vmem, any_space),
+        out_specs=(vmem, vmem, vmem, vmem, any_space),
         scratch_shapes=scratch,
         compiler_params=pltpu.CompilerParams(
             collective_id=0, has_side_effects=True, vmem_limit_bytes=VMEM_LIMIT
@@ -989,15 +991,14 @@
 
 
 def small_results(packed, width, hidden, heads, deep, own, place):
-    span, more = 8 * min(2, width // LANES), hidden // LANES
-    sums = jnp.transpose(packed[:span].reshape(-1, 8, LANES), (1, 0, 2)).reshape(8, -1)
+    sums = jnp.transpose(packed[0].reshape(-1, 8, LANES), (1, 0, 2)).reshape(8, -1)
     depth = place * own // (width // deep)
     first = place * own - LANES * window_start(depth, width, deep)
     sums = lax.dynamic_slice_in_dim(sums, first, own, 1)
     fold = hidden // width * own
-    up_sum = packed[span : span + more].reshape(hidden)
+    up_sum = packed[1].reshape(hidden)
     up_sum = lax.dynamic_slice_in_dim(up_sum, place * fold, fold, 0)
-    return sums, up_sum, table_grad(packed[span + more :], heads)
+    return sums, up_sum, table_grad(packed[2], heads)
 
 
 def local_step(dims, lengths, pos_buckets, box_buckets, layer_input, cotangent, w_mixed, w_down, vectors, up_row, table):
@@ -1052,7 +1053,7 @@
     d_weights = lax.psum_scatter(
         d_weights.reshape(width, -1), axes, scatter_dimension=0, tiled=True
     )
-    d_qkv, packed, input_grad = tail(*rest)
+    d_qkv, *packed, input_grad = tail(*rest)
     input_grad, d_out, d_up, d_down, d_qkv = handed_on(input_grad, d_weights, d_qkv)
     sums, up_sum, d_table = small_results(
         packed, width, hidden, heads, dims[0], own, lax.axis_index(axes)

time: 421 us -> 422 us (level)
  no operation moved by 1% of the time
where the time goes in v11:
time: 422 us; the launch traced here: 414 us
  Pallas kernels  359 us (85%)
  local copies, waits for them, and re-layouts  24.7 us (6%)
  between operations  14.2 us (3%)
  blocking collectives  6.2 us (1%)
  waiting for transfers between devices  5.07 us (1%)
  other arithmetic  4.99 us (1%)
    pallas_call x1, Pallas kernels, attend_back(): pl.pallas_call(partial(attend_back_kernel, rows), out_shape=(jax.ShapeDty...  120 us
    pallas_call x1, Pallas kernels, bias_rows(): pl.pallas_call(partial(bias_kernel, rows), out_shape=jax.ShapeDtypeStruct...  69.5 us
    pallas_call x1, Pallas kernels, dense(): pl.pallas_call(partial(dense_kernel, rows), out_shape=(jax.ShapeDtypeStru...  51.9 us
    pallas_call x1, Pallas kernels, attend(): pl.pallas_call(attend_kernel, out_shape=(jax.ShapeDtypeStruct((docs, head...  41.4 us
    pallas_call x1, Pallas kernels, tail(): pl.pallas_call(partial(tail_kernel, dims), out_shape=(jax.ShapeDtypeStruc...  38.1 us
    pallas_call x1, Pallas kernels, weight_grads(): pl.pallas_call(kernel, out_shape=jax.ShapeDtypeStruct((devices, own, (1 +...  22.7 us
    unnamed x19, local copies, waits for them, and re-layouts  18.6 us
    pallas_call x1, Pallas kernels, project(): pl.pallas_call(partial(project_kernel, rows), out_shape=(jax.ShapeDtypeSt...  10 us
  transfers between devices with their start and end apart: 3, of which 1 were waited for; matrix products, arithmetic and copies ran while one was open for 6% of the time, Pallas kernels for 67%

profile of v11, /device:TPU:0, one launch (start us, length us, event | category | flops | bytes accessed | tf_op | source)
XLA Modules:
  0.0 414.1 jit_solution(12459039235103017306)
XLA Ops:
  7.2 0.7 pad_maximum_fusion.2
  8.0 0.8 reshape.52
  8.9 1.7 pad_maximum_fusion
  10.7 0.7 all-gather.6.cloned.1.call-update
  11.4 3.3 copy.59.x_ref
  14.7 6.2 %all-gather = bf16[4,40,12]{1,2,0:T(8,128)(2,1)S(1)} all-gather(bf16[1,40,12]{1,2,0:T(8,128)(2,1)S(1)} %bitcast.28), channel_id=1, replica_groups=mesh['dp'=8,'fsdp'=4] {'fsdp'}, dimensions={0}, use_global_device_ids=true | all-gather | bytes 4800 | tf_op jit(solution)/shard_map/all_gather | solution.py:1031
  21.0 8.2 %copy.58.box_ref = s32[2,1,2,709,709]{4,3,2,1,0:T(8,128)} copy(s32[2,1,2,709,709]{4,2,3,1,0:T(2,128)} %param.17) | data formatting | bytes 16085792 | tf_op args[3]
  29.2 2.3 copy.57.pos_ref
  31.7 1.6 copy.60.cot_ref
  34.0 69.5 %bias_rows.1.bias_ref = f32[2,12,768,768]{3,2,1,0:T(8,128)} custom-call(s32[2]{0:T(128)} %bitcast.30, f32[24,128]{1,0:T(8,128)} %pad_maximum_fusion.1.tab_ref, s32[2,1,709,709]{3,2,1,0:T(8,128)} %copy.57.pos_ref, s32[2,1,2,709,709]{4,3,2,1,0:T(8,128)} %copy.58.box_ref), custom_call_target="tpu_custom_call" | custom-call | flops 36193032 | bytes 70778880 | tf_op jit(solution)/shard_map/bias_rows/pallas_call | solution.py:97
  103.5 1.0 slice_convert_fusion
  104.7 0.7 copy.55.vec_ref
  105.5 0.9 reshape.53.upb_ref
  106.3 10.0 %project.1 = (bf16[2,768,2304]{2,1,0:T(8,128)(2,1)}, bf16[768,1536]{1,0:T(8,128)(2,1)}) custom-call(bf16[2,1,709,768]{3,2,1,0:T(8,128)(2,1)} %copy.59.x_ref, bf16[768,6272]{1,0:T(8,128)(2,1)} %all-gather.4.cloned.1.call-done.w_ref.wo_ref.wu_ref, f32[8,768]{1,0:T(8,128)} %copy.55.vec_ref), custom_call_target="tpu_custom_call" | custom-call | tf_op jit(solution)/shard_map/project/pallas_call | solution.py:132
  116.3 41.4 %attend.1 = (bf16[2,12,768,768]{3,2,1,0:T(8,128)(2,1)}, bf16[2,768,768]{2,1,0:T(8,128)(2,1)}, bf16[768,1536]{1,0:T(8,128)(2,1)}) custom-call(bf16[2,768,2304]{2,1,0:T(8,128)(2,1)} %get-tuple-element.38.q_ref.k_ref.v_ref, bf16[2,768,2304]{2,1,0:T(8,128)(2,1)} %get-tuple-element.38.q_ref.k_ref.v_ref, ...), custom_call_target="tpu_custom_call" | custom-call | tf_op jit(solution)/shard_map/attend/pallas_call | solution.py:178
  157.7 4.3 %all-gather.6.cloned.1.call-done.wd_ref = bf16[3072,768]{1,0:T(8,128)(2,1)} async-done(((bf16[96,768]{1,0:T(8,128)(2,1)}), bf16[3072,768]{1,0:T(8,128)(2,1)}) %all-gather.6.cloned.1.call-update) | async-done | bytes 4718608 | tf_op jit(solution)/shard_map/all_gather | solution.py:1044
  162.1 51.9 %dense.1 = (bf16[2,1,709,768]{3,2,1,0:T(8,128)(2,1)}, f32[2,768,768]{2,1,0:T(8,128)}, bf16[3840,1536]{1,0:T(8,128)(2,1)}, bf16[2,768,3072]{2,1,0:T(8,128)(2,1)},...) custom-call(bf16[2,1,709,768]{3,2,1,0:T(8,128)(2,1)} %copy.59.x_ref,, ...), custom_call_target="tpu_custom_call" | custom-call | tf_op jit(solution)/shard_map/dense/pallas_call | solution.py:286
  213.9 22.7 %weight_grads.1 = bf16[32,24,6912]{2,1,0:T(8,128)(2,1)} custom-call(bf16[3840,1536]{1,0:T(8,128)(2,1)} %get-tuple-element.51.l_ref, bf16[1536,3072]{1,0:T(8,128)(2,1)} %bitcast.31, bf16[768,1536]{1,0:T(8,128)(2,1)} %get-tuple-element.53.a_ref, bf16[1536,768]{1,0:T(8,128)(2,1)} %bitcast.34, bf16[1536,768]{1,0:T(8,128)(2,1)} %bitcast.33), custom_call_target="tpu_custom_call" | custom-call | flops 16307453952 | bytes 28311552 | tf_op jit(solution)/shard_map/weight_grads/pallas_call | solution.py:572
  236.7 119.7 %attend_back.1 = (bf16[2,768,2304]{2,1,0:T(8,128)(2,1)}, f32[64,128]{1,0:T(8,128)}, f32[8,2304]{1,0:T(8,128)}) custom-call(bf16[2,768,2304]{2,1,0:T(8,128)(2,1)} %get-tuple-element.38.q_ref.k_ref.v_ref, bf16[2,768,2304]{2,1,0:T(8,128)(2,1)} %get-tuple-element.38.q_ref.k_ref.v_ref, bf16[2,768,2304]{2,1,0:T(8,128)(2,1)} %get-tuple-element.38.q_ref.k_ref.v_ref, ...), custom_call_target="tpu_custom_call" | custom-call | tf_op jit(solution)/shard_map/attend_back/pallas_call | solution.py:439
  356.4 38.1 %tail.1 = (f32[24,2304]{1,0:T(8,128)}, f32[16,128]{1,0:T(8,128)}, f32[24,128]{1,0:T(8,128)}, f32[64,128]{1,0:T(8,128)}, f32[2,709,1,768]{3,2,1,0:T(1,128)}) custom-call(bf16[768,6272]{1,0:T(8,128)(2,1)} %all-gather.4.cloned.1.call-done.w_ref.wo_ref.wu_ref, bf16[768,1536]{1,0:T(8,128)(2,1)} %get-tuple-element.41.tok_ref, bf16[1536,2304]{1,0:T(8,128)(2,1)} %bitcast.23, ...), custom_call_target="tpu_custom_call" | custom-call | tf_op jit(solution)/shard_map/tail/pallas_call | solution.py:916
  394.5 0.8 constant_dynamic-slice_fusion
  395.9 3.0 copy.64
  398.9 1.3 dynamic_slice.10
  401.7 5.7 %handed_on.1 = (f32[2,709,1,768]{3,2,1,0:T(1,128)}, f32[24,768]{1,0:T(8,128)}, f32[24,3072]{1,0:T(8,128)}, f32[96,768]{1,0:T(8,128)}, f32[24,2304]{1,0:T(8,128)}) custom-call(f32[2,709,1,768]{3,2,1,0:T(1,128)} %get-tuple-element.50.in_ref, bf16[24,6912]{1,0:T(8,128)(2,1)} %reduce-scatter.2.cloned.1.call-done.w_ref, f32[24,2304]{1,0:T(8,128)} %get-tuple-element.56.q_ref), custom_call_target="tpu_custom_call" | custom-call | tf_op jit(solution)/shard_map/handed_on/pallas_call | solution.py:972
  (37 shorter events, 3.6 us)
Async XLA Ops:
  7.2 7.5 %copy-start.3 = (bf16[40,12]{0,1:T(8,128)(2,1)S(1)}, bf16[40,12]{0,1:T(8,128)(2,1)}, u32[]{:S(2)}) copy-start(bf16[40,12]{0,1:T(8,128)(2,1)} %param.26) | copy-start | bytes 2884
  7.2 96.4 %all-gather.4.cloned.1.call-start = ((), (), s32[]{:S(2)}) async-start(), calls=%async_computation.1 | async-start | bytes 9934848 | tf_op jit(solution)/shard_map/all_gather | solution.py:1041
  10.6 151.4 %all-gather.6.cloned.1.call-start = ((), (), s32[]{:S(2)}) async-start(), calls=%async_computation.2 | async-start | bytes 4866048 | tf_op jit(solution)/shard_map/all_gather | solution.py:1044
  11.4 390.3 %reduce-scatter.2.cloned.1.call-start = ((), (), s32[]{:S(2)}) async-start(), calls=%async_computation.3 | async-start | bytes 10948608 | tf_op jit(solution)/shard_map/reduce_scatter | solution.py:1053
  11.4 17.8 %slice-start = ((s8[4356096]{0:T(1024)(128)(4,1)}), s8[161792]{0:T(1024)(128)(4,1)S(1)}, s32[]{:S(2)}) async-start(s8[4356096]{0:T(1024)(128)(4,1)} %bitcast.24), calls=%async_computation.4 | async-start | bytes 323584
  21.0 8.2 %slice-start.1 = ((s8[4356096]{0:T(1024)(128)(4,1)}), s8[4194304]{0:T(1024)(128)(4,1)S(1)}, s32[]{:S(2)}) async-start(s8[4356096]{0:T(1024)(128)(4,1)} %bitcast.24), calls=%async_computation.5 | async-start | bytes 8388608
  29.2 2.5 copy-start.1
  31.7 1.6 copy-start.4
  356.4 39.5 %copy-start = (bf16[2,1,709,768]{3,2,1,0:T(8,128)(2,1)S(1)}, bf16[2,1,709,768]{3,2,1,0:T(8,128)(2,1)}, u32[]{:S(2)}) copy-start(bf16[2,1,709,768]{3,2,1,0:T(8,128)(2,1)} %get-tuple-element.87) | copy-start | bytes 6534148
  394.5 5.7 %copy-start.2 = (f32[64,128]{1,0:T(8,128)S(1)}, f32[64,128]{1,0:T(8,128)}, u32[]{:S(2)}) copy-start(f32[64,128]{1,0:T(8,128)} %get-tuple-element.64) | copy-start | bytes 98308
Sparse Core Ops, SparseCore 0:
  11.4 85.4 all-gather.3
  99.8 62.2 all-gather.5
  236.8 144.0 reduce-scatter.1
